TPU v7x, 32 devices: a whole 2x2x4 slice. The times are simulated.
32 devices in a mesh: section: 4 (over x, core), dp: 8 (over z, y).
Axes of the slice: x: 2, y: 2, z: 4, core: 2. Of those that a mesh axis runs over, the one named last changes fastest.
Arguments:
- images: bfloat16 [2, 8, 12, 3840], P(None, 'dp'), may hold values from -6 to 6
- targets: bfloat16 [2, 8, 12, 3840], P(None, 'dp'), may hold values from -6 to 6
- kernels: bfloat16 [4, 2880, 640], P('section'), may hold values from -0.109375 to 0.109375
Outputs:
- kernel_grad: float32 [4, 2880, 640], P('section', 'dp')
All inputs are finite; a program needn't handle non-finite values.
Results may differ from a plain program's by a relative error of at most 0.0075.
Values may be sent and summed in bfloat16 or wider, within the bound.
No kernel may reach another device: no remote copies, remote signals or barrier semaphores. Data moves between devices by JAX's collectives and lax.ppermute only.
A program may use at most 128 MiB of HBM per device.

v0:
```python
import functools

import jax
import jax.numpy as jnp
import numpy as np
from jax import lax
from jax.experimental import pallas as pl
from jax.experimental.pallas import tpu as pltpu
from jax.sharding import PartitionSpec as P

BF = jnp.bfloat16
F32 = jnp.float32
TAPS = [(a, b) for a in range(3) for b in range(3)]
PARITIES = [(r, s) for r in range(2) for s in range(2)]


def offset_of(parity, tap):
    return (parity + tap - 1) // 2


def dot(left, right, dims=((1,), (0,))):
    return lax.dot_general(left, right, (dims, ((), ())), preferred_element_type=F32)


def dot_nt(left, right):
    return dot(left, right, ((1,), (1,)))


def dot_tn(left, right):
    return dot(left, right, ((0,), (0,)))


def sigmoid(v):
    return 1.0 / (1.0 + jnp.exp(-v))


def silu(v):
    return v * sigmoid(v)


def slope(v):
    g = sigmoid(v)
    return g * (1.0 + v * (1.0 - g))


class Sizes:
    def __init__(self, images, kernel, dp):
        self.micro = images.shape[0]
        self.full = images.shape[2]
        self.half = self.full // 2
        self.taps_rows, self.width = kernel.shape
        self.chan = self.taps_rows // 9
        self.cells = self.half * self.half
        self.used = self.micro * self.cells
        self.rows = -(-self.used // 16) * 16
        self.group = self.width // 2
        self.low = -(-self.group // 128) * 128
        self.high = self.group // 128 * 128
        self.fine = self.micro * self.full * self.full
        self.dp = dp
        self.share = self.taps_rows // dp


def selectors(z):
    rows, n = z.rows, z.half

    def at(m, i, j):
        return m * z.cells + i * n + j

    shift = np.zeros((9, rows, rows), np.float32)
    enc = np.zeros((9, rows, z.fine), np.float32)
    parity = np.zeros((4, rows, z.fine), np.float32)
    gather = np.zeros((9, rows, 4, rows), np.float32)
    for m in range(z.micro):
        for i in range(n):
            for j in range(n):
                r = at(m, i, j)
                for t, (a, b) in enumerate(TAPS):
                    ii, jj = i + a - 1, j + b - 1
                    if 0 <= ii < n and 0 <= jj < n:
                        shift[t, r, at(m, ii, jj)] = 1
                    ii, jj = 2 * i + a - 1, 2 * j + b - 1
                    if 0 <= ii < z.full and 0 <= jj < z.full:
                        enc[t, r, (m * z.full + ii) * z.full + jj] = 1
                    for p, (pr, ps) in enumerate(PARITIES):
                        ii, jj = i + offset_of(pr, a), j + offset_of(ps, b)
                        if 0 <= ii < n and 0 <= jj < n:
                            gather[t, at(m, ii, jj), p, r] = 1
                for p, (pr, ps) in enumerate(PARITIES):
                    parity[p, r, (m * z.full + 2 * i + pr) * z.full + 2 * j + ps] = 1
    back = shift.transpose(0, 2, 1)
    return dict(
        shift=shift.reshape(9 * rows, rows),
        back=back.reshape(9 * rows, rows),
        enc=enc.reshape(9 * rows, z.fine),
        parity=parity.reshape(4 * rows, z.fine),
        gather=gather.reshape(9 * rows, 4 * rows),
    )


def lanes(shape):
    return lax.broadcasted_iota(jnp.int32, shape, 1)


def join_columns(z, first, second):
    overlap = z.low - z.high
    if overlap == 0:
        return jnp.concatenate([first, second], axis=1)
    mid_first = first[:, z.high :]
    mid = jnp.where(lanes(mid_first.shape) < z.group - z.high, mid_first, second[:, :overlap])
    return jnp.concatenate([first[:, : z.high], mid, second[:, overlap:]], axis=1)


def split_groups(z, value):
    swapped = pltpu.roll(value.astype(F32), z.group, 1).astype(BF)
    return value[:, : z.group], swapped[:, : z.group]


def tap_rows(z, t):
    return slice(t * z.rows, (t + 1) * z.rows)


def tap_kernel(z, kernel, t, low):
    rows = pl.ds(t * z.chan, z.chan)
    return kernel[rows, : z.low] if low else kernel[rows, z.high :]


def conv_forward(z, value, kernel, shift):
    first, second = split_groups(z, value)
    first = dot(shift[...], first).astype(BF)
    second = dot(shift[...], second).astype(BF)
    total_first = total_second = None
    for t in range(9):
        a = dot(first[tap_rows(z, t)], tap_kernel(z, kernel, t, True))
        b = dot(second[tap_rows(z, t)], tap_kernel(z, kernel, t, False))
        total_first = a if total_first is None else total_first + a
        total_second = b if total_second is None else total_second + b
    return join_columns(z, total_first, total_second)


def join_groups(z, first, second, scratch):
    scratch[0, :, : z.group] = first
    scratch[1, :, : z.group] = second
    left = scratch[0]
    right = pltpu.roll(scratch[1], z.group, 1)
    return jnp.where(lanes(left.shape) < z.group, left, right)


def rows_times_kernel(z, first, second, kernel, scratch):
    total_first = total_second = None
    for t in range(9):
        a = dot_nt(first[tap_rows(z, t)], tap_kernel(z, kernel, t, True))
        b = dot_nt(second[tap_rows(z, t)], tap_kernel(z, kernel, t, False))
        total_first = a if total_first is None else total_first + a
        total_second = b if total_second is None else total_second + b
    return join_groups(z, total_first, total_second, scratch)


def conv_backward(z, delta, kernel, back, scratch):
    first = delta[:, : z.low].astype(F32)
    first = jnp.where(lanes(first.shape) < z.group, first, 0.0).astype(BF)
    second = delta[:, z.high :].astype(F32)
    second = jnp.where(lanes(second.shape) >= z.group - z.high, second, 0.0).astype(BF)
    first = dot(back[...], first).astype(BF)
    second = dot(back[...], second).astype(BF)
    return rows_times_kernel(z, first, second, kernel, scratch)


def encoder_kernel(z, images, kernel, enc, out, patches_out):
    columns = dot(enc[...], images[...]).astype(BF)
    total = None
    for t in range(9):
        part = columns[tap_rows(z, t)]
        patches_out[t, :, : z.chan] = part
        a = dot(part, kernel[pl.ds(t * z.chan, z.chan), :])
        total = a if total is None else total + a
    out[0] = silu(total).astype(BF)
    out[1] = slope(total).astype(BF)


def centre_kernel(z, inbound, kernel, shift, out, slope_out):
    value = inbound[0]
    preact = conv_forward(z, value, kernel, shift)
    out[0] = value
    out[1] = (value.astype(F32) + silu(preact)).astype(BF)
    slope_out[...] = slope(preact)


def middle_kernel(
    z, scale, inbound, centre, decoder, targets, shift, back, parity, gather,
    grads, kept, sums, joined_out, scratch, delta_p, delta_q, sums_p, sums_q,
):
    scratch[...] = jnp.zeros_like(scratch)
    encoded = inbound[0]
    hidden = inbound[1]
    preact = conv_forward(z, hidden, centre, shift)
    hidden3 = (hidden.astype(F32) + silu(preact)).astype(BF)
    joined = (hidden3.astype(F32) + encoded.astype(F32)).astype(BF)
    joined_out[...] = joined
    first, second = split_groups(z, joined)
    first = dot(shift[...], first).astype(BF)
    second = dot(shift[...], second).astype(BF)
    total_p = [None] * 4
    total_q = [None] * 4
    for t, (a, b) in enumerate(TAPS):
        shifts = sorted({(offset_of(r, a), offset_of(s, b)) for r, s in PARITIES})
        blocks = [tap_rows(z, (i + 1) * 3 + j + 1) for i, j in shifts]
        left_p = jnp.concatenate([first[block] for block in blocks], axis=0)
        left_q = jnp.concatenate([second[block] for block in blocks], axis=0)
        part_p = dot(left_p, tap_kernel(z, decoder, t, True))
        part_q = dot(left_q, tap_kernel(z, decoder, t, False))
        for p, (r, s) in enumerate(PARITIES):
            at = tap_rows(z, shifts.index((offset_of(r, a), offset_of(s, b))))
            total_p[p] = part_p[at] if total_p[p] is None else total_p[p] + part_p[at]
            total_q[p] = part_q[at] if total_q[p] is None else total_q[p] + part_q[at]
    wanted = dot(parity[...], targets[...])
    move = z.group - z.high
    delta_p[...] = jnp.zeros_like(delta_p)
    delta_q[...] = jnp.zeros_like(delta_q)
    for p in range(4):
        value = total_p[p][:, : z.group]
        gate = total_q[p]
        if move:
            gate = pltpu.roll(gate, z.low - move, 1)
        gate = gate[:, : z.group]
        act = silu(gate)
        residual = (value * act - wanted[tap_rows(z, p)]) * scale
        delta_p[tap_rows(z, p), : z.group] = residual * act
        delta_q[tap_rows(z, p), : z.group] = residual * value * slope(gate)
    moved = delta_q[...]
    if move:
        moved = pltpu.roll(moved, move, 1)
    sums_p[...] = dot(gather[...], delta_p[...].astype(BF)).astype(BF)
    sums_q[...] = dot(gather[...], moved.astype(BF)).astype(BF)
    for t in range(9):
        part_p = sums_p[tap_rows(z, t)].astype(F32)
        part_q = sums_q[tap_rows(z, t)].astype(F32)
        sums[t] = join_columns(z, part_p, part_q).astype(BF)
    grad = rows_times_kernel(z, sums_p, sums_q, decoder, scratch).astype(BF)
    delta = (grad.astype(F32) * slope(preact)).astype(BF)
    flow = conv_backward(z, delta, centre, back, scratch)
    grads[0] = (grad.astype(F32) + flow).astype(BF)
    grads[1] = grad
    kept[0] = delta
    kept[1] = hidden


def centre_back_kernel(z, grads, enc_slope, centre_slope, kernel, back, out, delta_out, scratch):
    scratch[...] = jnp.zeros_like(scratch)
    above = grads[0].astype(F32)
    delta = (above * centre_slope[...]).astype(BF)
    delta_out[...] = delta
    flow = conv_backward(z, delta, kernel, back, scratch)
    below = (above + flow).astype(BF)
    total = below.astype(F32) + grads[1].astype(F32)
    out[...] = (total * enc_slope[1].astype(F32)).astype(BF)


def partner_of(z, place, k, relative):
    if not relative:
        return k
    return place ^ k


def first_tap(z, dest):
    return dest * z.share // z.chan


def prepare_kernel(z, relative, where, patches, encoded, kept_in, joined, deep, delta, sums, *outs):
    section, place = where[0], where[1]
    n = z.dp
    left, right, extra = outs[:n], outs[n : 2 * n], outs[2 * n :]

    @pl.when(section == 0)
    def _():
        for k in range(n):
            tap = first_tap(z, partner_of(z, place, k, relative))
            near = patches[tap].astype(F32)
            far = patches[jnp.minimum(tap + 1, 8)].astype(F32)
            both = jnp.where(lanes(near.shape) < z.chan, near, pltpu.roll(far, z.chan, 1))
            left[k][...] = both.astype(BF)
            right[k][...] = deep[...]

    @pl.when(section == 1)
    def _():
        for k in range(n):
            left[k][...] = encoded[0]
            right[k][...] = delta[...]

    @pl.when(section == 2)
    def _():
        for k in range(n):
            left[k][...] = kept_in[1]
            right[k][...] = kept_in[0]

    @pl.when(section == 3)
    def _():
        for k in range(n):
            tap = first_tap(z, partner_of(z, place, k, relative))
            left[k][...] = joined[...]
            right[k][...] = sums[tap]
            extra[k][...] = sums[jnp.minimum(tap + 1, 8)]


def weight_kernel(z, where, shift, *refs):
    n = z.dp
    left, right, extra = refs[:n], refs[n : 2 * n], refs[2 * n : 3 * n]
    out, lefts, rights, rows_out = refs[3 * n :]
    section, place = where[0], where[1]
    tap = first_tap(z, place)

    def stack(target, pieces):
        for k in range(n):
            target[pl.ds(k * z.rows, z.rows), :] = pieces[k][...]

    def grouped(at):
        overlap = z.low - z.high
        first = dot_tn(lefts[:, : z.low], rights[:, : z.low])
        second = dot_tn(lefts[:, z.high :], rights[:, z.high :])
        move = z.group - z.high
        both = join_columns(z, first[: z.chan], second[move : move + z.chan])
        rows_out[pl.ds(at * z.chan, z.chan), :] = both

    @pl.when(section == 0)
    def _():
        stack(lefts, left)
        stack(rights, right)
        rows_out[...] = dot_tn(lefts[...], rights[...])

    @pl.when(jnp.logical_or(section == 1, section == 2))
    def _():
        stack(rights, right)
        for at in range(2):
            here = jnp.minimum(tap + at, 8)
            move = shift[pl.ds(pl.multiple_of(here * z.rows, 16), z.rows), :]
            for k in range(n):
                lefts[pl.ds(k * z.rows, z.rows), :] = dot(move, left[k][...]).astype(BF)
            grouped(at)

    @pl.when(section == 3)
    def _():
        stack(lefts, left)
        stack(rights, right)
        grouped(0)
        stack(rights, extra)
        grouped(1)

    begin = place * z.share - tap * z.chan
    if z.share % 8 == 0 and z.chan % 8 == 0:
        out[...] = rows_out[pl.ds(pl.multiple_of(begin, 8), z.share), :]
    else:
        size = -(-(z.share + 7) // 8) * 8
        rest = lax.rem(begin, 8)
        block = rows_out[pl.ds(pl.multiple_of(begin - rest, 8), size), :]
        out[...] = pltpu.roll(block, lax.rem(size - rest, size), 0)[: z.share]


def call(body, outs, scratch=(), smem=False, n_in=1, flops=10**9):
    specs = [pl.BlockSpec(memory_space=pltpu.VMEM)] * n_in
    if smem:
        specs[0] = pl.BlockSpec(memory_space=pltpu.SMEM)
    single = not isinstance(outs, (list, tuple))
    return pl.pallas_call(
        body,
        out_shape=outs,
        in_specs=specs,
        out_specs=pl.BlockSpec(memory_space=pltpu.VMEM)
        if single
        else [pl.BlockSpec(memory_space=pltpu.VMEM)] * len(outs),
        scratch_shapes=list(scratch),
        compiler_params=pltpu.CompilerParams(vmem_limit_bytes=40 * 2**20),
    )


def exchange(z, relative, pieces):
    n = z.dp
    if not relative:
        stacked = lax.all_to_all(jnp.stack(pieces), "dp", 0, 0, tiled=True)
        return [stacked[k] for k in range(n)]
    return [pieces[0]] + [
        lax.ppermute(pieces[k], "dp", [(d, d ^ k) for d in range(n)]) for k in range(1, n)
    ]


def on_device(images, targets, kernels):
    kernel = kernels[0]
    dp = lax.axis_size("dp")
    n_section = lax.axis_size("section")
    z = Sizes(images, kernel, dp)
    relative = dp <= 16 and dp & (dp - 1) == 0
    sel = {k: jnp.asarray(v, BF) for k, v in selectors(z).items()}
    scale = 1.0 / (z.micro * dp * images.shape[1])
    where = jnp.stack([lax.axis_index("section"), lax.axis_index("dp")]).astype(jnp.int32)
    image_rows = images.reshape(z.fine, z.chan)
    target_rows = targets.reshape(z.fine, z.chan)
    rows, width = z.rows, z.width
    pair = jax.ShapeDtypeStruct((2, rows, width), BF)
    one = jax.ShapeDtypeStruct((rows, width), BF)
    nine = jax.ShapeDtypeStruct((9, rows, width), BF)
    join = pltpu.VMEM((2, rows, width), F32)

    def across(x, bit):
        return lax.ppermute(x, "section", [(s, s ^ bit) for s in range(n_section)])

    other = across(kernel, 1)
    encoded, patches = call(functools.partial(encoder_kernel, z), [pair, nine], n_in=3)(
        image_rows, kernel, sel["enc"]
    )
    encoded_in = across(encoded, 1)
    forward, centre_slope = call(
        functools.partial(centre_kernel, z),
        [pair, jax.ShapeDtypeStruct((rows, width), F32)],
        n_in=3,
    )(encoded_in, kernel, sel["shift"])
    forward_in = across(forward, 2)
    grads, kept, sums, joined = call(
        functools.partial(middle_kernel, z, scale),
        [pair, pair, nine, one],
        scratch=[
            join,
            pltpu.VMEM((4 * rows, z.low), F32),
            pltpu.VMEM((4 * rows, z.low), F32),
            pltpu.VMEM((9 * rows, z.low), BF),
            pltpu.VMEM((9 * rows, z.width - z.high), BF),
        ],
        n_in=8,
    )(forward_in, other, kernel, target_rows, sel["shift"], sel["back"], sel["parity"], sel["gather"])
    grads_in = across(grads, 2)
    kept_in = across(kept, 1)
    deep, delta = call(functools.partial(centre_back_kernel, z), [one, one], scratch=[join], n_in=5)(
        grads_in, encoded_in, centre_slope, kernel, sel["back"]
    )
    deep_in = across(deep, 1)
    pieces = call(
        functools.partial(prepare_kernel, z, relative), [one] * (3 * dp), smem=True, n_in=8
    )(where, patches, encoded_in, kept_in, joined, deep_in, delta, sums)
    left = exchange(z, relative, pieces[:dp])
    right = exchange(z, relative, pieces[dp : 2 * dp])
    extra = exchange(z, relative, pieces[2 * dp :])
    out = call(
        functools.partial(weight_kernel, z),
        jax.ShapeDtypeStruct((z.share, width), F32),
        scratch=[
            pltpu.VMEM((dp * rows, width), BF),
            pltpu.VMEM((dp * rows, width), BF),
            pltpu.VMEM((2 * z.chan, width), F32),
        ],
        smem=True,
        n_in=2 + 3 * dp,
    )(where, sel["shift"], *left, *right, *extra)
    return out[None]


def solution(mesh):
    return jax.shard_map(
        on_device,
        mesh=mesh,
        in_specs=(P(None, "dp", None, None), P(None, "dp", None, None), P("section", None, None)),
        out_specs=P("section", "dp", None),
        check_vma=False,
    )
```

profile of v0, /device:TPU:1, one launch (start us, length us, event | category | flops | bytes accessed | tf_op | source)
XLA Modules:
  0.0 112.9 jit_solution(12167812782736146062)
XLA Ops:
  0.0 0.0 collective-permute-start.2
  0.0 1.0 copy.11
  1.0 0.3 reshape.6.images
  1.3 0.0 copy-start
  1.3 2.0 %copy-done = bf16[1,2880,640]{2,1,0:T(8,128)(2,1)S(1)} copy-done((bf16[1,2880,640]{2,1,0:T(8,128)(2,1)S(1)}, bf16[1,2880,640]{2,1,0:T(8,128)(2,1)}, u32[]{:S(2)}) %copy-start) | copy-done | bytes 3686424
  3.4 1.0 copy-done.6
  4.4 0.0 copy-start.8
  4.4 1.4 %shard_map.82 = (bf16[2,80,640]{2,1,0:T(8,128)(2,1)S(1)}, bf16[9,80,640]{2,1,0:T(8,128)(2,1)S(1)}) custom-call(bf16[288,320]{1,0:T(8,128)(2,1)S(1)} %reshape.6.images, bf16[2880,640]{1,0:T(8,128)(2,1)S(1)} %bitcast.9, bf16[720,288]{1,0:T(8,128)(2,1)S(1)} %copy-done.6), custom_call_target="tpu_custom_call" | custom-call | tf_op jit(solution)/shard_map/pallas_call | solution.py:406
  5.9 0.6 collective-permute-start
  6.4 1.1 collective-permute-done.inbound.enc_slope.encoded
  7.5 1.5 %shard_map.83 = (bf16[2,80,640]{2,1,0:T(8,128)(2,1)S(1)}, f32[80,640]{1,0:T(8,128)S(1)}) custom-call(bf16[2,80,640]{2,1,0:T(8,128)(2,1)S(1)} %collective-permute-done.inbound.enc_slope.encoded, bf16[2880,640]{1,0:T(8,128)(2,1)S(1)} %bitcast.10, bf16[720,80]{1,0:T(8,128)(2,1)S(1)} %copy-done.4), custom_call_target="tpu_custom_call" | custom-call | tf_op jit(solution)/shard_map/pallas_call | solution.py:410
  9.0 2.6 %collective-permute-start.1 = (bf16[2,80,640]{2,1,0:T(8,128)(2,1)S(1)}, bf16[2,80,640]{2,1,0:T(8,128)(2,1)S(1)}, u32[]{:S(2)}, u32[]{:S(2)}) collective-permute-start(bf16[2,80,640]{2,1,0:T(8,128)(2,1)S(1)} %get-tuple-element.41), channel_id=1, source_target_pairs={{0,16},{8,24},{16,0},{24,8},{1,17},{9,25},{17,1},{25,9},{2,18},{10... | collective-permute-start | bytes 614408 | tf_op jit(solution)/shard_map/ppermute | solution.py:403
  11.7 0.3 reshape.7.targets
  12.0 5.0 %collective-permute-done.1.inbound = bf16[2,80,640]{2,1,0:T(8,128)(2,1)S(1)} collective-permute-done((bf16[2,80,640]{2,1,0:T(8,128)(2,1)S(1)}, bf16[2,80,640]{2,1,0:T(8,128)(2,1)S(1)}, u32[]{:S(2)}, u32[]{:S(2)}) %collective-permute-start.1) | collective-permute-done | bytes 204832 | tf_op jit(solution)/shard_map/ppermute | solution.py:403
  17.0 0.7 copy-done.11
  17.7 0.0 collective-permute-done.2.centre
  17.7 0.0 copy-start.2
  17.7 2.0 %copy-done.2 = bf16[1,2880,640]{2,1,0:T(8,128)(2,1)S(1)} copy-done((bf16[1,2880,640]{2,1,0:T(8,128)(2,1)S(1)}, bf16[1,2880,640]{2,1,0:T(8,128)(2,1)}, u32[]{:S(2)}) %copy-start.2) | copy-done | bytes 3686424
  19.7 0.9 copy-done.12
  20.7 14.2 %shard_map.84 = (bf16[2,80,640]{2,1,0:T(8,128)(2,1)}, bf16[2,80,640]{2,1,0:T(8,128)(2,1)}, bf16[9,80,640]{2,1,0:T(8,128)(2,1)S(1)}, bf16[80,640]{1,0:T(8,128)(2,1)S(1)}) custom-call(bf16[2,80,640]{2,1,0:T(8,128)(2,1)S(1)} %copy-done.12, bf16[2880,640]{1,0:T(8,128)(2,1)} %collective-permute-done.2.centre, bf16[2880,640]{1,0:T(8,128)(2,1)S(1)} %bitcast.11, ...), custom_call_target="tpu_custom_call" | custom-call | tf_op jit(solution)/shard_map/pallas_call | solution.py:416
  34.9 1.2 %collective-permute-start.4 = (bf16[2,80,640]{2,1,0:T(8,128)(2,1)}, bf16[2,80,640]{2,1,0:T(8,128)(2,1)S(1)}, u32[]{:S(2)}, u32[]{:S(2)}) collective-permute-start(bf16[2,80,640]{2,1,0:T(8,128)(2,1)} %get-tuple-element.44), channel_id=1, source_target_pairs={{0,16},{8,24},{16,0},{24,8},{1,17},{9,25},{17,1},{25,9},{2,18},{10... | collective-permute-start | bytes 614408 | tf_op jit(solution)/shard_map/ppermute | solution.py:403
  36.1 1.3 %collective-permute-start.3 = (bf16[2,80,640]{2,1,0:T(8,128)(2,1)}, bf16[2,80,640]{2,1,0:T(8,128)(2,1)S(1)}, u32[]{:S(2)}, u32[]{:S(2)}) collective-permute-start(bf16[2,80,640]{2,1,0:T(8,128)(2,1)} %get-tuple-element.42), channel_id=1, source_target_pairs={{0,8},{8,0},{16,24},{24,16},{1,9},{9,1},{17,25},{25,17},{2,10},{10... | collective-permute-start | bytes 614408 | tf_op jit(solution)/shard_map/ppermute | solution.py:403
  37.4 3.7 %collective-permute-done.4.grads = bf16[2,80,640]{2,1,0:T(8,128)(2,1)S(1)} collective-permute-done((bf16[2,80,640]{2,1,0:T(8,128)(2,1)}, bf16[2,80,640]{2,1,0:T(8,128)(2,1)S(1)}, u32[]{:S(2)}, u32[]{:S(2)}) %collective-permute-start.4) | collective-permute-done | bytes 204832 | tf_op jit(solution)/shard_map/ppermute | solution.py:403
  41.0 2.0 %copy-done.3 = bf16[1,2880,640]{2,1,0:T(8,128)(2,1)S(1)} copy-done((bf16[1,2880,640]{2,1,0:T(8,128)(2,1)S(1)}, bf16[1,2880,640]{2,1,0:T(8,128)(2,1)}, u32[]{:S(2)}) %copy-start.3) | copy-done | bytes 3686424
  43.1 0.9 copy-done.10
  44.0 2.1 %shard_map.85 = (bf16[80,640]{1,0:T(8,128)(2,1)S(1)}, bf16[80,640]{1,0:T(8,128)(2,1)S(1)}) custom-call(bf16[2,80,640]{2,1,0:T(8,128)(2,1)S(1)} %collective-permute-done.4.grads, bf16[2,80,640]{2,1,0:T(8,128)(2,1)S(1)} %collective-permute-done.inbound.enc_slope.encoded, f32[80,640]{1,0:T(8,128)S(1)} %copy-done.10, bf16[2880,640]{1,0:T(8,128)(2,1)S(1)} %bitcast.12, ...), custom_call_target="tpu_custom_call" | custom-call | tf_op jit(solution)/shard_map/pallas_call | solution.py:430
  46.2 1.6 %collective-permute-start.5 = (bf16[80,640]{1,0:T(8,128)(2,1)S(1)}, bf16[80,640]{1,0:T(8,128)(2,1)S(1)}, u32[]{:S(2)}, u32[]{:S(2)}) collective-permute-start(bf16[80,640]{1,0:T(8,128)(2,1)S(1)} %get-tuple-element.46), channel_id=1, source_target_pairs={{0,8},{8,0},{16,24},{24,16},{1,9},{9,1},{17,25},{25,17},{2,10},{10... | collective-permute-start | bytes 307208 | tf_op jit(solution)/shard_map/ppermute | solution.py:403
  47.8 0.1 pad_add_fusion.where
  47.9 0.0 collective-permute-done.3.kept_in
  47.9 0.9 collective-permute-done.5.deep
  48.8 0.7 shard_map.86
  49.4 3.3 %collective-permute-start.10 = (bf16[80,640]{1,0:T(8,128)(2,1)S(1)}, bf16[80,640]{1,0:T(8,128)(2,1)S(1)}, u32[]{:S(2)}, u32[]{:S(2)}) collective-permute-start(bf16[80,640]{1,0:T(8,128)(2,1)S(1)} %get-tuple-element.54), channel_id=1, source_target_pairs={{0,5},{1,4},{2,7},{3,6},{4,1},{5,0},{6,3},{7,2},{8,13},{9,12},{10,... | collective-permute-start | bytes 307208 | tf_op jit(solution)/shard_map/ppermute | solution.py:381
  52.7 1.1 collective-permute-start.11
  53.8 2.1 %collective-permute-start.12 = (bf16[80,640]{1,0:T(8,128)(2,1)S(1)}, bf16[80,640]{1,0:T(8,128)(2,1)S(1)}, u32[]{:S(2)}, u32[]{:S(2)}) collective-permute-start(bf16[80,640]{1,0:T(8,128)(2,1)S(1)} %get-tuple-element.56), channel_id=1, source_target_pairs={{0,7},{1,6},{2,5},{3,4},{4,3},{5,2},{6,1},{7,0},{8,15},{9,14},{10,... | collective-permute-start | bytes 307208 | tf_op jit(solution)/shard_map/ppermute | solution.py:381
  55.9 1.2 %collective-permute-start.13 = (bf16[80,640]{1,0:T(8,128)(2,1)S(1)}, bf16[80,640]{1,0:T(8,128)(2,1)S(1)}, u32[]{:S(2)}, u32[]{:S(2)}) collective-permute-start(bf16[80,640]{1,0:T(8,128)(2,1)S(1)} %get-tuple-element.58), channel_id=1, source_target_pairs={{0,1},{1,0},{2,3},{3,2},{4,5},{5,4},{6,7},{7,6},{8,9},{9,8},{10,11... | collective-permute-start | bytes 307208 | tf_op jit(solution)/shard_map/ppermute | solution.py:381
  57.2 3.5 %collective-permute-done.10.refs_5_ = bf16[80,640]{1,0:T(8,128)(2,1)S(1)} collective-permute-done((bf16[80,640]{1,0:T(8,128)(2,1)S(1)}, bf16[80,640]{1,0:T(8,128)(2,1)S(1)}, u32[]{:S(2)}, u32[]{:S(2)}) %collective-permute-start.10) | collective-permute-done | bytes 102432 | tf_op jit(solution)/shard_map/ppermute | solution.py:381
  60.7 2.4 %collective-permute-start.15 = (bf16[80,640]{1,0:T(8,128)(2,1)S(1)}, bf16[80,640]{1,0:T(8,128)(2,1)S(1)}, u32[]{:S(2)}, u32[]{:S(2)}) collective-permute-start(bf16[80,640]{1,0:T(8,128)(2,1)S(1)} %get-tuple-element.60), channel_id=1, source_target_pairs={{0,3},{1,2},{2,1},{3,0},{4,7},{5,6},{6,5},{7,4},{8,11},{9,10},{10,... | collective-permute-start | bytes 307208 | tf_op jit(solution)/shard_map/ppermute | solution.py:381
  63.1 4.2 %collective-permute-start.16 = (bf16[80,640]{1,0:T(8,128)(2,1)S(1)}, bf16[80,640]{1,0:T(8,128)(2,1)S(1)}, u32[]{:S(2)}, u32[]{:S(2)}) collective-permute-start(bf16[80,640]{1,0:T(8,128)(2,1)S(1)} %get-tuple-element.61), channel_id=1, source_target_pairs={{0,4},{1,5},{2,6},{3,7},{4,0},{5,1},{6,2},{7,3},{8,12},{9,13},{10,... | collective-permute-start | bytes 307208 | tf_op jit(solution)/shard_map/ppermute | solution.py:381
  67.3 4.8 %collective-permute-start.17 = (bf16[80,640]{1,0:T(8,128)(2,1)S(1)}, bf16[80,640]{1,0:T(8,128)(2,1)S(1)}, u32[]{:S(2)}, u32[]{:S(2)}) collective-permute-start(bf16[80,640]{1,0:T(8,128)(2,1)S(1)} %get-tuple-element.62), channel_id=1, source_target_pairs={{0,5},{1,4},{2,7},{3,6},{4,1},{5,0},{6,3},{7,2},{8,13},{9,12},{10,... | collective-permute-start | bytes 307208 | tf_op jit(solution)/shard_map/ppermute | solution.py:381
  72.1 0.0 collective-permute-done.13.refs_9_
  72.1 0.0 collective-permute-start.18
  72.1 2.2 %collective-permute-start.19 = (bf16[80,640]{1,0:T(8,128)(2,1)S(1)}, bf16[80,640]{1,0:T(8,128)(2,1)S(1)}, u32[]{:S(2)}, u32[]{:S(2)}) collective-permute-start(bf16[80,640]{1,0:T(8,128)(2,1)S(1)} %get-tuple-element.64), channel_id=1, source_target_pairs={{0,7},{1,6},{2,5},{3,4},{4,3},{5,2},{6,1},{7,0},{8,15},{9,14},{10,... | collective-permute-start | bytes 307208 | tf_op jit(solution)/shard_map/ppermute | solution.py:381
  74.3 0.0 collective-permute-done.15.refs_11_
  74.3 2.2 %collective-permute-start.20 = (bf16[80,640]{1,0:T(8,128)(2,1)S(1)}, bf16[80,640]{1,0:T(8,128)(2,1)S(1)}, u32[]{:S(2)}, u32[]{:S(2)}) collective-permute-start(bf16[80,640]{1,0:T(8,128)(2,1)S(1)} %get-tuple-element.66), channel_id=1, source_target_pairs={{0,1},{1,0},{2,3},{3,2},{4,5},{5,4},{6,7},{7,6},{8,9},{9,8},{10,11... | collective-permute-start | bytes 307208 | tf_op jit(solution)/shard_map/ppermute | solution.py:381
  76.5 0.0 collective-permute-done.16.refs_12_
  76.6 0.0 collective-permute-start.21
  76.6 5.1 %collective-permute-done.17.refs_13_ = bf16[80,640]{1,0:T(8,128)(2,1)S(1)} collective-permute-done((bf16[80,640]{1,0:T(8,128)(2,1)S(1)}, bf16[80,640]{1,0:T(8,128)(2,1)S(1)}, u32[]{:S(2)}, u32[]{:S(2)}) %collective-permute-start.17) | collective-permute-done | bytes 102432 | tf_op jit(solution)/shard_map/ppermute | solution.py:381
  81.7 0.0 collective-permute-start.22
  81.7 0.0 collective-permute-done.18.refs_14_
  81.7 4.2 %collective-permute-start.23 = (bf16[80,640]{1,0:T(8,128)(2,1)S(1)}, bf16[80,640]{1,0:T(8,128)(2,1)S(1)}, u32[]{:S(2)}, u32[]{:S(2)}) collective-permute-start(bf16[80,640]{1,0:T(8,128)(2,1)S(1)} %get-tuple-element.69), channel_id=1, source_target_pairs={{0,4},{1,5},{2,6},{3,7},{4,0},{5,1},{6,2},{7,3},{8,12},{9,13},{10,... | collective-permute-start | bytes 307208 | tf_op jit(solution)/shard_map/ppermute | solution.py:381
  85.9 0.0 collective-permute-done.19.refs_15_
  85.9 3.9 %collective-permute-start.24 = (bf16[80,640]{1,0:T(8,128)(2,1)S(1)}, bf16[80,640]{1,0:T(8,128)(2,1)S(1)}, u32[]{:S(2)}, u32[]{:S(2)}) collective-permute-start(bf16[80,640]{1,0:T(8,128)(2,1)S(1)} %get-tuple-element.70), channel_id=1, source_target_pairs={{0,5},{1,4},{2,7},{3,6},{4,1},{5,0},{6,3},{7,2},{8,13},{9,12},{10,... | collective-permute-start | bytes 307208 | tf_op jit(solution)/shard_map/ppermute | solution.py:381
  89.8 0.0 collective-permute-done.20.refs_17_
  89.8 0.7 collective-permute-start.26
  90.5 3.8 %collective-permute-start.6 = (bf16[80,640]{1,0:T(8,128)(2,1)S(1)}, bf16[80,640]{1,0:T(8,128)(2,1)S(1)}, u32[]{:S(2)}, u32[]{:S(2)}) collective-permute-start(bf16[80,640]{1,0:T(8,128)(2,1)S(1)} %get-tuple-element.50), channel_id=1, source_target_pairs={{0,1},{1,0},{2,3},{3,2},{4,5},{5,4},{6,7},{7,6},{8,9},{9,8},{10,11... | collective-permute-start | bytes 307208 | tf_op jit(solution)/shard_map/ppermute | solution.py:381
  94.2 0.0 collective-permute-done.23.refs_20_
  94.2 0.0 collective-permute-start.7
  94.2 5.7 %collective-permute-done.24.refs_21_ = bf16[80,640]{1,0:T(8,128)(2,1)S(1)} collective-permute-done((bf16[80,640]{1,0:T(8,128)(2,1)S(1)}, bf16[80,640]{1,0:T(8,128)(2,1)S(1)}, u32[]{:S(2)}, u32[]{:S(2)}) %collective-permute-start.24) | collective-permute-done | bytes 102432 | tf_op jit(solution)/shard_map/ppermute | solution.py:381
  99.9 0.0 collective-permute-start.8
  99.9 0.0 collective-permute-done.25.refs_22_
  99.9 3.9 %collective-permute-start.9 = (bf16[80,640]{1,0:T(8,128)(2,1)S(1)}, bf16[80,640]{1,0:T(8,128)(2,1)S(1)}, u32[]{:S(2)}, u32[]{:S(2)}) collective-permute-start(bf16[80,640]{1,0:T(8,128)(2,1)S(1)} %get-tuple-element.53), channel_id=1, source_target_pairs={{0,4},{1,5},{2,6},{3,7},{4,0},{5,1},{6,2},{7,3},{8,12},{9,13},{10,... | collective-permute-start | bytes 307208 | tf_op jit(solution)/shard_map/ppermute | solution.py:381
  103.9 0.5 collective-permute-done.8.refs_3_
  104.3 5.1 %collective-permute-done.9.refs_4_ = bf16[80,640]{1,0:T(8,128)(2,1)S(1)} collective-permute-done((bf16[80,640]{1,0:T(8,128)(2,1)S(1)}, bf16[80,640]{1,0:T(8,128)(2,1)S(1)}, u32[]{:S(2)}, u32[]{:S(2)}) %collective-permute-start.9) | collective-permute-done | bytes 102432 | tf_op jit(solution)/shard_map/ppermute | solution.py:381
  109.5 3.4 %shard_map.87 = f32[360,640]{1,0:T(8,128)} custom-call(s32[2]{0:T(128)S(1)} %pad_add_fusion.where, bf16[720,80]{1,0:T(8,128)(2,1)S(1)} %copy-done.4, bf16[80,640]{1,0:T(8,128)(2,1)S(1)} %get-tuple-element.49.refs_0_, bf16[80,640]{1,0:T(8,128)(2,1)S(1)} %collective-permute-done.6.refs_1_, bf16[80,640]{1,0:T(8,128)(2,1)S(1)} %collective-permute-done.7.refs_2_, ...), custom_call_target="tpu_custom_call" | custom-call | tf_op jit(solution)/shard_map/pallas_call | solution.py:440
  (29 shorter events, 0.1 us)
Async XLA Ops:
  0.0 7.5 %copy-start.4 = (bf16[720,80]{1,0:T(8,128)(2,1)S(1)}, bf16[720,80]{1,0:T(8,128)(2,1)}, u32[]{:S(2)}) copy-start(bf16[720,80]{1,0:T(8,128)(2,1)} %constant.18.clone.shift) | copy-start | bytes 345604
  0.0 17.7 %collective-permute-start.2 = (bf16[2880,640]{1,0:T(8,128)(2,1)}, bf16[2880,640]{1,0:T(8,128)(2,1)}, u32[]{:S(2)}, u32[]{:S(2)}) collective-permute-start(bf16[2880,640]{1,0:T(8,128)(2,1)} %bitcast.8), channel_id=1, source_target_pairs={{0,8},{8,0},{16,24},{24,16},{1,9},{9,1},{17,25},{25,17},{2,10},{10... | collective-permute-start | bytes 11059208 | tf_op jit(solution)/shard_map/ppermute | solution.py:403
  1.3 2.0 %copy-start = (bf16[1,2880,640]{2,1,0:T(8,128)(2,1)S(1)}, bf16[1,2880,640]{2,1,0:T(8,128)(2,1)}, u32[]{:S(2)}) copy-start(bf16[1,2880,640]{2,1,0:T(8,128)(2,1)} %param.10) | copy-start | bytes 11059204
  3.4 1.1 copy-start.6
  4.4 3.1 %copy-start.1 = (bf16[1,2880,640]{2,1,0:T(8,128)(2,1)S(1)}, bf16[1,2880,640]{2,1,0:T(8,128)(2,1)}, u32[]{:S(2)}) copy-start(bf16[1,2880,640]{2,1,0:T(8,128)(2,1)} %param.10) | copy-start | bytes 11059204
  4.4 7.3 %copy-start.13 = (bf16[2,1,12,3840]{3,0,2,1:T(2,128)(2,1)S(1)}, bf16[2,1,12,3840]{3,0,2,1:T(2,128)(2,1)}, u32[]{:S(2)}) copy-start(bf16[2,1,12,3840]{3,0,2,1:T(2,128)(2,1)} %param.9) | copy-start | bytes 552964
  4.4 13.3 %copy-start.5 = (bf16[720,80]{1,0:T(8,128)(2,1)S(1)}, bf16[720,80]{1,0:T(8,128)(2,1)}, u32[]{:S(2)}) copy-start(bf16[720,80]{1,0:T(8,128)(2,1)} %constant.19.clone.back) | copy-start | bytes 345604
  4.4 13.3 %copy-start.7 = (bf16[720,320]{1,0:T(8,128)(2,1)S(1)}, bf16[720,320]{1,0:T(8,128)(2,1)}, u32[]{:S(2)}) copy-start(bf16[720,320]{1,0:T(8,128)(2,1)} %constant.22.clone.gather) | copy-start | bytes 1382404
  4.4 13.3 %copy-start.8 = (bf16[320,288]{1,0:T(8,128)(2,1)S(1)}, bf16[320,288]{1,0:T(8,128)(2,1)}, u32[]{:S(2)}) copy-start(bf16[320,288]{1,0:T(8,128)(2,1)} %constant.21.clone.parity) | copy-start | bytes 552964
  5.9 1.6 %collective-permute-start = (bf16[2,80,640]{2,1,0:T(8,128)(2,1)S(1)}, bf16[2,80,640]{2,1,0:T(8,128)(2,1)S(1)}, u32[]{:S(2)}, u32[]{:S(2)}) collective-permute-start(bf16[2,80,640]{2,1,0:T(8,128)(2,1)S(1)} %get-tuple-element.40), channel_id=1, source_target_pairs={{0,8},{8,0},{16,24},{24,16},{1,9},{9,1},{17,25},{25,17},{2,10},{10... | collective-permute-start | bytes 614408 | tf_op jit(solution)/shard_map/ppermute | solution.py:403
  9.0 8.0 %copy-start.9 = (f32[80,640]{1,0:T(8,128)}, f32[80,640]{1,0:T(8,128)S(1)}, u32[]{:S(2)}) copy-start(f32[80,640]{1,0:T(8,128)S(1)} %get-tuple-element.45.centre_slope) | copy-start | bytes 614404
  9.0 7.9 %collective-permute-start.1 = (bf16[2,80,640]{2,1,0:T(8,128)(2,1)S(1)}, bf16[2,80,640]{2,1,0:T(8,128)(2,1)S(1)}, u32[]{:S(2)}, u32[]{:S(2)}) collective-permute-start(bf16[2,80,640]{2,1,0:T(8,128)(2,1)S(1)} %get-tuple-element.41), channel_id=1, source_target_pairs={{0,16},{8,24},{16,0},{24,8},{1,17},{9,25},{17,1},{25,9},{2,18},{10... | collective-permute-start | bytes 614408 | tf_op jit(solution)/shard_map/ppermute | solution.py:403
  17.0 0.7 copy-start.11
  17.7 2.0 %copy-start.2 = (bf16[1,2880,640]{2,1,0:T(8,128)(2,1)S(1)}, bf16[1,2880,640]{2,1,0:T(8,128)(2,1)}, u32[]{:S(2)}) copy-start(bf16[1,2880,640]{2,1,0:T(8,128)(2,1)} %param.10) | copy-start | bytes 11059204
  19.7 0.9 copy-start.12
  34.9 6.1 %collective-permute-start.4 = (bf16[2,80,640]{2,1,0:T(8,128)(2,1)}, bf16[2,80,640]{2,1,0:T(8,128)(2,1)S(1)}, u32[]{:S(2)}, u32[]{:S(2)}) collective-permute-start(bf16[2,80,640]{2,1,0:T(8,128)(2,1)} %get-tuple-element.44), channel_id=1, source_target_pairs={{0,16},{8,24},{16,0},{24,8},{1,17},{9,25},{17,1},{25,9},{2,18},{10... | collective-permute-start | bytes 614408 | tf_op jit(solution)/shard_map/ppermute | solution.py:403
  36.1 11.8 %collective-permute-start.3 = (bf16[2,80,640]{2,1,0:T(8,128)(2,1)}, bf16[2,80,640]{2,1,0:T(8,128)(2,1)S(1)}, u32[]{:S(2)}, u32[]{:S(2)}) collective-permute-start(bf16[2,80,640]{2,1,0:T(8,128)(2,1)} %get-tuple-element.42), channel_id=1, source_target_pairs={{0,8},{8,0},{16,24},{24,16},{1,9},{9,1},{17,25},{25,17},{2,10},{10... | collective-permute-start | bytes 614408 | tf_op jit(solution)/shard_map/ppermute | solution.py:403
  41.0 2.0 %copy-start.3 = (bf16[1,2880,640]{2,1,0:T(8,128)(2,1)S(1)}, bf16[1,2880,640]{2,1,0:T(8,128)(2,1)}, u32[]{:S(2)}) copy-start(bf16[1,2880,640]{2,1,0:T(8,128)(2,1)} %param.10) | copy-start | bytes 11059204
  43.1 0.9 copy-start.10
  46.2 2.6 %collective-permute-start.5 = (bf16[80,640]{1,0:T(8,128)(2,1)S(1)}, bf16[80,640]{1,0:T(8,128)(2,1)S(1)}, u32[]{:S(2)}, u32[]{:S(2)}) collective-permute-start(bf16[80,640]{1,0:T(8,128)(2,1)S(1)} %get-tuple-element.46), channel_id=1, source_target_pairs={{0,8},{8,0},{16,24},{24,16},{1,9},{9,1},{17,25},{25,17},{2,10},{10... | collective-permute-start | bytes 307208 | tf_op jit(solution)/shard_map/ppermute | solution.py:403
  49.4 11.3 %collective-permute-start.10 = (bf16[80,640]{1,0:T(8,128)(2,1)S(1)}, bf16[80,640]{1,0:T(8,128)(2,1)S(1)}, u32[]{:S(2)}, u32[]{:S(2)}) collective-permute-start(bf16[80,640]{1,0:T(8,128)(2,1)S(1)} %get-tuple-element.54), channel_id=1, source_target_pairs={{0,5},{1,4},{2,7},{3,6},{4,1},{5,0},{6,3},{7,2},{8,13},{9,12},{10,... | collective-permute-start | bytes 307208 | tf_op jit(solution)/shard_map/ppermute | solution.py:381
  52.7 10.4 %collective-permute-start.11 = (bf16[80,640]{1,0:T(8,128)(2,1)S(1)}, bf16[80,640]{1,0:T(8,128)(2,1)S(1)}, u32[]{:S(2)}, u32[]{:S(2)}) collective-permute-start(bf16[80,640]{1,0:T(8,128)(2,1)S(1)} %get-tuple-element.55), channel_id=1, source_target_pairs={{0,6},{1,7},{2,4},{3,5},{4,2},{5,3},{6,0},{7,1},{8,14},{9,15},{10,... | collective-permute-start | bytes 307208 | tf_op jit(solution)/shard_map/ppermute | solution.py:381
  53.8 13.5 %collective-permute-start.12 = (bf16[80,640]{1,0:T(8,128)(2,1)S(1)}, bf16[80,640]{1,0:T(8,128)(2,1)S(1)}, u32[]{:S(2)}, u32[]{:S(2)}) collective-permute-start(bf16[80,640]{1,0:T(8,128)(2,1)S(1)} %get-tuple-element.56), channel_id=1, source_target_pairs={{0,7},{1,6},{2,5},{3,4},{4,3},{5,2},{6,1},{7,0},{8,15},{9,14},{10,... | collective-permute-start | bytes 307208 | tf_op jit(solution)/shard_map/ppermute | solution.py:381
  55.9 16.2 %collective-permute-start.13 = (bf16[80,640]{1,0:T(8,128)(2,1)S(1)}, bf16[80,640]{1,0:T(8,128)(2,1)S(1)}, u32[]{:S(2)}, u32[]{:S(2)}) collective-permute-start(bf16[80,640]{1,0:T(8,128)(2,1)S(1)} %get-tuple-element.58), channel_id=1, source_target_pairs={{0,1},{1,0},{2,3},{3,2},{4,5},{5,4},{6,7},{7,6},{8,9},{9,8},{10,11... | collective-permute-start | bytes 307208 | tf_op jit(solution)/shard_map/ppermute | solution.py:381
  57.2 14.9 %collective-permute-start.14 = (bf16[80,640]{1,0:T(8,128)(2,1)S(1)}, bf16[80,640]{1,0:T(8,128)(2,1)S(1)}, u32[]{:S(2)}, u32[]{:S(2)}) collective-permute-start(bf16[80,640]{1,0:T(8,128)(2,1)S(1)} %get-tuple-element.59), channel_id=1, source_target_pairs={{0,2},{1,3},{2,0},{3,1},{4,6},{5,7},{6,4},{7,5},{8,10},{9,11},{10,... | collective-permute-start | bytes 307208 | tf_op jit(solution)/shard_map/ppermute | solution.py:381
  60.7 13.6 %collective-permute-start.15 = (bf16[80,640]{1,0:T(8,128)(2,1)S(1)}, bf16[80,640]{1,0:T(8,128)(2,1)S(1)}, u32[]{:S(2)}, u32[]{:S(2)}) collective-permute-start(bf16[80,640]{1,0:T(8,128)(2,1)S(1)} %get-tuple-element.60), channel_id=1, source_target_pairs={{0,3},{1,2},{2,1},{3,0},{4,7},{5,6},{6,5},{7,4},{8,11},{9,10},{10,... | collective-permute-start | bytes 307208 | tf_op jit(solution)/shard_map/ppermute | solution.py:381
  63.1 13.4 %collective-permute-start.16 = (bf16[80,640]{1,0:T(8,128)(2,1)S(1)}, bf16[80,640]{1,0:T(8,128)(2,1)S(1)}, u32[]{:S(2)}, u32[]{:S(2)}) collective-permute-start(bf16[80,640]{1,0:T(8,128)(2,1)S(1)} %get-tuple-element.61), channel_id=1, source_target_pairs={{0,4},{1,5},{2,6},{3,7},{4,0},{5,1},{6,2},{7,3},{8,12},{9,13},{10,... | collective-permute-start | bytes 307208 | tf_op jit(solution)/shard_map/ppermute | solution.py:381
  67.3 14.4 %collective-permute-start.17 = (bf16[80,640]{1,0:T(8,128)(2,1)S(1)}, bf16[80,640]{1,0:T(8,128)(2,1)S(1)}, u32[]{:S(2)}, u32[]{:S(2)}) collective-permute-start(bf16[80,640]{1,0:T(8,128)(2,1)S(1)} %get-tuple-element.62), channel_id=1, source_target_pairs={{0,5},{1,4},{2,7},{3,6},{4,1},{5,0},{6,3},{7,2},{8,13},{9,12},{10,... | collective-permute-start | bytes 307208 | tf_op jit(solution)/shard_map/ppermute | solution.py:381
  72.1 9.6 %collective-permute-start.18 = (bf16[80,640]{1,0:T(8,128)(2,1)S(1)}, bf16[80,640]{1,0:T(8,128)(2,1)S(1)}, u32[]{:S(2)}, u32[]{:S(2)}) collective-permute-start(bf16[80,640]{1,0:T(8,128)(2,1)S(1)} %get-tuple-element.63), channel_id=1, source_target_pairs={{0,6},{1,7},{2,4},{3,5},{4,2},{5,3},{6,0},{7,1},{8,14},{9,15},{10,... | collective-permute-start | bytes 307208 | tf_op jit(solution)/shard_map/ppermute | solution.py:381
  72.1 13.8 %collective-permute-start.19 = (bf16[80,640]{1,0:T(8,128)(2,1)S(1)}, bf16[80,640]{1,0:T(8,128)(2,1)S(1)}, u32[]{:S(2)}, u32[]{:S(2)}) collective-permute-start(bf16[80,640]{1,0:T(8,128)(2,1)S(1)} %get-tuple-element.64), channel_id=1, source_target_pairs={{0,7},{1,6},{2,5},{3,4},{4,3},{5,2},{6,1},{7,0},{8,15},{9,14},{10,... | collective-permute-start | bytes 307208 | tf_op jit(solution)/shard_map/ppermute | solution.py:381
  74.3 15.5 %collective-permute-start.20 = (bf16[80,640]{1,0:T(8,128)(2,1)S(1)}, bf16[80,640]{1,0:T(8,128)(2,1)S(1)}, u32[]{:S(2)}, u32[]{:S(2)}) collective-permute-start(bf16[80,640]{1,0:T(8,128)(2,1)S(1)} %get-tuple-element.66), channel_id=1, source_target_pairs={{0,1},{1,0},{2,3},{3,2},{4,5},{5,4},{6,7},{7,6},{8,9},{9,8},{10,11... | collective-permute-start | bytes 307208 | tf_op jit(solution)/shard_map/ppermute | solution.py:381
  76.6 13.2 %collective-permute-start.21 = (bf16[80,640]{1,0:T(8,128)(2,1)S(1)}, bf16[80,640]{1,0:T(8,128)(2,1)S(1)}, u32[]{:S(2)}, u32[]{:S(2)}) collective-permute-start(bf16[80,640]{1,0:T(8,128)(2,1)S(1)} %get-tuple-element.67), channel_id=1, source_target_pairs={{0,2},{1,3},{2,0},{3,1},{4,6},{5,7},{6,4},{7,5},{8,10},{9,11},{10,... | collective-permute-start | bytes 307208 | tf_op jit(solution)/shard_map/ppermute | solution.py:381
  81.7 8.8 %collective-permute-start.22 = (bf16[80,640]{1,0:T(8,128)(2,1)S(1)}, bf16[80,640]{1,0:T(8,128)(2,1)S(1)}, u32[]{:S(2)}, u32[]{:S(2)}) collective-permute-start(bf16[80,640]{1,0:T(8,128)(2,1)S(1)} %get-tuple-element.68), channel_id=1, source_target_pairs={{0,3},{1,2},{2,1},{3,0},{4,7},{5,6},{6,5},{7,4},{8,11},{9,10},{10,... | collective-permute-start | bytes 307208 | tf_op jit(solution)/shard_map/ppermute | solution.py:381
  81.7 12.6 %collective-permute-start.23 = (bf16[80,640]{1,0:T(8,128)(2,1)S(1)}, bf16[80,640]{1,0:T(8,128)(2,1)S(1)}, u32[]{:S(2)}, u32[]{:S(2)}) collective-permute-start(bf16[80,640]{1,0:T(8,128)(2,1)S(1)} %get-tuple-element.69), channel_id=1, source_target_pairs={{0,4},{1,5},{2,6},{3,7},{4,0},{5,1},{6,2},{7,3},{8,12},{9,13},{10,... | collective-permute-start | bytes 307208 | tf_op jit(solution)/shard_map/ppermute | solution.py:381
  85.9 14.0 %collective-permute-start.24 = (bf16[80,640]{1,0:T(8,128)(2,1)S(1)}, bf16[80,640]{1,0:T(8,128)(2,1)S(1)}, u32[]{:S(2)}, u32[]{:S(2)}) collective-permute-start(bf16[80,640]{1,0:T(8,128)(2,1)S(1)} %get-tuple-element.70), channel_id=1, source_target_pairs={{0,5},{1,4},{2,7},{3,6},{4,1},{5,0},{6,3},{7,2},{8,13},{9,12},{10,... | collective-permute-start | bytes 307208 | tf_op jit(solution)/shard_map/ppermute | solution.py:381
  89.8 10.1 %collective-permute-start.25 = (bf16[80,640]{1,0:T(8,128)(2,1)S(1)}, bf16[80,640]{1,0:T(8,128)(2,1)S(1)}, u32[]{:S(2)}, u32[]{:S(2)}) collective-permute-start(bf16[80,640]{1,0:T(8,128)(2,1)S(1)} %get-tuple-element.71), channel_id=1, source_target_pairs={{0,6},{1,7},{2,4},{3,5},{4,2},{5,3},{6,0},{7,1},{8,14},{9,15},{10,... | collective-permute-start | bytes 307208 | tf_op jit(solution)/shard_map/ppermute | solution.py:381
  89.8 14.1 %collective-permute-start.26 = (bf16[80,640]{1,0:T(8,128)(2,1)S(1)}, bf16[80,640]{1,0:T(8,128)(2,1)S(1)}, u32[]{:S(2)}, u32[]{:S(2)}) collective-permute-start(bf16[80,640]{1,0:T(8,128)(2,1)S(1)} %get-tuple-element.72), channel_id=1, source_target_pairs={{0,7},{1,6},{2,5},{3,4},{4,3},{5,2},{6,1},{7,0},{8,15},{9,14},{10,... | collective-permute-start | bytes 307208 | tf_op jit(solution)/shard_map/ppermute | solution.py:381
  90.5 13.4 %collective-permute-start.6 = (bf16[80,640]{1,0:T(8,128)(2,1)S(1)}, bf16[80,640]{1,0:T(8,128)(2,1)S(1)}, u32[]{:S(2)}, u32[]{:S(2)}) collective-permute-start(bf16[80,640]{1,0:T(8,128)(2,1)S(1)} %get-tuple-element.50), channel_id=1, source_target_pairs={{0,1},{1,0},{2,3},{3,2},{4,5},{5,4},{6,7},{7,6},{8,9},{9,8},{10,11... | collective-permute-start | bytes 307208 | tf_op jit(solution)/shard_map/ppermute | solution.py:381
  94.2 9.6 %collective-permute-start.7 = (bf16[80,640]{1,0:T(8,128)(2,1)S(1)}, bf16[80,640]{1,0:T(8,128)(2,1)S(1)}, u32[]{:S(2)}, u32[]{:S(2)}) collective-permute-start(bf16[80,640]{1,0:T(8,128)(2,1)S(1)} %get-tuple-element.51), channel_id=1, source_target_pairs={{0,2},{1,3},{2,0},{3,1},{4,6},{5,7},{6,4},{7,5},{8,10},{9,11},{10,... | collective-permute-start | bytes 307208 | tf_op jit(solution)/shard_map/ppermute | solution.py:381
  99.9 4.4 %collective-permute-start.8 = (bf16[80,640]{1,0:T(8,128)(2,1)S(1)}, bf16[80,640]{1,0:T(8,128)(2,1)S(1)}, u32[]{:S(2)}, u32[]{:S(2)}) collective-permute-start(bf16[80,640]{1,0:T(8,128)(2,1)S(1)} %get-tuple-element.52), channel_id=1, source_target_pairs={{0,3},{1,2},{2,1},{3,0},{4,7},{5,6},{6,5},{7,4},{8,11},{9,10},{10,... | collective-permute-start | bytes 307208 | tf_op jit(solution)/shard_map/ppermute | solution.py:381
  99.9 9.5 %collective-permute-start.9 = (bf16[80,640]{1,0:T(8,128)(2,1)S(1)}, bf16[80,640]{1,0:T(8,128)(2,1)S(1)}, u32[]{:S(2)}, u32[]{:S(2)}) collective-permute-start(bf16[80,640]{1,0:T(8,128)(2,1)S(1)} %get-tuple-element.53), channel_id=1, source_target_pairs={{0,4},{1,5},{2,6},{3,7},{4,0},{5,1},{6,2},{7,3},{8,12},{9,13},{10,... | collective-permute-start | bytes 307208 | tf_op jit(solution)/shard_map/ppermute | solution.py:381
where the time goes:
time: 113 us
  starting transfers between devices  47.3 us (42%)
  waiting for transfers between devices  30.6 us (27%)
  Pallas kernels  23.4 us (21%)
  local copies, waits for them, and re-layouts  11.4 us (10%)
    ppermute x21, starting transfers between devices, exchange(): lax.ppermute(pieces[k], 'dp', [(d, d ^ k) for d in range(n)])  40 us
    ppermute x21, waiting for transfers between devices, exchange(): lax.ppermute(pieces[k], 'dp', [(d, d ^ k) for d in range(n)])  20 us
    pallas_call x1, Pallas kernels, on_device(): call(functools.partial(middle_kernel, z, scale), [pair, pair, nine, one],...  14.2 us
    unnamed x30, local copies, waits for them, and re-layouts  10.8 us
    ppermute x6, waiting for transfers between devices, across(): return lax.ppermute(x, 'section', [(s, s ^ bit) for s in range(n_section)])  10.6 us
    ppermute x6, starting transfers between devices, across(): return lax.ppermute(x, 'section', [(s, s ^ bit) for s in range(n_section)])  7.3 us
    pallas_call x1, Pallas kernels, on_device(): call(functools.partial(weight_kernel, z), jax.ShapeDtypeStruct((z.share,...  3.42 us
  transfers between devices with their start and end apart: 27, of which 9 were waited for; matrix products, arithmetic and copies ran while one was open for 2% of the time, Pallas kernels for 4%

commit v1 on v0

v1 whole, which is shorter than its diff:
```python
import functools

import jax
import jax.numpy as jnp
import numpy as np
from jax import lax
from jax.experimental import pallas as pl
from jax.experimental.pallas import tpu as pltpu
from jax.sharding import PartitionSpec as P

BF = jnp.bfloat16
F32 = jnp.float32
TAPS = [(a, b) for a in range(3) for b in range(3)]
PARITIES = [(r, s) for r in range(2) for s in range(2)]


def offset_of(parity, tap):
    return (parity + tap - 1) // 2


def dot(left, right, dims=((1,), (0,))):
    return lax.dot_general(left, right, (dims, ((), ())), preferred_element_type=F32)


def dot_nt(left, right):
    return dot(left, right, ((1,), (1,)))


def dot_tn(left, right):
    return dot(left, right, ((0,), (0,)))


def sigmoid(v):
    return 1.0 / (1.0 + jnp.exp(-v))


def silu(v):
    return v * sigmoid(v)


def slope(v):
    g = sigmoid(v)
    return g * (1.0 + v * (1.0 - g))


class Sizes:
    def __init__(self, images, kernel, dp):
        self.micro = images.shape[0]
        self.full = images.shape[2]
        self.half = self.full // 2
        self.taps_rows, self.width = kernel.shape
        self.chan = self.taps_rows // 9
        self.cells = self.half * self.half
        self.rows = -(-self.cells // 8) * 8
        self.both = self.micro * self.rows
        self.group = self.width // 2
        self.low = -(-self.group // 128) * 128
        self.high = self.group // 128 * 128
        self.fine = self.full * self.full
        self.dp = dp
        self.share = self.taps_rows // dp


def selectors(z):
    rows, n = z.rows, z.half
    shift = np.zeros((9, rows, rows), np.float32)
    enc = np.zeros((9, z.micro, rows, z.micro, z.fine), np.float32)
    parity = np.zeros((4, rows, z.fine), np.float32)
    gather = np.zeros((9, rows, 4, rows), np.float32)
    for i in range(n):
        for j in range(n):
            r = i * n + j
            for t, (a, b) in enumerate(TAPS):
                ii, jj = i + a - 1, j + b - 1
                if 0 <= ii < n and 0 <= jj < n:
                    shift[t, r, ii * n + jj] = 1
                ii, jj = 2 * i + a - 1, 2 * j + b - 1
                if 0 <= ii < z.full and 0 <= jj < z.full:
                    for m in range(z.micro):
                        enc[t, m, r, m, ii * z.full + jj] = 1
                for p, (pr, ps) in enumerate(PARITIES):
                    ii, jj = i + offset_of(pr, a), j + offset_of(ps, b)
                    if 0 <= ii < n and 0 <= jj < n:
                        gather[t, ii * n + jj, p, r] = 1
            for p, (pr, ps) in enumerate(PARITIES):
                parity[p, r, (2 * i + pr) * z.full + 2 * j + ps] = 1
    back = shift.transpose(0, 2, 1)
    return dict(
        shift=shift.reshape(9 * rows, rows),
        back=back.reshape(9 * rows, rows),
        enc=enc.reshape(9 * z.both, z.micro * z.fine),
        parity=parity.reshape(4 * rows, z.fine),
        gather=gather.reshape(9 * rows, 4 * rows),
    )


def lanes(shape):
    return lax.broadcasted_iota(jnp.int32, shape, 1)


def join_columns(z, first, second):
    overlap = z.low - z.high
    if overlap == 0:
        return jnp.concatenate([first, second], axis=1)
    mid_first = first[:, z.high :]
    mid = jnp.where(lanes(mid_first.shape) < z.group - z.high, mid_first, second[:, :overlap])
    return jnp.concatenate([first[:, : z.high], mid, second[:, overlap:]], axis=1)


def split_groups(z, value):
    swapped = pltpu.roll(value.astype(F32), z.group, 1).astype(BF)
    return value[:, : z.group], swapped[:, : z.group]


def tap_rows(z, t):
    return slice(t * z.rows, (t + 1) * z.rows)


class Weights:
    def __init__(self, z, mine, own, other, buffer, sems):
        self.z, self.buffer, self.seen = z, buffer, set()

        def copies(source):
            for t in range(9):
                rows = pl.ds(t * z.chan, z.chan)
                yield pltpu.make_async_copy(source.at[rows], buffer.at[rows], sems.at[t])

        self.waits = list(copies(own))
        if mine is None:
            for copy in self.waits:
                copy.start()
            return

        @pl.when(mine)
        def _():
            for copy in copies(own):
                copy.start()

        @pl.when(jnp.logical_not(mine))
        def _():
            for copy in copies(other):
                copy.start()

    def tap(self, t, columns=slice(None)):
        if t not in self.seen:
            self.seen.add(t)
            self.waits[t].wait()
        return self.buffer[pl.ds(t * self.z.chan, self.z.chan), columns]

    def first(self, t):
        return self.tap(t, slice(0, self.z.low))

    def second(self, t):
        return self.tap(t, slice(self.z.high, self.z.width))


def conv_forward(z, value, weights, shift):
    first, second = split_groups(z, value)
    first = dot(shift[...], first).astype(BF)
    second = dot(shift[...], second).astype(BF)
    total_first = total_second = None
    for t in range(9):
        a = dot(first[tap_rows(z, t)], weights.first(t))
        b = dot(second[tap_rows(z, t)], weights.second(t))
        total_first = a if total_first is None else total_first + a
        total_second = b if total_second is None else total_second + b
    return join_columns(z, total_first, total_second)


def join_groups(z, first, second, scratch):
    scratch[0, :, : z.group] = first
    scratch[1, :, : z.group] = second
    left = scratch[0]
    right = pltpu.roll(scratch[1], z.group, 1)
    return jnp.where(lanes(left.shape) < z.group, left, right)


def rows_times_kernel(z, first, second, weights, scratch):
    total_first = total_second = None
    for t in range(9):
        a = dot_nt(first[tap_rows(z, t)], weights.first(t))
        b = dot_nt(second[tap_rows(z, t)], weights.second(t))
        total_first = a if total_first is None else total_first + a
        total_second = b if total_second is None else total_second + b
    return join_groups(z, total_first, total_second, scratch)


def conv_backward(z, delta, weights, back, scratch):
    first = delta[:, : z.low].astype(F32)
    first = jnp.where(lanes(first.shape) < z.group, first, 0.0).astype(BF)
    second = delta[:, z.high :].astype(F32)
    second = jnp.where(lanes(second.shape) >= z.group - z.high, second, 0.0).astype(BF)
    first = dot(back[...], first).astype(BF)
    second = dot(back[...], second).astype(BF)
    return rows_times_kernel(z, first, second, weights, scratch)


def encoder_kernel(z, kernel, images, enc, out, patches_out, buffer, sems):
    weights = Weights(z, None, kernel, None, buffer, sems)
    columns = dot(enc[...], images[...]).astype(BF)
    total = None
    for t in range(9):
        part = columns[t * z.both : (t + 1) * z.both]
        patches_out[t, :, : z.chan] = part
        a = dot(part, weights.tap(t))
        total = a if total is None else total + a
    encoded = silu(total).astype(BF)
    steep = slope(total).astype(BF)
    for m in range(z.micro):
        out[m] = encoded[m * z.rows : (m + 1) * z.rows]
        out[z.micro + m] = steep[m * z.rows : (m + 1) * z.rows]


def centre_kernel(z, where, kernel, other, own, received, shift, out, slope_out, enc_slope_out, buffer, sems):
    odd = lax.rem(where[0], 2) == 1
    weights = Weights(z, odd, kernel, other, buffer, sems)
    value = jnp.where(odd, received[1].astype(F32), own[0].astype(F32)).astype(BF)
    enc_slope_out[...] = jnp.where(odd, received[3].astype(F32), own[2].astype(F32))
    preact = conv_forward(z, value, weights, shift)
    out[0] = value
    out[1] = (value.astype(F32) + silu(preact)).astype(BF)
    slope_out[...] = slope(preact)


def middle_kernel(
    z, scale, where, kernel, other, inbound, targets, shift, back, parity, gather,
    grads, own_out, send, scratch, delta_p, delta_q, sums_p, sums_q, buffer2, buffer3, sems2, sems3,
):
    odd = lax.rem(where[0], 2) == 1
    centre = Weights(z, jnp.logical_not(odd), kernel, other, buffer2, sems2)
    decoder = Weights(z, odd, kernel, other, buffer3, sems3)
    scratch[...] = jnp.zeros_like(scratch)
    encoded = inbound[0]
    hidden = inbound[1]
    preact = conv_forward(z, hidden, centre, shift)
    hidden3 = (hidden.astype(F32) + silu(preact)).astype(BF)
    joined = (hidden3.astype(F32) + encoded.astype(F32)).astype(BF)
    first, second = split_groups(z, joined)
    first = dot(shift[...], first).astype(BF)
    second = dot(shift[...], second).astype(BF)
    total_p = [None] * 4
    total_q = [None] * 4
    for t, (a, b) in enumerate(TAPS):
        shifts = sorted({(offset_of(r, a), offset_of(s, b)) for r, s in PARITIES})
        blocks = [tap_rows(z, (i + 1) * 3 + j + 1) for i, j in shifts]
        left_p = jnp.concatenate([first[block] for block in blocks], axis=0)
        left_q = jnp.concatenate([second[block] for block in blocks], axis=0)
        part_p = dot(left_p, decoder.first(t))
        part_q = dot(left_q, decoder.second(t))
        for p, (r, s) in enumerate(PARITIES):
            at = tap_rows(z, shifts.index((offset_of(r, a), offset_of(s, b))))
            total_p[p] = part_p[at] if total_p[p] is None else total_p[p] + part_p[at]
            total_q[p] = part_q[at] if total_q[p] is None else total_q[p] + part_q[at]
    wanted = dot(parity[...], targets[lax.rem(where[0], 2)])
    move = z.group - z.high
    delta_p[...] = jnp.zeros_like(delta_p)
    delta_q[...] = jnp.zeros_like(delta_q)
    for p in range(4):
        value = total_p[p][:, : z.group]
        gate = total_q[p]
        if move:
            gate = pltpu.roll(gate, z.low - move, 1)
        gate = gate[:, : z.group]
        act = silu(gate)
        residual = (value * act - wanted[tap_rows(z, p)]) * scale
        delta_p[tap_rows(z, p), : z.group] = residual * act
        delta_q[tap_rows(z, p), : z.group] = residual * value * slope(gate)
    moved = delta_q[...]
    if move:
        moved = pltpu.roll(moved, move, 1)
    sums_p[...] = dot(gather[...], delta_p[...].astype(BF)).astype(BF)
    sums_q[...] = dot(gather[...], moved.astype(BF)).astype(BF)
    grad = rows_times_kernel(z, sums_p, sums_q, decoder, scratch).astype(BF)
    delta = (grad.astype(F32) * slope(preact)).astype(BF)
    flow = conv_backward(z, delta, centre, back, scratch)
    grads[0] = (grad.astype(F32) + flow).astype(BF)
    grads[1] = grad

    def sums(t):
        part_p = sums_p[tap_rows(z, t)].astype(F32)
        part_q = sums_q[tap_rows(z, t)].astype(F32)
        return join_columns(z, part_p, part_q).astype(BF)

    @pl.when(odd)
    def _():
        for t in range(9):
            own_out[t] = sums(t)
        own_out[9] = joined
        send[0] = delta
        send[1] = hidden

    @pl.when(jnp.logical_not(odd))
    def _():
        for t in range(9):
            send[t] = sums(t)
        own_out[0] = delta
        own_out[1] = hidden
        own_out[9] = joined


def centre_back_kernel(
    z, where, kernel, other, grads, enc_slope, centre_slope, back, own_out, send, scratch, buffer, sems
):
    odd = lax.rem(where[0], 2) == 1
    weights = Weights(z, odd, kernel, other, buffer, sems)
    scratch[...] = jnp.zeros_like(scratch)
    above = grads[0].astype(F32)
    delta = (above * centre_slope[...]).astype(BF)
    flow = conv_backward(z, delta, weights, back, scratch)
    below = (above + flow).astype(BF)
    total = below.astype(F32) + grads[1].astype(F32)
    deep = total * enc_slope[...]
    own_out[...] = jnp.where(odd, delta.astype(F32), deep).astype(BF)
    send[...] = jnp.where(odd, deep, delta.astype(F32)).astype(BF)


def first_tap(z, dest):
    return dest * z.share // z.chan


def prepare_first_kernel(z, where, patches, own, received, middle_own, middle_received, out, joined):
    section = where[0]
    n, rows = z.dp, z.rows

    @pl.when(section == 0)
    def _():
        for k in range(n):
            tap = first_tap(z, k)
            near = patches[tap].astype(F32)
            far = patches[min(tap + 1, 8)].astype(F32)
            both = jnp.where(lanes(near.shape) < z.chan, near, pltpu.roll(far, z.chan, 1))
            out[k] = both.astype(BF)

    @pl.when(section == 1)
    def _():
        for k in range(n):
            out[k, :rows] = received[0]
            out[k, rows:] = received[1]

    @pl.when(section == 2)
    def _():
        for k in range(n):
            out[k, :rows] = middle_own[1]
            out[k, rows:] = middle_received[1]

    @pl.when(section == 3)
    def _():
        for k in range(n):
            tap = first_tap(z, k)
            out[k, :rows] = middle_received[tap]
            out[k, rows:] = middle_own[tap]

    for k in range(n):
        joined[k] = middle_own[9]


def prepare_second_kernel(z, where, back_own, back_received, middle_own, middle_received, out):
    section = where[0]
    n, rows = z.dp, z.rows

    def fill(top, bottom):
        for k in range(n):
            out[k, :rows] = top[...]
            out[k, rows:] = bottom[...]

    pl.when(section == 0)(lambda: fill(back_own, back_received))
    pl.when(section == 1)(lambda: fill(back_received, back_own))
    pl.when(section == 2)(lambda: fill(middle_own.at[0], middle_received.at[0]))

    @pl.when(section == 3)
    def _():
        for k in range(n):
            tap = min(first_tap(z, k) + 1, 8)
            out[k, :rows] = middle_received[tap]
            out[k, rows:] = middle_own[tap]


def weight_kernel(z, where, shift, left, right, joined, joined_received, out, lefts, rows_out):
    n = z.dp
    section, place = where[0], where[1]
    tap = first_tap(z, place)
    total = n * z.both

    def grouped(at, pairs):
        first = second = None
        for a, b in pairs:
            one = dot_tn(a[:, : z.low], b[:, : z.low])
            two = dot_tn(a[:, z.high :], b[:, z.high :])
            first = one if first is None else first + one
            second = two if second is None else second + two
        move = z.group - z.high
        both = join_columns(z, first[: z.chan], second[move : move + z.chan])
        rows_out[pl.ds(at * z.chan, z.chan), :] = both

    @pl.when(section == 0)
    def _():
        a = left[...].reshape(total, z.width)
        b = right[...].reshape(total, z.width)
        rows_out[...] = dot_tn(a, b)

    @pl.when(jnp.logical_or(section == 1, section == 2))
    def _():
        for at in range(2):
            here = jnp.minimum(tap + at, 8)
            move = shift[pl.ds(pl.multiple_of(here * z.rows, 8), z.rows), :]
            for k in range(n):
                for m in range(z.micro):
                    part = left[k, pl.ds(m * z.rows, z.rows)]
                    lefts[pl.ds((k * z.micro + m) * z.rows, z.rows), :] = dot(move, part).astype(BF)
            grouped(at, [(lefts[...], right[...].reshape(total, z.width))])

    @pl.when(section == 3)
    def _():
        for k in range(n):
            lefts[pl.ds(k * z.both, z.rows), :] = joined_received[k]
            lefts[pl.ds(k * z.both + z.rows, z.rows), :] = joined[k]
        grouped(0, [(lefts[...], left[...].reshape(total, z.width))])
        grouped(1, [(lefts[...], right[...].reshape(total, z.width))])

    begin = place * z.share - tap * z.chan
    if z.share % 8 == 0 and z.chan % 8 == 0:
        out[...] = rows_out[pl.ds(pl.multiple_of(begin, 8), z.share), :]
    else:
        size = -(-(z.share + 7) // 8) * 8
        rest = lax.rem(begin, 8)
        block = rows_out[pl.ds(pl.multiple_of(begin - rest, 8), size), :]
        out[...] = pltpu.roll(block, lax.rem(size - rest, size), 0)[: z.share]


def call(body, outs, spaces, scratch=()):
    kinds = dict(s=pltpu.SMEM, h=pltpu.HBM, v=pltpu.VMEM)
    single = not isinstance(outs, (list, tuple))
    vmem = pl.BlockSpec(memory_space=pltpu.VMEM)
    return pl.pallas_call(
        body,
        out_shape=outs,
        in_specs=[pl.BlockSpec(memory_space=kinds[k]) for k in spaces],
        out_specs=vmem if single else [vmem] * len(outs),
        scratch_shapes=list(scratch),
        compiler_params=pltpu.CompilerParams(vmem_limit_bytes=40 * 2**20),
    )


def on_device(images, targets, kernels):
    kernel = kernels[0]
    dp = lax.axis_size("dp")
    n_section = lax.axis_size("section")
    z = Sizes(images, kernel, dp)
    sel = {k: jnp.asarray(v, BF) for k, v in selectors(z).items()}
    scale = 1.0 / (z.micro * dp * images.shape[1])
    where = jnp.stack([lax.axis_index("section"), lax.axis_index("dp")]).astype(jnp.int32)
    image_rows = images.reshape(z.micro * z.fine, z.chan)
    target_rows = targets.reshape(z.micro, z.fine, z.chan)
    rows, width, both = z.rows, z.width, z.both

    def shape(*dims, dtype=BF):
        return jax.ShapeDtypeStruct(dims, dtype)

    join = pltpu.VMEM((2, rows, width), F32)
    buffer = pltpu.VMEM((z.taps_rows, width), BF)
    sems = pltpu.SemaphoreType.DMA((9,))

    def across(x, bit):
        return lax.ppermute(x, "section", [(s, s ^ bit) for s in range(n_section)])

    def spread(x):
        return lax.all_to_all(x, "dp", 0, 0, tiled=True)

    other = across(kernel, 1)
    encoded, patches = call(
        functools.partial(encoder_kernel, z),
        [shape(2 * z.micro, rows, width), shape(9, both, width)],
        "hvv",
        [buffer, sems],
    )(kernel, image_rows, sel["enc"])
    encoded_in = across(encoded, 1)
    forward, centre_slope, enc_slope = call(
        functools.partial(centre_kernel, z),
        [shape(2, rows, width), shape(rows, width, dtype=F32), shape(rows, width, dtype=F32)],
        "shhvvv",
        [buffer, sems],
    )(where, kernel, other, encoded, encoded_in, sel["shift"])
    forward_in = across(forward, 2)
    grads, middle_own, middle_send = call(
        functools.partial(middle_kernel, z, scale),
        [shape(2, rows, width), shape(10, rows, width), shape(9, rows, width)],
        "shhvvvvvv",
        [
            join,
            pltpu.VMEM((4 * rows, z.low), F32),
            pltpu.VMEM((4 * rows, z.low), F32),
            pltpu.VMEM((9 * rows, z.low), BF),
            pltpu.VMEM((9 * rows, z.width - z.high), BF),
            buffer,
            buffer,
            sems,
            sems,
        ],
    )(
        where, kernel, other, forward_in, target_rows,
        sel["shift"], sel["back"], sel["parity"], sel["gather"],
    )
    grads_in = across(grads, 2)
    middle_in = across(middle_send, 1)
    first, joined = call(
        functools.partial(prepare_first_kernel, z),
        [shape(dp, both, width), shape(dp, rows, width)],
        "svvvvv",
    )(where, patches, encoded, encoded_in, middle_own, middle_in)
    left = spread(first)
    back_own, back_send = call(
        functools.partial(centre_back_kernel, z),
        [shape(rows, width), shape(rows, width)],
        "shhvvvv",
        [join, buffer, sems],
    )(where, kernel, other, grads_in, enc_slope, centre_slope, sel["back"])
    back_in = across(back_send, 1)
    second = call(functools.partial(prepare_second_kernel, z), shape(dp, both, width), "svvvv")(
        where, back_own, back_in, middle_own, middle_in
    )
    right = spread(second)
    joined = spread(joined)
    joined_in = across(joined, 1)
    out = call(
        functools.partial(weight_kernel, z),
        shape(z.share, width, dtype=F32),
        "svvvvv",
        [pltpu.VMEM((dp * both, width), BF), pltpu.VMEM((2 * z.chan, width), F32)],
    )(where, sel["shift"], left, right, joined, joined_in)
    return out[None]


def solution(mesh):
    return jax.shard_map(
        on_device,
        mesh=mesh,
        in_specs=(P(None, "dp", None, None), P(None, "dp", None, None), P("section", None, None)),
        out_specs=P("section", "dp", None),
        check_vma=False,
    )
```

time: 113 us -> 109 us (0.965); the launches traced: 113 us -> 107 us
  starting transfers between devices: 47.3 us -> 16.1 us
  blocking collectives: 0 us -> 17.4 us
  Pallas kernels: 23.4 us -> 30.7 us
  waiting for transfers between devices: 30.6 us -> 32.3 us
    ppermute x21 -> x0, starting transfers between devices: 40 us -> none  [exchange(): lax.ppermute(pieces[k], 'dp', [(d, d ^ k) for d in range(n)])]
    all_to_all x0 -> x2, waiting for transfers between devices: none -> 23.2 us  [spread(): return lax.all_to_all(x, 'dp', 0, 0, tiled=True)]
    ppermute x21 -> x0, waiting for transfers between devices: 20 us -> none  [exchange(): lax.ppermute(pieces[k], 'dp', [(d, d ^ k) for d in range(n)])]
    all_to_all x0 -> x1, blocking collectives: none -> 17.4 us  [spread(): return lax.all_to_all(x, 'dp', 0, 0, tiled=True)]
    all_to_all x0 -> x2, starting transfers between devices: none -> 8.92 us  [spread(): return lax.all_to_all(x, 'dp', 0, 0, tiled=True)]
    pallas_call x6 -> x7, Pallas kernels: 23.4 us -> 30.7 us  [the longest x1 11.2 us: on_device(): call(functools.partial(middle_kernel, z, scale), [shape(2, rows, width),...]
    ppermute x6 -> x7, waiting for transfers between devices: 10.6 us -> 9.09 us  [across(): return lax.ppermute(x, 'section', [(s, s ^ bit) for s in range(n_section)])]
    unnamed x30 -> x24, local copies, waits for them, and re-layouts: 10.8 us -> 10.2 us
  transfers between devices with their start and end apart: 27 -> 9, of which waited for: 9 -> 8; matrix products, arithmetic and copies ran while one was open for 2% -> 2% of each run, Pallas kernels for 4% -> 10%
where the time goes in v1:
time: 109 us; the launch traced here: 107 us
  waiting for transfers between devices  32.3 us (30%)
  Pallas kernels  30.7 us (28%)
  blocking collectives  17.4 us (16%)
  starting transfers between devices  16.1 us (15%)
  local copies, waits for them, and re-layouts  10.9 us (10%)
    all_to_all x2, waiting for transfers between devices, spread(): return lax.all_to_all(x, 'dp', 0, 0, tiled=True)  23.2 us
    all_to_all x1, blocking collectives, spread(): return lax.all_to_all(x, 'dp', 0, 0, tiled=True)  17.4 us
    pallas_call x1, Pallas kernels, on_device(): call(functools.partial(middle_kernel, z, scale), [shape(2, rows, width),...  11.2 us
    unnamed x24, local copies, waits for them, and re-layouts  10.2 us
    ppermute x7, waiting for transfers between devices, across(): return lax.ppermute(x, 'section', [(s, s ^ bit) for s in range(n_section)])  9.09 us
    all_to_all x2, starting transfers between devices, spread(): return lax.all_to_all(x, 'dp', 0, 0, tiled=True)  8.92 us
    ppermute x7, starting transfers between devices, across(): return lax.ppermute(x, 'section', [(s, s ^ bit) for s in range(n_section)])  7.17 us
    pallas_call x1, Pallas kernels, on_device(): call(functools.partial(centre_back_kernel, z), [shape(rows, width), shape...  4.66 us
  transfers between devices with their start and end apart: 9, of which 8 were waited for; matrix products, arithmetic and copies ran while one was open for 2% of the time, Pallas kernels for 10%

profile of v1, /device:TPU:1, one launch (start us, length us, event | category | flops | bytes accessed | tf_op | source)
XLA Modules:
  0.0 107.5 jit_solution(4306701026088735741)
XLA Ops:
  0.0 0.0 copy-start.4
  0.0 0.0 collective-permute-start.1
  0.0 1.0 copy.11
  1.0 0.3 reshape.6.images
  1.3 0.0 copy-start
  1.3 2.0 %copy-done = bf16[1,2880,640]{2,1,0:T(8,128)(2,1)S(1)} copy-done((bf16[1,2880,640]{2,1,0:T(8,128)(2,1)S(1)}, bf16[1,2880,640]{2,1,0:T(8,128)(2,1)}, u32[]{:S(2)}) %copy-start) | copy-done | bytes 3686424
  3.4 0.0 copy-start.6
  3.4 1.0 copy-done.6
  4.4 4.5 %shard_map.82 = (bf16[4,40,640]{2,1,0:T(8,128)(2,1)S(1)}, bf16[9,80,640]{2,1,0:T(8,128)(2,1)S(1)}) custom-call(bf16[2880,640]{1,0:T(8,128)(2,1)S(1)} %bitcast.9, bf16[288,320]{1,0:T(8,128)(2,1)S(1)} %reshape.6.images, bf16[720,288]{1,0:T(8,128)(2,1)S(1)} %copy-done.6), custom_call_target="tpu_custom_call" | custom-call | tf_op jit(solution)/shard_map/pallas_call | solution.py:470
  8.9 0.5 collective-permute-start
  9.4 0.1 pad_add_fusion.where
  9.5 1.0 collective-permute-done.received
  10.5 0.0 collective-permute-done.1.other
  10.5 0.0 copy-done.4
  10.5 0.0 copy-start.1
  10.5 2.0 %copy-done.1 = bf16[1,2880,640]{2,1,0:T(8,128)(2,1)S(1)} copy-done((bf16[1,2880,640]{2,1,0:T(8,128)(2,1)S(1)}, bf16[1,2880,640]{2,1,0:T(8,128)(2,1)}, u32[]{:S(2)}) %copy-start.1) | copy-done | bytes 3686424
  12.5 0.0 copy-start.10
  12.5 0.0 copy-start.7
  12.5 0.0 copy-start.8
  12.5 0.0 copy-start.9
  12.5 4.6 %shard_map.83 = (bf16[2,40,640]{2,1,0:T(8,128)(2,1)S(1)}, f32[40,640]{1,0:T(8,128)S(1)}, f32[40,640]{1,0:T(8,128)S(1)}) custom-call(s32[2]{0:T(128)S(1)} %pad_add_fusion.where, bf16[2880,640]{1,0:T(8,128)(2,1)S(1)} %bitcast.10, bf16[2880,640]{1,0:T(8,128)(2,1)} %collective-permute-done.1.other, bf16[4,40,640]{2,1,0:T(8,128)(2,1)S(1)} %get-tuple-element.18.own, ...), custom_call_target="tpu_custom_call" | custom-call | tf_op jit(solution)/shard_map/pallas_call | solution.py:477
  17.1 2.6 %collective-permute-start.2 = (bf16[2,40,640]{2,1,0:T(8,128)(2,1)S(1)}, bf16[2,40,640]{2,1,0:T(8,128)(2,1)S(1)}, u32[]{:S(2)}, u32[]{:S(2)}) collective-permute-start(bf16[2,40,640]{2,1,0:T(8,128)(2,1)S(1)} %get-tuple-element.19), channel_id=1, source_target_pairs={{0,16},{8,24},{16,0},{24,8},{1,17},{9,25},{17,1},{25,9},{2,18},{10... | collective-permute-start | bytes 307208 | tf_op jit(solution)/shard_map/ppermute | solution.py:464
  19.8 0.0 copy-done.10
  19.8 0.3 reshape.7.targets
  20.1 2.0 %collective-permute-done.2.inbound = bf16[2,40,640]{2,1,0:T(8,128)(2,1)S(1)} collective-permute-done((bf16[2,40,640]{2,1,0:T(8,128)(2,1)S(1)}, bf16[2,40,640]{2,1,0:T(8,128)(2,1)S(1)}, u32[]{:S(2)}, u32[]{:S(2)}) %collective-permute-start.2) | collective-permute-done | bytes 102432 | tf_op jit(solution)/shard_map/ppermute | solution.py:464
  22.1 0.0 copy-done.7
  22.1 0.0 copy-done.8
  22.1 0.0 copy-done.9
  22.1 0.0 copy-start.2
  22.1 2.0 %copy-done.2 = bf16[1,2880,640]{2,1,0:T(8,128)(2,1)S(1)} copy-done((bf16[1,2880,640]{2,1,0:T(8,128)(2,1)S(1)}, bf16[1,2880,640]{2,1,0:T(8,128)(2,1)}, u32[]{:S(2)}) %copy-start.2) | copy-done | bytes 3686424
  24.1 11.2 %shard_map.84 = (bf16[2,40,640]{2,1,0:T(8,128)(2,1)S(1)}, bf16[10,40,640]{2,1,0:T(8,128)(2,1)S(1)}, bf16[9,40,640]{2,1,0:T(8,128)(2,1)S(1)}) custom-call(s32[2]{0:T(128)S(1)} %pad_add_fusion.where, bf16[2880,640]{1,0:T(8,128)(2,1)S(1)} %bitcast.11, bf16[2880,640]{1,0:T(8,128)(2,1)} %collective-permute-done.1.other, ...), custom_call_target="tpu_custom_call" | custom-call | tf_op jit(solution)/shard_map/pallas_call | solution.py:484
  35.4 0.1 collective-permute-start.3
  35.5 1.8 %collective-permute-done.3.middle_received = bf16[9,40,640]{2,1,0:T(8,128)(2,1)S(1)} collective-permute-done((bf16[9,40,640]{2,1,0:T(8,128)(2,1)S(1)}, bf16[9,40,640]{2,1,0:T(8,128)(2,1)S(1)}, u32[]{:S(2)}, u32[]{:S(2)}) %collective-permute-start.3) | collective-permute-done | bytes 460832 | tf_op jit(solution)/shard_map/ppermute | solution.py:464
  37.3 0.7 shard_map.85
  37.9 0.0 copy-start.5
  37.9 17.4 %all_to_all.15.joined = bf16[8,40,640]{2,1,0:T(8,128)(2,1)S(1)} all-to-all(bf16[8,40,640]{2,1,0:T(8,128)(2,1)S(1)} %get-tuple-element.28), channel_id=1, replica_groups=mesh['section'=4,'dp'=8] {'dp'}, dimensions={0} | all-to-all | bytes 819200 | tf_op jit(solution)/shard_map/all_to_all | solution.py:467
  55.3 0.0 copy-done.5
  55.3 4.0 %all-to-all-start = ((bf16[8,80,640]{2,1,0:T(8,128)(2,1)}), bf16[8,80,640]{2,1,0:T(8,128)(2,1)S(1)}, u32[]{:S(2)}, u32[]{:S(2)}) async-start(bf16[8,80,640]{2,1,0:T(8,128)(2,1)} %copy-done.5), calls=%async_computation | async-start | bytes 1638400 | tf_op jit(solution)/shard_map/all_to_all | solution.py:467
  59.3 1.5 %collective-permute-start.4 = (bf16[2,40,640]{2,1,0:T(8,128)(2,1)S(1)}, bf16[2,40,640]{2,1,0:T(8,128)(2,1)S(1)}, u32[]{:S(2)}, u32[]{:S(2)}) collective-permute-start(bf16[2,40,640]{2,1,0:T(8,128)(2,1)S(1)} %get-tuple-element.23), channel_id=1, source_target_pairs={{0,16},{8,24},{16,0},{24,8},{1,17},{9,25},{17,1},{25,9},{2,18},{10... | collective-permute-start | bytes 307208 | tf_op jit(solution)/shard_map/ppermute | solution.py:464
  60.8 2.0 %collective-permute-done.4.grads = bf16[2,40,640]{2,1,0:T(8,128)(2,1)S(1)} collective-permute-done((bf16[2,40,640]{2,1,0:T(8,128)(2,1)S(1)}, bf16[2,40,640]{2,1,0:T(8,128)(2,1)S(1)}, u32[]{:S(2)}, u32[]{:S(2)}) %collective-permute-start.4) | collective-permute-done | bytes 102432 | tf_op jit(solution)/shard_map/ppermute | solution.py:464
  62.8 0.0 copy-start.3
  62.8 2.0 %copy-done.3 = bf16[1,2880,640]{2,1,0:T(8,128)(2,1)S(1)} copy-done((bf16[1,2880,640]{2,1,0:T(8,128)(2,1)S(1)}, bf16[1,2880,640]{2,1,0:T(8,128)(2,1)}, u32[]{:S(2)}) %copy-start.3) | copy-done | bytes 3686424
  64.9 4.7 %shard_map.86 = (bf16[40,640]{1,0:T(8,128)(2,1)S(1)}, bf16[40,640]{1,0:T(8,128)(2,1)S(1)}) custom-call(s32[2]{0:T(128)S(1)} %pad_add_fusion.where, bf16[2880,640]{1,0:T(8,128)(2,1)S(1)} %bitcast.12, bf16[2880,640]{1,0:T(8,128)(2,1)} %collective-permute-done.1.other, bf16[2,40,640]{2,1,0:T(8,128)(2,1)S(1)} %collective-permute-done.4.grads, ...), custom_call_target="tpu_custom_call" | custom-call | tf_op jit(solution)/shard_map/pallas_call | solution.py:511
  69.5 1.5 %collective-permute-start.5 = (bf16[40,640]{1,0:T(8,128)(2,1)S(1)}, bf16[40,640]{1,0:T(8,128)(2,1)S(1)}, u32[]{:S(2)}, u32[]{:S(2)}) collective-permute-start(bf16[40,640]{1,0:T(8,128)(2,1)S(1)} %get-tuple-element.27), channel_id=1, source_target_pairs={{0,8},{8,0},{16,24},{24,16},{1,9},{9,1},{17,25},{25,17},{2,10},{10... | collective-permute-start | bytes 153608 | tf_op jit(solution)/shard_map/ppermute | solution.py:464
  71.0 0.9 collective-permute-done.5.back_received
  71.9 1.5 %shard_map.87 = bf16[8,80,640]{2,1,0:T(8,128)(2,1)} custom-call(s32[2]{0:T(128)S(1)} %pad_add_fusion.where, bf16[40,640]{1,0:T(8,128)(2,1)S(1)} %get-tuple-element.26.back_own, bf16[40,640]{1,0:T(8,128)(2,1)S(1)} %collective-permute-done.5.back_received, bf16[10,40,640]{2,1,0:T(8,128)(2,1)S(1)} %get-tuple-element.20.middle_own, ...), custom_call_target="tpu_custom_call" | custom-call | tf_op jit(solution)/shard_map/pallas_call | solution.py:518
  73.4 5.5 %all-to-all-done.left = bf16[8,80,640]{2,1,0:T(8,128)(2,1)S(1)} async-done(((bf16[8,80,640]{2,1,0:T(8,128)(2,1)}), bf16[8,80,640]{2,1,0:T(8,128)(2,1)S(1)}, u32[]{:S(2)}, u32[]{:S(2)}) %all-to-all-start) | async-done | bytes 819232 | tf_op jit(solution)/shard_map/all_to_all | solution.py:467
  79.0 4.9 %all-to-all-start.1 = ((bf16[8,80,640]{2,1,0:T(8,128)(2,1)}), bf16[8,80,640]{2,1,0:T(8,128)(2,1)S(1)}, u32[]{:S(2)}, u32[]{:S(2)}) async-start(bf16[8,80,640]{2,1,0:T(8,128)(2,1)} %shard_map.87), calls=%async_computation.1 | async-start | bytes 1638400 | tf_op jit(solution)/shard_map/all_to_all | solution.py:467
  83.9 0.9 collective-permute-start.6
  84.8 1.4 %collective-permute-done.6.joined_received = bf16[8,40,640]{2,1,0:T(8,128)(2,1)S(1)} collective-permute-done((bf16[8,40,640]{2,1,0:T(8,128)(2,1)S(1)}, bf16[8,40,640]{2,1,0:T(8,128)(2,1)S(1)}, u32[]{:S(2)}, u32[]{:S(2)}) %collective-permute-start.6) | collective-permute-done | bytes 409632 | tf_op jit(solution)/shard_map/ppermute | solution.py:464
  86.2 17.7 %all-to-all-done.1.right = bf16[8,80,640]{2,1,0:T(8,128)(2,1)S(1)} async-done(((bf16[8,80,640]{2,1,0:T(8,128)(2,1)}), bf16[8,80,640]{2,1,0:T(8,128)(2,1)S(1)}, u32[]{:S(2)}, u32[]{:S(2)}) %all-to-all-start.1) | async-done | bytes 819232 | tf_op jit(solution)/shard_map/all_to_all | solution.py:467
  103.9 3.5 %shard_map.88 = f32[360,640]{1,0:T(8,128)} custom-call(s32[2]{0:T(128)S(1)} %pad_add_fusion.where, bf16[360,40]{1,0:T(8,128)(2,1)S(1)} %copy-done.4, bf16[8,80,640]{2,1,0:T(8,128)(2,1)S(1)} %all-to-all-done.left, bf16[8,80,640]{2,1,0:T(8,128)(2,1)S(1)} %all-to-all-done.1.right, bf16[8,40,640]{2,1,0:T(8,128)(2,1)S(1)} %all_to_all.15.joined, ...), custom_call_target="tpu_custom_call" | custom-call | tf_op jit(solution)/shard_map/pallas_call | solution.py:524
  (1 shorter events, 0.0 us)
Async XLA Ops:
  0.0 10.5 %copy-start.4 = (bf16[360,40]{1,0:T(8,128)(2,1)S(1)}, bf16[360,40]{1,0:T(8,128)(2,1)}, u32[]{:S(2)}) copy-start(bf16[360,40]{1,0:T(8,128)(2,1)} %constant.18.clone.shift) | copy-start | bytes 86404
  0.0 10.5 %collective-permute-start.1 = (bf16[2880,640]{1,0:T(8,128)(2,1)}, bf16[2880,640]{1,0:T(8,128)(2,1)}, u32[]{:S(2)}, u32[]{:S(2)}) collective-permute-start(bf16[2880,640]{1,0:T(8,128)(2,1)} %bitcast.8), channel_id=1, source_target_pairs={{0,8},{8,0},{16,24},{24,16},{1,9},{9,1},{17,25},{25,17},{2,10},{10... | collective-permute-start | bytes 11059208 | tf_op jit(solution)/shard_map/ppermute | solution.py:464
  1.3 2.0 %copy-start = (bf16[1,2880,640]{2,1,0:T(8,128)(2,1)S(1)}, bf16[1,2880,640]{2,1,0:T(8,128)(2,1)}, u32[]{:S(2)}) copy-start(bf16[1,2880,640]{2,1,0:T(8,128)(2,1)} %param.10) | copy-start | bytes 11059204
  3.4 1.1 copy-start.6
  8.9 1.6 %collective-permute-start = (bf16[4,40,640]{2,1,0:T(8,128)(2,1)S(1)}, bf16[4,40,640]{2,1,0:T(8,128)(2,1)S(1)}, u32[]{:S(2)}, u32[]{:S(2)}) collective-permute-start(bf16[4,40,640]{2,1,0:T(8,128)(2,1)S(1)} %get-tuple-element.18.own), channel_id=1, source_target_pairs={{0,8},{8,0},{16,24},{24,16},{1,9},{9,1},{17,25},{25,17},{2,10},{10... | collective-permute-start | bytes 614408 | tf_op jit(solution)/shard_map/ppermute | solution.py:464
  10.5 2.0 %copy-start.1 = (bf16[1,2880,640]{2,1,0:T(8,128)(2,1)S(1)}, bf16[1,2880,640]{2,1,0:T(8,128)(2,1)}, u32[]{:S(2)}) copy-start(bf16[1,2880,640]{2,1,0:T(8,128)(2,1)} %param.10) | copy-start | bytes 11059204
  12.5 7.2 %copy-start.10 = (bf16[2,1,12,3840]{3,0,2,1:T(2,128)(2,1)S(1)}, bf16[2,1,12,3840]{3,0,2,1:T(2,128)(2,1)}, u32[]{:S(2)}) copy-start(bf16[2,1,12,3840]{3,0,2,1:T(2,128)(2,1)} %param.9) | copy-start | bytes 552964
  12.5 9.5 %copy-start.7 = (bf16[360,40]{1,0:T(8,128)(2,1)S(1)}, bf16[360,40]{1,0:T(8,128)(2,1)}, u32[]{:S(2)}) copy-start(bf16[360,40]{1,0:T(8,128)(2,1)} %constant.19.clone.back) | copy-start | bytes 86404
  12.5 9.5 %copy-start.8 = (bf16[360,160]{1,0:T(8,128)(2,1)S(1)}, bf16[360,160]{1,0:T(8,128)(2,1)}, u32[]{:S(2)}) copy-start(bf16[360,160]{1,0:T(8,128)(2,1)} %constant.22.clone.gather) | copy-start | bytes 345604
  12.5 9.5 %copy-start.9 = (bf16[160,144]{1,0:T(8,128)(2,1)S(1)}, bf16[160,144]{1,0:T(8,128)(2,1)}, u32[]{:S(2)}) copy-start(bf16[160,144]{1,0:T(8,128)(2,1)} %constant.21.clone.parity) | copy-start | bytes 138244
  17.1 4.9 %collective-permute-start.2 = (bf16[2,40,640]{2,1,0:T(8,128)(2,1)S(1)}, bf16[2,40,640]{2,1,0:T(8,128)(2,1)S(1)}, u32[]{:S(2)}, u32[]{:S(2)}) collective-permute-start(bf16[2,40,640]{2,1,0:T(8,128)(2,1)S(1)} %get-tuple-element.19), channel_id=1, source_target_pairs={{0,16},{8,24},{16,0},{24,8},{1,17},{9,25},{17,1},{25,9},{2,18},{10... | collective-permute-start | bytes 307208 | tf_op jit(solution)/shard_map/ppermute | solution.py:464
  22.1 2.0 %copy-start.2 = (bf16[1,2880,640]{2,1,0:T(8,128)(2,1)S(1)}, bf16[1,2880,640]{2,1,0:T(8,128)(2,1)}, u32[]{:S(2)}) copy-start(bf16[1,2880,640]{2,1,0:T(8,128)(2,1)} %param.10) | copy-start | bytes 11059204
  35.4 1.9 %collective-permute-start.3 = (bf16[9,40,640]{2,1,0:T(8,128)(2,1)S(1)}, bf16[9,40,640]{2,1,0:T(8,128)(2,1)S(1)}, u32[]{:S(2)}, u32[]{:S(2)}) collective-permute-start(bf16[9,40,640]{2,1,0:T(8,128)(2,1)S(1)} %get-tuple-element.21), channel_id=1, source_target_pairs={{0,8},{8,0},{16,24},{24,16},{1,9},{9,1},{17,25},{25,17},{2,10},{10... | collective-permute-start | bytes 1382408 | tf_op jit(solution)/shard_map/ppermute | solution.py:464
  37.9 17.4 %copy-start.5 = (bf16[8,80,640]{2,1,0:T(8,128)(2,1)}, bf16[8,80,640]{2,1,0:T(8,128)(2,1)S(1)}, u32[]{:S(2)}) copy-start(bf16[8,80,640]{2,1,0:T(8,128)(2,1)S(1)} %get-tuple-element.22) | copy-start | bytes 2457604
  55.3 23.7 %all-to-all-start = ((bf16[8,80,640]{2,1,0:T(8,128)(2,1)}), bf16[8,80,640]{2,1,0:T(8,128)(2,1)S(1)}, u32[]{:S(2)}, u32[]{:S(2)}) async-start(bf16[8,80,640]{2,1,0:T(8,128)(2,1)} %copy-done.5), calls=%async_computation | async-start | bytes 1638400 | tf_op jit(solution)/shard_map/all_to_all | solution.py:467
  59.3 3.5 %collective-permute-start.4 = (bf16[2,40,640]{2,1,0:T(8,128)(2,1)S(1)}, bf16[2,40,640]{2,1,0:T(8,128)(2,1)S(1)}, u32[]{:S(2)}, u32[]{:S(2)}) collective-permute-start(bf16[2,40,640]{2,1,0:T(8,128)(2,1)S(1)} %get-tuple-element.23), channel_id=1, source_target_pairs={{0,16},{8,24},{16,0},{24,8},{1,17},{9,25},{17,1},{25,9},{2,18},{10... | collective-permute-start | bytes 307208 | tf_op jit(solution)/shard_map/ppermute | solution.py:464
  62.8 2.0 %copy-start.3 = (bf16[1,2880,640]{2,1,0:T(8,128)(2,1)S(1)}, bf16[1,2880,640]{2,1,0:T(8,128)(2,1)}, u32[]{:S(2)}) copy-start(bf16[1,2880,640]{2,1,0:T(8,128)(2,1)} %param.10) | copy-start | bytes 11059204
  69.5 2.4 %collective-permute-start.5 = (bf16[40,640]{1,0:T(8,128)(2,1)S(1)}, bf16[40,640]{1,0:T(8,128)(2,1)S(1)}, u32[]{:S(2)}, u32[]{:S(2)}) collective-permute-start(bf16[40,640]{1,0:T(8,128)(2,1)S(1)} %get-tuple-element.27), channel_id=1, source_target_pairs={{0,8},{8,0},{16,24},{24,16},{1,9},{9,1},{17,25},{25,17},{2,10},{10... | collective-permute-start | bytes 153608 | tf_op jit(solution)/shard_map/ppermute | solution.py:464
  79.0 25.0 %all-to-all-start.1 = ((bf16[8,80,640]{2,1,0:T(8,128)(2,1)}), bf16[8,80,640]{2,1,0:T(8,128)(2,1)S(1)}, u32[]{:S(2)}, u32[]{:S(2)}) async-start(bf16[8,80,640]{2,1,0:T(8,128)(2,1)} %shard_map.87), calls=%async_computation.1 | async-start | bytes 1638400 | tf_op jit(solution)/shard_map/all_to_all | solution.py:467
  83.9 2.3 %collective-permute-start.6 = (bf16[8,40,640]{2,1,0:T(8,128)(2,1)S(1)}, bf16[8,40,640]{2,1,0:T(8,128)(2,1)S(1)}, u32[]{:S(2)}, u32[]{:S(2)}) collective-permute-start(bf16[8,40,640]{2,1,0:T(8,128)(2,1)S(1)} %all_to_all.15.joined), channel_id=1, source_target_pairs={{0,8},{8,0},{16,24},{24,16},{1,9},{9,1},{17,25},{25,17},{2,10},{10... | collective-permute-start | bytes 1228808 | tf_op jit(solution)/shard_map/ppermute | solution.py:464

commit v2 on v1

--- a/solution.py
+++ b/solution.py
@@ -7,6 +7,7 @@
 from jax.experimental import pallas as pl
 from jax.experimental.pallas import tpu as pltpu
 from jax.sharding import PartitionSpec as P
+
 
 BF = jnp.bfloat16
 F32 = jnp.float32
@@ -53,6 +54,7 @@
         self.cells = self.half * self.half
         self.rows = -(-self.cells // 8) * 8
         self.both = self.micro * self.rows
+        self.packed = -(-self.micro * self.cells // 8) * 8
         self.group = self.width // 2
         self.low = -(-self.group // 128) * 128
         self.high = self.group // 128 * 128
@@ -85,7 +87,12 @@
             for p, (pr, ps) in enumerate(PARITIES):
                 parity[p, r, (2 * i + pr) * z.full + 2 * j + ps] = 1
     back = shift.transpose(0, 2, 1)
+    many = np.zeros((9, z.packed, z.packed), np.float32)
+    for m in range(z.micro):
+        at = slice(m * z.cells, (m + 1) * z.cells)
+        many[:, at, at] = shift[:, : z.cells, : z.cells]
     return dict(
+        many=many.reshape(9 * z.packed, z.packed),
         shift=shift.reshape(9 * rows, rows),
         back=back.reshape(9 * rows, rows),
         enc=enc.reshape(9 * z.both, z.micro * z.fine),
@@ -195,9 +202,12 @@
     return rows_times_kernel(z, first, second, weights, scratch)
 
 
-def encoder_kernel(z, kernel, images, enc, out, patches_out, buffer, sems):
+def encoder_kernel(z, kernel, enc, images, out, patches_out, buffer, moves, sems, move_sem):
+    fetch = pltpu.make_async_copy(enc, moves, move_sem)
+    fetch.start()
     weights = Weights(z, None, kernel, None, buffer, sems)
-    columns = dot(enc[...], images[...]).astype(BF)
+    fetch.wait()
+    columns = dot(moves[...], images[...]).astype(BF)
     total = None
     for t in range(9):
         part = columns[t * z.both : (t + 1) * z.both]
@@ -223,8 +233,8 @@
 
 
 def middle_kernel(
-    z, scale, where, kernel, other, inbound, targets, shift, back, parity, gather,
-    grads, own_out, send, scratch, delta_p, delta_q, sums_p, sums_q, buffer2, buffer3, sems2, sems3,
+    z, where, kernel, other, inbound, targets, shift, back, parity, gather,
+    grads, own_out, send, scratch, delta_p, delta_q, sums_p, sums_q, buffer2, buffer3, sems2, sems3, *, scale,
 ):
     odd = lax.rem(where[0], 2) == 1
     centre = Weights(z, jnp.logical_not(odd), kernel, other, buffer2, sems2)
@@ -281,21 +291,14 @@
         part_q = sums_q[tap_rows(z, t)].astype(F32)
         return join_columns(z, part_p, part_q).astype(BF)
 
-    @pl.when(odd)
-    def _():
-        for t in range(9):
-            own_out[t] = sums(t)
-        own_out[9] = joined
-        send[0] = delta
-        send[1] = hidden
-
-    @pl.when(jnp.logical_not(odd))
-    def _():
-        for t in range(9):
-            send[t] = sums(t)
-        own_out[0] = delta
-        own_out[1] = hidden
-        own_out[9] = joined
+    for t in range(9):
+        here = sums(t)
+        own_out[t] = here
+        send[t] = here
+    own_out[9] = joined
+    send[9] = joined
+    own_out[10] = delta
+    send[10] = delta
 
 
 def centre_back_kernel(
@@ -318,104 +321,128 @@
     return dest * z.share // z.chan
 
 
-def prepare_first_kernel(z, where, patches, own, received, middle_own, middle_received, out, joined):
+def pack(z, scratch, top, bottom):
+    scratch[: z.rows] = top.astype(F32)
+    scratch[z.cells : z.cells + z.rows] = bottom.astype(F32)
+    return scratch[: z.packed].astype(BF)
+
+
+def prepare_zero_kernel(z, where, patches, inbound, out):
     section = where[0]
     n, rows = z.dp, z.rows
-
-    @pl.when(section == 0)
+    mine = pl.ds(pl.multiple_of(lax.rem(section, 2) * rows, 8), rows)
+
+    @pl.when(section < 2)
     def _():
         for k in range(n):
             tap = first_tap(z, k)
-            near = patches[tap].astype(F32)
-            far = patches[min(tap + 1, 8)].astype(F32)
+            near = patches[tap, mine].astype(F32)
+            far = patches[min(tap + 1, 8), mine].astype(F32)
             both = jnp.where(lanes(near.shape) < z.chan, near, pltpu.roll(far, z.chan, 1))
             out[k] = both.astype(BF)
 
-    @pl.when(section == 1)
-    def _():
-        for k in range(n):
-            out[k, :rows] = received[0]
-            out[k, rows:] = received[1]
+    @pl.when(section >= 2)
+    def _():
+        for k in range(n):
+            out[k] = inbound[1]
+
+
+def prepare_first_kernel(z, where, encoded, own, received, out, scratch):
+    section = where[0]
+    n = z.dp
+
+    def fill(top, bottom):
+        both = pack(z, scratch, top, bottom)
+        for k in range(n):
+            out[k] = both
+
+    pl.when(section < 2)(lambda: fill(encoded[0], encoded[1]))
+    pl.when(section == 3)(lambda: fill(received[9], own[9]))
 
     @pl.when(section == 2)
     def _():
         for k in range(n):
-            out[k, :rows] = middle_own[1]
-            out[k, rows:] = middle_received[1]
-
-    @pl.when(section == 3)
-    def _():
-        for k in range(n):
             tap = first_tap(z, k)
-            out[k, :rows] = middle_received[tap]
-            out[k, rows:] = middle_own[tap]
-
-    for k in range(n):
-        joined[k] = middle_own[9]
-
-
-def prepare_second_kernel(z, where, back_own, back_received, middle_own, middle_received, out):
+            out[k] = pack(z, scratch, own[tap], received[tap])
+
+
+def prepare_second_kernel(z, where, back_own, back_received, middle_own, middle_received, out, scratch):
     section = where[0]
-    n, rows = z.dp, z.rows
+    n = z.dp
 
     def fill(top, bottom):
-        for k in range(n):
-            out[k, :rows] = top[...]
-            out[k, rows:] = bottom[...]
+        both = pack(z, scratch, top[...], bottom[...])
+        for k in range(n):
+            out[k] = both
 
     pl.when(section == 0)(lambda: fill(back_own, back_received))
     pl.when(section == 1)(lambda: fill(back_received, back_own))
-    pl.when(section == 2)(lambda: fill(middle_own.at[0], middle_received.at[0]))
+    pl.when(section == 2)(lambda: fill(middle_own.at[10], middle_received.at[10]))
 
     @pl.when(section == 3)
     def _():
         for k in range(n):
             tap = min(first_tap(z, k) + 1, 8)
-            out[k, :rows] = middle_received[tap]
-            out[k, rows:] = middle_own[tap]
-
-
-def weight_kernel(z, where, shift, left, right, joined, joined_received, out, lefts, rows_out):
+            out[k] = pack(z, scratch, middle_received[tap], middle_own[tap])
+
+
+def grouped(z, a, b):
+    first = dot_tn(a[:, : z.low], b[:, : z.low])
+    second = dot_tn(a[:, z.high :], b[:, z.high :])
+    move = z.group - z.high
+    return join_columns(z, first[: z.chan], second[move : move + z.chan])
+
+
+def left_kernel(z, where, many, zero, zero_other, one, one_other, lefts, early, scratch):
     n = z.dp
     section, place = where[0], where[1]
     tap = first_tap(z, place)
-    total = n * z.both
-
-    def grouped(at, pairs):
-        first = second = None
-        for a, b in pairs:
-            one = dot_tn(a[:, : z.low], b[:, : z.low])
-            two = dot_tn(a[:, z.high :], b[:, z.high :])
-            first = one if first is None else first + one
-            second = two if second is None else second + two
-        move = z.group - z.high
-        both = join_columns(z, first[: z.chan], second[move : move + z.chan])
-        rows_out[pl.ds(at * z.chan, z.chan), :] = both
+
+    def rows_of(k):
+        return pl.ds(k * z.packed, z.packed)
+
+    def moved(value_of):
+        for k in range(n):
+            value = value_of(k)
+            for at in range(2):
+                here = jnp.minimum(tap + at, 8)
+                move = many[pl.ds(pl.multiple_of(here * z.packed, 8), z.packed), :]
+                lefts[at, rows_of(k), :] = dot(move, value).astype(BF)
 
     @pl.when(section == 0)
     def _():
-        a = left[...].reshape(total, z.width)
-        b = right[...].reshape(total, z.width)
-        rows_out[...] = dot_tn(a, b)
+        for k in range(n):
+            lefts[0, rows_of(k), :] = pack(z, scratch, zero[k], zero_other[k])
+
+    pl.when(section == 1)(lambda: moved(lambda k: one[k]))
+    pl.when(section == 2)(lambda: moved(lambda k: pack(z, scratch, zero[k], zero_other[k])))
+
+    @pl.when(section == 3)
+    def _():
+        for k in range(n):
+            lefts[0, rows_of(k), :] = one[k]
+        early[...] = grouped(z, lefts[0], one_other[...].reshape(n * z.packed, z.width))
+
+
+def weight_kernel(z, where, right, lefts, early, out, rows_out):
+    n = z.dp
+    section, place = where[0], where[1]
+    tap = first_tap(z, place)
+    b = right[...].reshape(n * z.packed, z.width)
+
+    @pl.when(section == 0)
+    def _():
+        rows_out[...] = dot_tn(lefts[0], b)
 
     @pl.when(jnp.logical_or(section == 1, section == 2))
     def _():
         for at in range(2):
-            here = jnp.minimum(tap + at, 8)
-            move = shift[pl.ds(pl.multiple_of(here * z.rows, 8), z.rows), :]
-            for k in range(n):
-                for m in range(z.micro):
-                    part = left[k, pl.ds(m * z.rows, z.rows)]
-                    lefts[pl.ds((k * z.micro + m) * z.rows, z.rows), :] = dot(move, part).astype(BF)
-            grouped(at, [(lefts[...], right[...].reshape(total, z.width))])
+            rows_out[pl.ds(at * z.chan, z.chan), :] = grouped(z, lefts[at], b)
 
     @pl.when(section == 3)
     def _():
-        for k in range(n):
-            lefts[pl.ds(k * z.both, z.rows), :] = joined_received[k]
-            lefts[pl.ds(k * z.both + z.rows, z.rows), :] = joined[k]
-        grouped(0, [(lefts[...], left[...].reshape(total, z.width))])
-        grouped(1, [(lefts[...], right[...].reshape(total, z.width))])
+        rows_out[: z.chan] = early[...]
+        rows_out[z.chan :] = grouped(z, lefts[0], b)
 
     begin = place * z.share - tap * z.chan
     if z.share % 8 == 0 and z.chan % 8 == 0:
@@ -427,7 +454,7 @@
         out[...] = pltpu.roll(block, lax.rem(size - rest, size), 0)[: z.share]
 
 
-def call(body, outs, spaces, scratch=()):
+def call(body, outs, spaces, scratch=(), flops=10**8, limit=None):
     kinds = dict(s=pltpu.SMEM, h=pltpu.HBM, v=pltpu.VMEM)
     single = not isinstance(outs, (list, tuple))
     vmem = pl.BlockSpec(memory_space=pltpu.VMEM)
@@ -437,7 +464,8 @@
         in_specs=[pl.BlockSpec(memory_space=kinds[k]) for k in spaces],
         out_specs=vmem if single else [vmem] * len(outs),
         scratch_shapes=list(scratch),
-        compiler_params=pltpu.CompilerParams(vmem_limit_bytes=40 * 2**20),
+        cost_estimate=pl.CostEstimate(flops=flops, bytes_accessed=4 * 2**20, transcendentals=0),
+        compiler_params=pltpu.CompilerParams(vmem_limit_bytes=limit),
     )
 
 
@@ -457,8 +485,11 @@
         return jax.ShapeDtypeStruct(dims, dtype)
 
     join = pltpu.VMEM((2, rows, width), F32)
+    packing = pltpu.VMEM((both, width), F32)
     buffer = pltpu.VMEM((z.taps_rows, width), BF)
     sems = pltpu.SemaphoreType.DMA((9,))
+    message = shape(dp, z.packed, width)
+    small = 16 * 2**20
 
     def across(x, bit):
         return lax.ppermute(x, "section", [(s, s ^ bit) for s in range(n_section)])
@@ -466,24 +497,34 @@
     def spread(x):
         return lax.all_to_all(x, "dp", 0, 0, tiled=True)
 
+    def run(body, outs, spaces, scratch, *operands, **options):
+        return call(functools.partial(body, z), outs, spaces, scratch, **options)(*operands)
+
     other = across(kernel, 1)
-    encoded, patches = call(
-        functools.partial(encoder_kernel, z),
+    encoded, patches = run(
+        encoder_kernel,
         [shape(2 * z.micro, rows, width), shape(9, both, width)],
-        "hvv",
-        [buffer, sems],
-    )(kernel, image_rows, sel["enc"])
+        "hhv",
+        [buffer, pltpu.VMEM((9 * both, z.micro * z.fine), BF), sems, pltpu.SemaphoreType.DMA],
+        kernel, sel["enc"], image_rows,
+    )
     encoded_in = across(encoded, 1)
-    forward, centre_slope, enc_slope = call(
-        functools.partial(centre_kernel, z),
+    forward, centre_slope, enc_slope = run(
+        centre_kernel,
         [shape(2, rows, width), shape(rows, width, dtype=F32), shape(rows, width, dtype=F32)],
         "shhvvv",
         [buffer, sems],
-    )(where, kernel, other, encoded, encoded_in, sel["shift"])
+        where, kernel, other, encoded, encoded_in, sel["shift"],
+    )
     forward_in = across(forward, 2)
-    grads, middle_own, middle_send = call(
-        functools.partial(middle_kernel, z, scale),
-        [shape(2, rows, width), shape(10, rows, width), shape(9, rows, width)],
+    zero = run(
+        prepare_zero_kernel, shape(dp, rows, width), "svv", [],
+        where, patches, forward_in, limit=small,
+    )
+    zero = spread(zero)
+    grads, middle_own, middle_send = run(
+        functools.partial(middle_kernel, scale=scale),
+        [shape(2, rows, width), shape(11, rows, width), shape(11, rows, width)],
         "shhvvvvvv",
         [
             join,
@@ -496,37 +537,48 @@
             sems,
             sems,
         ],
-    )(
         where, kernel, other, forward_in, target_rows,
         sel["shift"], sel["back"], sel["parity"], sel["gather"],
+        flops=10**10,
     )
     grads_in = across(grads, 2)
     middle_in = across(middle_send, 1)
-    first, joined = call(
-        functools.partial(prepare_first_kernel, z),
-        [shape(dp, both, width), shape(dp, rows, width)],
-        "svvvvv",
-    )(where, patches, encoded, encoded_in, middle_own, middle_in)
-    left = spread(first)
-    back_own, back_send = call(
-        functools.partial(centre_back_kernel, z),
+    one = run(
+        prepare_first_kernel, message, "svvv", [packing],
+        where, encoded_in, middle_own, middle_in, limit=small,
+    )
+    one = spread(one)
+    back_own, back_send = run(
+        centre_back_kernel,
         [shape(rows, width), shape(rows, width)],
         "shhvvvv",
         [join, buffer, sems],
-    )(where, kernel, other, grads_in, enc_slope, centre_slope, sel["back"])
+        where, kernel, other, grads_in, enc_slope, centre_slope, sel["back"],
+        flops=10**10,
+    )
     back_in = across(back_send, 1)
-    second = call(functools.partial(prepare_second_kernel, z), shape(dp, both, width), "svvvv")(
-        where, back_own, back_in, middle_own, middle_in
-    )
-    right = spread(second)
-    joined = spread(joined)
-    joined_in = across(joined, 1)
-    out = call(
-        functools.partial(weight_kernel, z),
+    right = run(
+        prepare_second_kernel, message, "svvvv", [packing],
+        where, back_own, back_in, middle_own, middle_in, limit=small,
+    )
+    right = spread(right)
+    zero_other = across(zero, 1)
+    one_other = across(one, 1)
+    lefts, early = run(
+        left_kernel,
+        [shape(2, dp * z.packed, width), shape(z.chan, width, dtype=F32)],
+        "svvvvv",
+        [packing],
+        where, sel["many"], zero, zero_other, one, one_other,
+        flops=10**10, limit=2 * small,
+    )
+    out = run(
+        weight_kernel,
         shape(z.share, width, dtype=F32),
-        "svvvvv",
-        [pltpu.VMEM((dp * both, width), BF), pltpu.VMEM((2 * z.chan, width), F32)],
-    )(where, sel["shift"], left, right, joined, joined_in)
+        "svvv",
+        [pltpu.VMEM((2 * z.chan, width), F32)],
+        where, right, lefts, early, limit=2 * small,
+    )
     return out[None]
 
 

time: 109 us -> 110 us (level)
  blocking collectives: 17.4 us -> 0 us
  Pallas kernels: 30.7 us -> 37.5 us
  waiting for transfers between devices: 32.3 us -> 38.8 us
  starting transfers between devices: 16.1 us -> 20.2 us
    all_to_all x1 -> x0, blocking collectives: 17.4 us -> none  [spread(): return lax.all_to_all(x, 'dp', 0, 0, tiled=True)]
    all_to_all x2 -> x3, waiting for transfers between devices: 23.2 us -> 33.7 us  [spread(): return lax.all_to_all(x, 'dp', 0, 0, tiled=True)]
    pallas_call x7 -> x9, Pallas kernels: 30.7 us -> 37.5 us  [run(): call(functools.partial(body, z), outs, spaces, scratch, **options)]
    all_to_all x2 -> x3, starting transfers between devices: 8.92 us -> 13.2 us  [spread(): return lax.all_to_all(x, 'dp', 0, 0, tiled=True)]
    ppermute x7 -> x8, waiting for transfers between devices: 9.09 us -> 5.11 us  [across(): return lax.ppermute(x, 'section', [(s, s ^ bit) for s in range(n_section)])]
    unnamed x24 -> x36, local copies, waits for them, and re-layouts: 10.2 us -> 9.75 us
    ppermute x7 -> x8, starting transfers between devices: 7.17 us -> 6.93 us  [across(): return lax.ppermute(x, 'section', [(s, s ^ bit) for s in range(n_section)])]
  transfers between devices with their start and end apart: 9 -> 11, of which waited for: 8 -> 6; matrix products, arithmetic and copies ran while one was open for 2% -> 3% of each run, Pallas kernels for 10% -> 14%
where the time goes in v2:
time: 110 us; the launch traced here: 109 us
  waiting for transfers between devices  38.8 us (35%)
  Pallas kernels  37.5 us (34%)
  starting transfers between devices  20.2 us (18%)
  local copies, waits for them, and re-layouts  11.7 us (11%)
    pallas_call x9, Pallas kernels, run(): call(functools.partial(body, z), outs, spaces, scratch, **options)  37.5 us
    all_to_all x3, waiting for transfers between devices, spread(): return lax.all_to_all(x, 'dp', 0, 0, tiled=True)  33.7 us
    all_to_all x3, starting transfers between devices, spread(): return lax.all_to_all(x, 'dp', 0, 0, tiled=True)  13.2 us
    unnamed x36, local copies, waits for them, and re-layouts  9.75 us
    ppermute x8, starting transfers between devices, across(): return lax.ppermute(x, 'section', [(s, s ^ bit) for s in range(n_section)])  6.93 us
    ppermute x8, waiting for transfers between devices, across(): return lax.ppermute(x, 'section', [(s, s ^ bit) for s in range(n_section)])  5.11 us
  transfers between devices with their start and end apart: 11, of which 6 were waited for; matrix products, arithmetic and copies ran while one was open for 3% of the time, Pallas kernels for 14%

profile of v2, /device:TPU:1, one launch (start us, length us, event | category | flops | bytes accessed | tf_op | source)
XLA Modules:
  0.0 109.1 jit_solution(17735078871525321329)
XLA Ops:
  0.0 0.0 collective-permute-start
  0.0 0.9 copy.12
  1.0 1.0 reshape.6.images
  2.0 6.3 %shard_map.91 = (bf16[4,40,640]{2,1,0:T(8,128)(2,1)}, bf16[9,80,640]{2,1,0:T(8,128)(2,1)}) custom-call(bf16[2880,640]{1,0:T(8,128)(2,1)} %bitcast.9, bf16[720,288]{1,0:T(8,128)(2,1)} %constant.23.clone.enc, bf16[288,320]{1,0:T(8,128)(2,1)} %reshape.6.images), custom_call_target="tpu_custom_call" | custom-call | flops 100000000 | bytes 4194304 | tf_op jit(solution)/shard_map/pallas_call | solution.py:501
  8.3 0.5 collective-permute-start.1
  8.8 0.7 pad_add_fusion.where
  9.5 0.0 copy-start.15
  9.5 0.6 collective-permute-done.1.received.encoded
  10.1 0.0 collective-permute-done.other
  10.1 0.7 copy-done.3
  10.8 4.6 %shard_map.92 = (bf16[2,40,640]{2,1,0:T(8,128)(2,1)}, f32[40,640]{1,0:T(8,128)}, f32[40,640]{1,0:T(8,128)}) custom-call(s32[2]{0:T(128)} %pad_add_fusion.where, bf16[2880,640]{1,0:T(8,128)(2,1)} %bitcast.10, bf16[2880,640]{1,0:T(8,128)(2,1)} %collective-permute-done.other, bf16[4,40,640]{2,1,0:T(8,128)(2,1)} %get-tuple-element.17.own, ...), custom_call_target="tpu_custom_call" | custom-call | flops 100000000 | bytes 4194304 | tf_op jit(solution)/shard_map/pallas_call | solution.py:501
  15.4 2.6 %collective-permute-start.2 = (bf16[2,40,640]{2,1,0:T(8,128)(2,1)}, bf16[2,40,640]{2,1,0:T(8,128)(2,1)S(1)}, u32[]{:S(2)}, u32[]{:S(2)}) collective-permute-start(bf16[2,40,640]{2,1,0:T(8,128)(2,1)} %get-tuple-element.18), channel_id=1, source_target_pairs={{0,16},{8,24},{16,0},{24,8},{1,17},{9,25},{17,1},{25,9},{2,18},{10... | collective-permute-start | bytes 307208 | tf_op jit(solution)/shard_map/ppermute | solution.py:495
  18.0 0.0 copy-done.15
  18.1 1.0 reshape.7.targets
  19.1 0.0 copy-start.4
  19.1 0.0 copy-start.10
  19.1 2.3 %collective-permute-done.2.inbound = bf16[2,40,640]{2,1,0:T(8,128)(2,1)S(1)} collective-permute-done((bf16[2,40,640]{2,1,0:T(8,128)(2,1)}, bf16[2,40,640]{2,1,0:T(8,128)(2,1)S(1)}, u32[]{:S(2)}, u32[]{:S(2)}) %collective-permute-start.2) | collective-permute-done | bytes 102432 | tf_op jit(solution)/shard_map/ppermute | solution.py:495
  21.4 0.0 copy-start.7
  21.4 0.6 copy-done.7
  22.0 0.0 copy-start.2
  22.0 12.9 %shard_map.93 = (bf16[2,40,640]{2,1,0:T(8,128)(2,1)}, bf16[11,40,640]{2,1,0:T(8,128)(2,1)}, bf16[11,40,640]{2,1,0:T(8,128)(2,1)}) custom-call(s32[2]{0:T(128)} %pad_add_fusion.where, bf16[2880,640]{1,0:T(8,128)(2,1)} %bitcast.11, bf16[2880,640]{1,0:T(8,128)(2,1)} %collective-permute-done.other, bf16[2,40,640]{2,1,0:T(8,128)(2,1)} %copy-done.7, ...), custom_call_target="tpu_custom_call" | custom-call | flops 10000000000 | bytes 4194304 | tf_op jit(solution)/shard_map/pallas_call | solution.py:501
  34.9 0.1 collective-permute-start.5
  35.0 2.2 %collective-permute-done.5.middle_received.received = bf16[11,40,640]{2,1,0:T(8,128)(2,1)S(1)} collective-permute-done((bf16[11,40,640]{2,1,0:T(8,128)(2,1)}, bf16[11,40,640]{2,1,0:T(8,128)(2,1)S(1)}, u32[]{:S(2)}, u32[]{:S(2)}) %collective-permute-start.5) | collective-permute-done | bytes 563232 | tf_op jit(solution)/shard_map/ppermute | solution.py:495
  37.2 0.0 copy-done.4
  37.2 0.0 copy-done.10
  37.2 0.0 copy-start
  37.2 1.1 copy-done
  38.2 1.5 %shard_map.97 = bf16[8,72,640]{2,1,0:T(8,128)(2,1)} custom-call(s32[2]{0:T(128)S(1)} %copy-done.10, bf16[4,40,640]{2,1,0:T(8,128)(2,1)S(1)} %copy-done.4, bf16[11,40,640]{2,1,0:T(8,128)(2,1)S(1)} %copy-done, bf16[11,40,640]{2,1,0:T(8,128)(2,1)S(1)} %collective-permute-done.5.middle_received.received), custom_call_target="tpu_custom_call" | custom-call | flops 100000000 | bytes 4194304 | tf_op jit(solution)/shard_map/pallas_call | solution.py:501
  39.7 5.5 %all-to-all-start.2 = ((bf16[8,72,640]{2,1,0:T(8,128)(2,1)}), bf16[8,72,640]{2,1,0:T(8,128)(2,1)S(1)}, u32[]{:S(2)}, u32[]{:S(2)}) async-start(bf16[8,72,640]{2,1,0:T(8,128)(2,1)} %shard_map.97), calls=%async_computation.2 | async-start | bytes 1474560 | tf_op jit(solution)/shard_map/all_to_all | solution.py:498
  45.2 1.2 %collective-permute-start.3 = (bf16[2,40,640]{2,1,0:T(8,128)(2,1)}, bf16[2,40,640]{2,1,0:T(8,128)(2,1)S(1)}, u32[]{:S(2)}, u32[]{:S(2)}) collective-permute-start(bf16[2,40,640]{2,1,0:T(8,128)(2,1)} %get-tuple-element.19), channel_id=1, source_target_pairs={{0,16},{8,24},{16,0},{24,8},{1,17},{9,25},{17,1},{25,9},{2,18},{10... | collective-permute-start | bytes 307208 | tf_op jit(solution)/shard_map/ppermute | solution.py:495
  46.5 0.0 copy-done.2
  46.5 0.0 copy-start.8
  46.5 0.9 copy-done.8
  47.3 1.5 %shard_map.96 = bf16[8,40,640]{2,1,0:T(8,128)(2,1)} custom-call(s32[2]{0:T(128)S(1)} %copy-done.10, bf16[9,80,640]{2,1,0:T(8,128)(2,1)S(1)} %copy-done.2, bf16[2,40,640]{2,1,0:T(8,128)(2,1)S(1)} %copy-done.8), custom_call_target="tpu_custom_call" | custom-call | flops 100000000 | bytes 4194304 | tf_op jit(solution)/shard_map/pallas_call | solution.py:501
  48.8 15.2 %all-to-all-done.2.one = bf16[8,72,640]{2,1,0:T(8,128)(2,1)S(1)} async-done(((bf16[8,72,640]{2,1,0:T(8,128)(2,1)}), bf16[8,72,640]{2,1,0:T(8,128)(2,1)S(1)}, u32[]{:S(2)}, u32[]{:S(2)}) %all-to-all-start.2) | async-done | bytes 737312 | tf_op jit(solution)/shard_map/all_to_all | solution.py:498
  64.0 0.0 copy-start.5
  64.0 4.2 %all-to-all-start.1 = ((bf16[8,40,640]{2,1,0:T(8,128)(2,1)}), bf16[8,40,640]{2,1,0:T(8,128)(2,1)S(1)}, u32[]{:S(2)}, u32[]{:S(2)}) async-start(bf16[8,40,640]{2,1,0:T(8,128)(2,1)} %shard_map.96), calls=%async_computation.1 | async-start | bytes 819200 | tf_op jit(solution)/shard_map/all_to_all | solution.py:498
  68.2 0.8 collective-permute-start.7
  68.9 0.0 collective-permute-done.3.grads
  68.9 0.0 copy-start.16
  68.9 0.6 copy-done.16
  69.6 0.0 copy-start.1
  69.6 4.5 %shard_map.94 = (bf16[40,640]{1,0:T(8,128)(2,1)}, bf16[40,640]{1,0:T(8,128)(2,1)}) custom-call(s32[2]{0:T(128)} %pad_add_fusion.where, bf16[2880,640]{1,0:T(8,128)(2,1)} %bitcast.12, bf16[2880,640]{1,0:T(8,128)(2,1)} %collective-permute-done.other, bf16[2,40,640]{2,1,0:T(8,128)(2,1)} %copy-done.16, f32[40,640]{1,0:T(8,128)} %get-tuple-element.20.enc_slope, ...), custom_call_target="tpu_custom_call" | custom-call | flops 10000000000 | bytes 4194304 | tf_op jit(solution)/shard_map/pallas_call | solution.py:501
  74.1 0.0 copy-done.5
  74.1 0.1 collective-permute-start.4
  74.2 5.3 %all-to-all-done.1.zero = bf16[8,40,640]{2,1,0:T(8,128)(2,1)S(1)} async-done(((bf16[8,40,640]{2,1,0:T(8,128)(2,1)}), bf16[8,40,640]{2,1,0:T(8,128)(2,1)S(1)}, u32[]{:S(2)}, u32[]{:S(2)}) %all-to-all-start.1) | async-done | bytes 409632 | tf_op jit(solution)/shard_map/all_to_all | solution.py:498
  79.6 1.6 %collective-permute-start.6 = (bf16[8,40,640]{2,1,0:T(8,128)(2,1)S(1)}, bf16[8,40,640]{2,1,0:T(8,128)(2,1)}, u32[]{:S(2)}, u32[]{:S(2)}) collective-permute-start(bf16[8,40,640]{2,1,0:T(8,128)(2,1)S(1)} %all-to-all-done.1.zero), channel_id=1, source_target_pairs={{0,8},{8,0},{16,24},{24,16},{1,9},{9,1},{17,25},{25,17},{2,10},{10... | collective-permute-start | bytes 1228808 | tf_op jit(solution)/shard_map/ppermute | solution.py:495
  81.2 0.0 collective-permute-done.4.back_received
  81.2 0.0 copy-done.1
  81.2 0.0 copy-done.11
  81.2 0.0 copy-start.9
  81.2 0.8 copy-done.9
  82.0 1.7 %shard_map.95 = bf16[8,72,640]{2,1,0:T(8,128)(2,1)} custom-call(s32[2]{0:T(128)S(1)} %copy-done.11, bf16[40,640]{1,0:T(8,128)(2,1)S(1)} %copy-done.9, bf16[40,640]{1,0:T(8,128)(2,1)S(1)} %collective-permute-done.4.back_received, bf16[11,40,640]{2,1,0:T(8,128)(2,1)S(1)} %copy-done.1, bf16[11,40,640]{2,1,0:T(8,128)(2,1)S(1)} %collective-permute-done.5.middle_received.received), custom_call_target="tpu_custom_call" | custom-call | flops 100000000 | bytes 4194304 | tf_op jit(solution)/shard_map/pallas_call | solution.py:501
  83.7 3.5 %all-to-all-start = ((bf16[8,72,640]{2,1,0:T(8,128)(2,1)}), bf16[8,72,640]{2,1,0:T(8,128)(2,1)S(1)}, u32[]{:S(2)}, u32[]{:S(2)}) async-start(bf16[8,72,640]{2,1,0:T(8,128)(2,1)} %shard_map.95), calls=%async_computation | async-start | bytes 1474560 | tf_op jit(solution)/shard_map/all_to_all | solution.py:498
  87.2 0.0 collective-permute-done.6.zero_other
  87.2 0.0 collective-permute-done.7.one_other
  87.2 0.0 copy-start.12
  87.2 0.9 copy-done.12
  88.1 1.1 %copy-done.6 = bf16[8,72,640]{2,1,0:T(8,128)(2,1)S(1)} copy-done((bf16[8,72,640]{2,1,0:T(8,128)(2,1)S(1)}, bf16[8,72,640]{2,1,0:T(8,128)(2,1)}, u32[]{:S(2)}) %copy-start.6) | copy-done | bytes 737304
  89.2 1.1 %copy-done.13 = bf16[8,72,640]{2,1,0:T(8,128)(2,1)S(1)} copy-done((bf16[8,72,640]{2,1,0:T(8,128)(2,1)S(1)}, bf16[8,72,640]{2,1,0:T(8,128)(2,1)}, u32[]{:S(2)}) %copy-start.13) | copy-done | bytes 737304
  90.3 0.9 copy-done.14
  91.2 1.7 %shard_map.98 = (bf16[2,576,640]{2,1,0:T(8,128)(2,1)S(1)}, f32[320,640]{1,0:T(8,128)S(1)}) custom-call(s32[2]{0:T(128)S(1)} %copy-done.11, bf16[648,72]{1,0:T(8,128)(2,1)S(1)} %copy-done.14, bf16[8,40,640]{2,1,0:T(8,128)(2,1)S(1)} %all-to-all-done.1.zero, bf16[8,40,640]{2,1,0:T(8,128)(2,1)} %collective-permute-done.6.zero_other, ...), custom_call_target="tpu_custom_call" | custom-call | flops 10000000000 | bytes 4194304 | tf_op jit(solution)/shard_map/pallas_call | solution.py:501
  92.9 13.2 %all-to-all-done.right = bf16[8,72,640]{2,1,0:T(8,128)(2,1)S(1)} async-done(((bf16[8,72,640]{2,1,0:T(8,128)(2,1)}), bf16[8,72,640]{2,1,0:T(8,128)(2,1)S(1)}, u32[]{:S(2)}, u32[]{:S(2)}) %all-to-all-start) | async-done | bytes 737312 | tf_op jit(solution)/shard_map/all_to_all | solution.py:498
  106.1 2.9 %shard_map.99 = f32[360,640]{1,0:T(8,128)} custom-call(s32[2]{0:T(128)S(1)} %copy-done.11, bf16[8,72,640]{2,1,0:T(8,128)(2,1)S(1)} %all-to-all-done.right, bf16[2,576,640]{2,1,0:T(8,128)(2,1)S(1)} %get-tuple-element.27.lefts, f32[320,640]{1,0:T(8,128)S(1)} %get-tuple-element.28.early), custom_call_target="tpu_custom_call" | custom-call | flops 100000000 | bytes 4194304 | tf_op jit(solution)/shard_map/pallas_call | solution.py:501
  (6 shorter events, 0.0 us)
Async XLA Ops:
  0.0 10.1 %collective-permute-start = (bf16[2880,640]{1,0:T(8,128)(2,1)}, bf16[2880,640]{1,0:T(8,128)(2,1)}, u32[]{:S(2)}, u32[]{:S(2)}) collective-permute-start(bf16[2880,640]{1,0:T(8,128)(2,1)} %bitcast.8), channel_id=1, source_target_pairs={{0,8},{8,0},{16,24},{24,16},{1,9},{9,1},{17,25},{25,17},{2,10},{10... | collective-permute-start | bytes 11059208 | tf_op jit(solution)/shard_map/ppermute | solution.py:495
  8.3 1.8 %collective-permute-start.1 = (bf16[4,40,640]{2,1,0:T(8,128)(2,1)}, bf16[4,40,640]{2,1,0:T(8,128)(2,1)S(1)}, u32[]{:S(2)}, u32[]{:S(2)}) collective-permute-start(bf16[4,40,640]{2,1,0:T(8,128)(2,1)} %get-tuple-element.17.own), channel_id=1, source_target_pairs={{0,8},{8,0},{16,24},{24,16},{1,9},{9,1},{17,25},{25,17},{2,10},{10... | collective-permute-start | bytes 614408 | tf_op jit(solution)/shard_map/ppermute | solution.py:495
  9.5 8.6 %copy-start.15 = (bf16[2,1,12,3840]{3,0,2,1:T(2,128)(2,1)S(1)}, bf16[2,1,12,3840]{3,0,2,1:T(2,128)(2,1)}, u32[]{:S(2)}) copy-start(bf16[2,1,12,3840]{3,0,2,1:T(2,128)(2,1)} %param.10) | copy-start | bytes 552964
  10.1 0.7 copy-start.3
  15.4 6.0 %collective-permute-start.2 = (bf16[2,40,640]{2,1,0:T(8,128)(2,1)}, bf16[2,40,640]{2,1,0:T(8,128)(2,1)S(1)}, u32[]{:S(2)}, u32[]{:S(2)}) collective-permute-start(bf16[2,40,640]{2,1,0:T(8,128)(2,1)} %get-tuple-element.18), channel_id=1, source_target_pairs={{0,16},{8,24},{16,0},{24,8},{1,17},{9,25},{17,1},{25,9},{2,18},{10... | collective-permute-start | bytes 307208 | tf_op jit(solution)/shard_map/ppermute | solution.py:495
  19.1 18.1 %copy-start.4 = (bf16[4,40,640]{2,1,0:T(8,128)(2,1)S(1)}, bf16[4,40,640]{2,1,0:T(8,128)(2,1)}, u32[]{:S(2)}) copy-start(bf16[4,40,640]{2,1,0:T(8,128)(2,1)} %copy-done.3) | copy-start | bytes 614404
  19.1 18.1 %copy-start.10 = (s32[2]{0:T(128)S(1)}, s32[2]{0:T(128)}, u32[]{:S(2)}) copy-start(s32[2]{0:T(128)} %pad_add_fusion.where) | copy-start | bytes 28
  21.4 0.7 copy-start.7
  22.0 24.4 %copy-start.2 = (bf16[9,80,640]{2,1,0:T(8,128)(2,1)S(1)}, bf16[9,80,640]{2,1,0:T(8,128)(2,1)}, u32[]{:S(2)}) copy-start(bf16[9,80,640]{2,1,0:T(8,128)(2,1)} %get-tuple-element.26.patches) | copy-start | bytes 2764804
  34.9 2.2 %collective-permute-start.5 = (bf16[11,40,640]{2,1,0:T(8,128)(2,1)}, bf16[11,40,640]{2,1,0:T(8,128)(2,1)S(1)}, u32[]{:S(2)}, u32[]{:S(2)}) collective-permute-start(bf16[11,40,640]{2,1,0:T(8,128)(2,1)} %get-tuple-element.25), channel_id=1, source_target_pairs={{0,8},{8,0},{16,24},{24,16},{1,9},{9,1},{17,25},{25,17},{2,10},{10... | collective-permute-start | bytes 1689608 | tf_op jit(solution)/shard_map/ppermute | solution.py:495
  37.2 1.1 copy-start
  39.7 24.3 %all-to-all-start.2 = ((bf16[8,72,640]{2,1,0:T(8,128)(2,1)}), bf16[8,72,640]{2,1,0:T(8,128)(2,1)S(1)}, u32[]{:S(2)}, u32[]{:S(2)}) async-start(bf16[8,72,640]{2,1,0:T(8,128)(2,1)} %shard_map.97), calls=%async_computation.2 | async-start | bytes 1474560 | tf_op jit(solution)/shard_map/all_to_all | solution.py:498
  45.2 23.7 %collective-permute-start.3 = (bf16[2,40,640]{2,1,0:T(8,128)(2,1)}, bf16[2,40,640]{2,1,0:T(8,128)(2,1)S(1)}, u32[]{:S(2)}, u32[]{:S(2)}) collective-permute-start(bf16[2,40,640]{2,1,0:T(8,128)(2,1)} %get-tuple-element.19), channel_id=1, source_target_pairs={{0,16},{8,24},{16,0},{24,8},{1,17},{9,25},{17,1},{25,9},{2,18},{10... | collective-permute-start | bytes 307208 | tf_op jit(solution)/shard_map/ppermute | solution.py:495
  46.5 0.9 copy-start.8
  64.0 10.1 %copy-start.5 = (bf16[8,72,640]{2,1,0:T(8,128)(2,1)}, bf16[8,72,640]{2,1,0:T(8,128)(2,1)S(1)}, u32[]{:S(2)}) copy-start(bf16[8,72,640]{2,1,0:T(8,128)(2,1)S(1)} %all-to-all-done.2.one) | copy-start | bytes 2211844
  64.0 15.5 %all-to-all-start.1 = ((bf16[8,40,640]{2,1,0:T(8,128)(2,1)}), bf16[8,40,640]{2,1,0:T(8,128)(2,1)S(1)}, u32[]{:S(2)}, u32[]{:S(2)}) async-start(bf16[8,40,640]{2,1,0:T(8,128)(2,1)} %shard_map.96), calls=%async_computation.1 | async-start | bytes 819200 | tf_op jit(solution)/shard_map/all_to_all | solution.py:498
  68.2 19.0 %collective-permute-start.7 = (bf16[8,72,640]{2,1,0:T(8,128)(2,1)S(1)}, bf16[8,72,640]{2,1,0:T(8,128)(2,1)S(1)}, u32[]{:S(2)}, u32[]{:S(2)}) collective-permute-start(bf16[8,72,640]{2,1,0:T(8,128)(2,1)S(1)} %all-to-all-done.2.one), channel_id=1, source_target_pairs={{0,8},{8,0},{16,24},{24,16},{1,9},{9,1},{17,25},{25,17},{2,10},{10... | collective-permute-start | bytes 2211848 | tf_op jit(solution)/shard_map/ppermute | solution.py:495
  68.9 0.6 copy-start.16
  69.6 11.6 %copy-start.1 = (bf16[11,40,640]{2,1,0:T(8,128)(2,1)S(1)}, bf16[11,40,640]{2,1,0:T(8,128)(2,1)}, u32[]{:S(2)}) copy-start(bf16[11,40,640]{2,1,0:T(8,128)(2,1)} %get-tuple-element.24.middle_own.own) | copy-start | bytes 1689604
  69.6 11.6 %copy-start.11 = (s32[2]{0:T(128)S(1)}, s32[2]{0:T(128)}, u32[]{:S(2)}) copy-start(s32[2]{0:T(128)} %pad_add_fusion.where) | copy-start | bytes 28
  74.1 7.0 %collective-permute-start.4 = (bf16[40,640]{1,0:T(8,128)(2,1)}, bf16[40,640]{1,0:T(8,128)(2,1)S(1)}, u32[]{:S(2)}, u32[]{:S(2)}) collective-permute-start(bf16[40,640]{1,0:T(8,128)(2,1)} %get-tuple-element.23), channel_id=1, source_target_pairs={{0,8},{8,0},{16,24},{24,16},{1,9},{9,1},{17,25},{25,17},{2,10},{10... | collective-permute-start | bytes 153608 | tf_op jit(solution)/shard_map/ppermute | solution.py:495
  79.6 7.6 %collective-permute-start.6 = (bf16[8,40,640]{2,1,0:T(8,128)(2,1)S(1)}, bf16[8,40,640]{2,1,0:T(8,128)(2,1)}, u32[]{:S(2)}, u32[]{:S(2)}) collective-permute-start(bf16[8,40,640]{2,1,0:T(8,128)(2,1)S(1)} %all-to-all-done.1.zero), channel_id=1, source_target_pairs={{0,8},{8,0},{16,24},{24,16},{1,9},{9,1},{17,25},{25,17},{2,10},{10... | collective-permute-start | bytes 1228808 | tf_op jit(solution)/shard_map/ppermute | solution.py:495
  81.2 0.8 copy-start.9
  83.7 22.5 %all-to-all-start = ((bf16[8,72,640]{2,1,0:T(8,128)(2,1)}), bf16[8,72,640]{2,1,0:T(8,128)(2,1)S(1)}, u32[]{:S(2)}, u32[]{:S(2)}) async-start(bf16[8,72,640]{2,1,0:T(8,128)(2,1)} %shard_map.95), calls=%async_computation | async-start | bytes 1474560 | tf_op jit(solution)/shard_map/all_to_all | solution.py:498
  87.2 0.9 copy-start.12
  88.1 1.1 %copy-start.6 = (bf16[8,72,640]{2,1,0:T(8,128)(2,1)S(1)}, bf16[8,72,640]{2,1,0:T(8,128)(2,1)}, u32[]{:S(2)}) copy-start(bf16[8,72,640]{2,1,0:T(8,128)(2,1)} %copy-done.5) | copy-start | bytes 2211844
  89.2 1.1 %copy-start.13 = (bf16[8,72,640]{2,1,0:T(8,128)(2,1)S(1)}, bf16[8,72,640]{2,1,0:T(8,128)(2,1)}, u32[]{:S(2)}) copy-start(bf16[8,72,640]{2,1,0:T(8,128)(2,1)} %copy-done.12) | copy-start | bytes 2211844
  90.3 0.9 copy-start.14

commit v3 on v2

--- a/solution.py
+++ b/solution.py
@@ -9,6 +9,7 @@
 from jax.sharding import PartitionSpec as P
 
 
+LIMIT = None
 BF = jnp.bfloat16
 F32 = jnp.float32
 TAPS = [(a, b) for a in range(3) for b in range(3)]
@@ -66,7 +67,6 @@
 def selectors(z):
     rows, n = z.rows, z.half
     shift = np.zeros((9, rows, rows), np.float32)
-    enc = np.zeros((9, z.micro, rows, z.micro, z.fine), np.float32)
     parity = np.zeros((4, rows, z.fine), np.float32)
     gather = np.zeros((9, rows, 4, rows), np.float32)
     for i in range(n):
@@ -76,10 +76,6 @@
                 ii, jj = i + a - 1, j + b - 1
                 if 0 <= ii < n and 0 <= jj < n:
                     shift[t, r, ii * n + jj] = 1
-                ii, jj = 2 * i + a - 1, 2 * j + b - 1
-                if 0 <= ii < z.full and 0 <= jj < z.full:
-                    for m in range(z.micro):
-                        enc[t, m, r, m, ii * z.full + jj] = 1
                 for p, (pr, ps) in enumerate(PARITIES):
                     ii, jj = i + offset_of(pr, a), j + offset_of(ps, b)
                     if 0 <= ii < n and 0 <= jj < n:
@@ -95,10 +91,21 @@
         many=many.reshape(9 * z.packed, z.packed),
         shift=shift.reshape(9 * rows, rows),
         back=back.reshape(9 * rows, rows),
-        enc=enc.reshape(9 * z.both, z.micro * z.fine),
         parity=parity.reshape(4 * rows, z.fine),
         gather=gather.reshape(9 * rows, 4 * rows),
     )
+
+
+def sources_of(z):
+    table = np.full((z.both, 9), -1, np.int32)
+    for m in range(z.micro):
+        for i in range(z.half):
+            for j in range(z.half):
+                for t, (a, b) in enumerate(TAPS):
+                    ii, jj = 2 * i + a - 1, 2 * j + b - 1
+                    if ii >= 0 and jj >= 0:
+                        table[m * z.rows + i * z.half + j, t] = (m * z.full + ii) * z.full + jj
+    return table
 
 
 def lanes(shape):
@@ -124,34 +131,32 @@
 
 
 class Weights:
-    def __init__(self, z, mine, own, other, buffer, sems):
-        self.z, self.buffer, self.seen = z, buffer, set()
-
-        def copies(source):
-            for t in range(9):
-                rows = pl.ds(t * z.chan, z.chan)
-                yield pltpu.make_async_copy(source.at[rows], buffer.at[rows], sems.at[t])
-
-        self.waits = list(copies(own))
-        if mine is None:
-            for copy in self.waits:
-                copy.start()
+    def __init__(self, z, mine, own, other, buffer, sems, ahead=2):
+        self.z, self.mine, self.own, self.other = z, mine, own, other
+        self.buffer, self.sems, self.ahead, self.started, self.seen = buffer, sems, ahead, 0, set()
+        for _ in range(ahead):
+            self.start()
+
+    def copy(self, source, t):
+        rows = pl.ds(t * self.z.chan, self.z.chan)
+        return pltpu.make_async_copy(source.at[rows], self.buffer.at[rows], self.sems.at[t])
+
+    def start(self):
+        t = self.started
+        if t == 9:
             return
-
-        @pl.when(mine)
-        def _():
-            for copy in copies(own):
-                copy.start()
-
-        @pl.when(jnp.logical_not(mine))
-        def _():
-            for copy in copies(other):
-                copy.start()
+        self.started = t + 1
+        if self.mine is None:
+            self.copy(self.own, t).start()
+            return
+        pl.when(self.mine)(lambda: self.copy(self.own, t).start())
+        pl.when(jnp.logical_not(self.mine))(lambda: self.copy(self.other, t).start())
 
     def tap(self, t, columns=slice(None)):
         if t not in self.seen:
             self.seen.add(t)
-            self.waits[t].wait()
+            self.copy(self.own, t).wait()
+            self.start()
         return self.buffer[pl.ds(t * self.z.chan, self.z.chan), columns]
 
     def first(self, t):
@@ -202,15 +207,13 @@
     return rows_times_kernel(z, first, second, weights, scratch)
 
 
-def encoder_kernel(z, kernel, enc, images, out, patches_out, buffer, moves, sems, move_sem):
-    fetch = pltpu.make_async_copy(enc, moves, move_sem)
-    fetch.start()
+def encoder_kernel(z, kernel, sources, images, out, patches_out, buffer, sems):
     weights = Weights(z, None, kernel, None, buffer, sems)
-    fetch.wait()
-    columns = dot(moves[...], images[...]).astype(BF)
     total = None
     for t in range(9):
-        part = columns[t * z.both : (t + 1) * z.both]
+        at = sources[:, t : t + 1]
+        move = jnp.where(lanes((z.both, z.micro * z.fine)) == at, 1.0, 0.0).astype(BF)
+        part = dot(move, images[...]).astype(BF)
         patches_out[t, :, : z.chan] = part
         a = dot(part, weights.tap(t))
         total = a if total is None else total + a
@@ -221,22 +224,29 @@
         out[z.micro + m] = steep[m * z.rows : (m + 1) * z.rows]
 
 
-def centre_kernel(z, where, kernel, other, own, received, shift, out, slope_out, enc_slope_out, buffer, sems):
+def centre_kernel(
+    z, where, kernel, other, own, received, shift, out, slope_out, enc_slope_out, copies_out, buffer, sems
+):
     odd = lax.rem(where[0], 2) == 1
     weights = Weights(z, odd, kernel, other, buffer, sems)
     value = jnp.where(odd, received[1].astype(F32), own[0].astype(F32)).astype(BF)
     enc_slope_out[...] = jnp.where(odd, received[3].astype(F32), own[2].astype(F32))
     preact = conv_forward(z, value, weights, shift)
+    hidden = (value.astype(F32) + silu(preact)).astype(BF)
     out[0] = value
-    out[1] = (value.astype(F32) + silu(preact)).astype(BF)
+    out[1] = hidden
+    for k in range(z.dp):
+        copies_out[k] = hidden
     slope_out[...] = slope(preact)
 
 
 def middle_kernel(
-    z, where, kernel, other, inbound, targets, shift, back, parity, gather,
-    grads, own_out, send, scratch, delta_p, delta_q, sums_p, sums_q, buffer2, buffer3, sems2, sems3, *, scale,
+    z, where, kernel, other, inbound, targets, shift, back, parity, gather, patches, mine_forward,
+    grads, own_out, send, message, scratch, delta_p, delta_q, sums_p, sums_q, packing,
+    buffer2, buffer3, sems2, sems3, *, scale,
 ):
-    odd = lax.rem(where[0], 2) == 1
+    section = where[0]
+    odd = lax.rem(section, 2) == 1
     centre = Weights(z, jnp.logical_not(odd), kernel, other, buffer2, sems2)
     decoder = Weights(z, odd, kernel, other, buffer3, sems3)
     scratch[...] = jnp.zeros_like(scratch)
@@ -295,10 +305,25 @@
         here = sums(t)
         own_out[t] = here
         send[t] = here
-    own_out[9] = joined
-    send[9] = joined
-    own_out[10] = delta
-    send[10] = delta
+    own_out[9] = delta
+    send[9] = delta
+
+    packing[...] = jnp.zeros_like(packing)
+
+    @pl.when(section >= 2)
+    def _():
+        for k in range(z.dp):
+            message[k] = pack(z, packing, own_out[first_tap(z, k)], joined)
+
+    @pl.when(section < 2)
+    def _():
+        mine = pl.ds(pl.multiple_of(lax.rem(section, 2) * z.rows, 8), z.rows)
+        for k in range(z.dp):
+            tap = first_tap(z, k)
+            near = patches[tap, mine].astype(F32)
+            far = patches[min(tap + 1, 8), mine].astype(F32)
+            both = jnp.where(lanes(near.shape) < z.chan, near, pltpu.roll(far, z.chan, 1))
+            message[k] = pack(z, packing, both, mine_forward[0])
 
 
 def centre_back_kernel(
@@ -327,45 +352,6 @@
     return scratch[: z.packed].astype(BF)
 
 
-def prepare_zero_kernel(z, where, patches, inbound, out):
-    section = where[0]
-    n, rows = z.dp, z.rows
-    mine = pl.ds(pl.multiple_of(lax.rem(section, 2) * rows, 8), rows)
-
-    @pl.when(section < 2)
-    def _():
-        for k in range(n):
-            tap = first_tap(z, k)
-            near = patches[tap, mine].astype(F32)
-            far = patches[min(tap + 1, 8), mine].astype(F32)
-            both = jnp.where(lanes(near.shape) < z.chan, near, pltpu.roll(far, z.chan, 1))
-            out[k] = both.astype(BF)
-
-    @pl.when(section >= 2)
-    def _():
-        for k in range(n):
-            out[k] = inbound[1]
-
-
-def prepare_first_kernel(z, where, encoded, own, received, out, scratch):
-    section = where[0]
-    n = z.dp
-
-    def fill(top, bottom):
-        both = pack(z, scratch, top, bottom)
-        for k in range(n):
-            out[k] = both
-
-    pl.when(section < 2)(lambda: fill(encoded[0], encoded[1]))
-    pl.when(section == 3)(lambda: fill(received[9], own[9]))
-
-    @pl.when(section == 2)
-    def _():
-        for k in range(n):
-            tap = first_tap(z, k)
-            out[k] = pack(z, scratch, own[tap], received[tap])
-
-
 def prepare_second_kernel(z, where, back_own, back_received, middle_own, middle_received, out, scratch):
     section = where[0]
     n = z.dp
@@ -377,7 +363,7 @@
 
     pl.when(section == 0)(lambda: fill(back_own, back_received))
     pl.when(section == 1)(lambda: fill(back_received, back_own))
-    pl.when(section == 2)(lambda: fill(middle_own.at[10], middle_received.at[10]))
+    pl.when(section == 2)(lambda: fill(middle_own.at[9], middle_received.at[9]))
 
     @pl.when(section == 3)
     def _():
@@ -393,13 +379,27 @@
     return join_columns(z, first[: z.chan], second[move : move + z.chan])
 
 
-def left_kernel(z, where, many, zero, zero_other, one, one_other, lefts, early, scratch):
+def left_kernel(z, where, many, zero, zero_other, one, one_other, lefts, early, scratch, first, second):
     n = z.dp
     section, place = where[0], where[1]
     tap = first_tap(z, place)
 
     def rows_of(k):
         return pl.ds(k * z.packed, z.packed)
+
+    def halves(k):
+        first[: z.packed] = one_other[k].astype(F32)
+        second[: z.packed] = one[k].astype(F32)
+
+    def upper(k, even_first):
+        halves(k)
+        top, bottom = (first, second) if even_first else (second, first)
+        return pack(z, scratch, top[: z.rows], bottom[: z.rows])
+
+    def lower(k):
+        halves(k)
+        here = slice(z.cells, z.cells + z.rows)
+        return pack(z, scratch, first[here], second[here])
 
     def moved(value_of):
         for k in range(n):
@@ -409,19 +409,23 @@
                 move = many[pl.ds(pl.multiple_of(here * z.packed, 8), z.packed), :]
                 lefts[at, rows_of(k), :] = dot(move, value).astype(BF)
 
+    first[...] = jnp.zeros_like(first)
+    second[...] = jnp.zeros_like(second)
+
     @pl.when(section == 0)
     def _():
         for k in range(n):
-            lefts[0, rows_of(k), :] = pack(z, scratch, zero[k], zero_other[k])
-
-    pl.when(section == 1)(lambda: moved(lambda k: one[k]))
+            lefts[0, rows_of(k), :] = upper(k, False)
+
+    pl.when(section == 1)(lambda: moved(lower))
     pl.when(section == 2)(lambda: moved(lambda k: pack(z, scratch, zero[k], zero_other[k])))
 
     @pl.when(section == 3)
     def _():
         for k in range(n):
-            lefts[0, rows_of(k), :] = one[k]
-        early[...] = grouped(z, lefts[0], one_other[...].reshape(n * z.packed, z.width))
+            lefts[0, rows_of(k), :] = lower(k)
+            lefts[1, rows_of(k), :] = upper(k, True)
+        early[...] = grouped(z, lefts[0], lefts[1])
 
 
 def weight_kernel(z, where, right, lefts, early, out, rows_out):
@@ -486,10 +490,11 @@
 
     join = pltpu.VMEM((2, rows, width), F32)
     packing = pltpu.VMEM((both, width), F32)
+    message = shape(dp, z.packed, width)
+    small = 16 * 2**20
+    large = LIMIT
     buffer = pltpu.VMEM((z.taps_rows, width), BF)
     sems = pltpu.SemaphoreType.DMA((9,))
-    message = shape(dp, z.packed, width)
-    small = 16 * 2**20
 
     def across(x, bit):
         return lax.ppermute(x, "section", [(s, s ^ bit) for s in range(n_section)])
@@ -504,49 +509,48 @@
     encoded, patches = run(
         encoder_kernel,
         [shape(2 * z.micro, rows, width), shape(9, both, width)],
-        "hhv",
-        [buffer, pltpu.VMEM((9 * both, z.micro * z.fine), BF), sems, pltpu.SemaphoreType.DMA],
-        kernel, sel["enc"], image_rows,
+        "hvv",
+        [buffer, sems],
+        kernel, jnp.asarray(sources_of(z)), image_rows,
+        limit=large,
     )
     encoded_in = across(encoded, 1)
-    forward, centre_slope, enc_slope = run(
+    forward, centre_slope, enc_slope, copies = run(
         centre_kernel,
-        [shape(2, rows, width), shape(rows, width, dtype=F32), shape(rows, width, dtype=F32)],
+        [
+            shape(2, rows, width),
+            shape(rows, width, dtype=F32),
+            shape(rows, width, dtype=F32),
+            shape(dp, rows, width),
+        ],
         "shhvvv",
         [buffer, sems],
         where, kernel, other, encoded, encoded_in, sel["shift"],
+        limit=large,
     )
     forward_in = across(forward, 2)
-    zero = run(
-        prepare_zero_kernel, shape(dp, rows, width), "svv", [],
-        where, patches, forward_in, limit=small,
-    )
-    zero = spread(zero)
-    grads, middle_own, middle_send = run(
+    zero = spread(copies)
+    grads, middle_own, middle_send, one = run(
         functools.partial(middle_kernel, scale=scale),
-        [shape(2, rows, width), shape(11, rows, width), shape(11, rows, width)],
-        "shhvvvvvv",
+        [shape(2, rows, width), shape(10, rows, width), shape(10, rows, width), message],
+        "shhvvvvvvvv",
         [
             join,
             pltpu.VMEM((4 * rows, z.low), F32),
             pltpu.VMEM((4 * rows, z.low), F32),
             pltpu.VMEM((9 * rows, z.low), BF),
             pltpu.VMEM((9 * rows, z.width - z.high), BF),
+            packing,
             buffer,
             buffer,
             sems,
             sems,
         ],
         where, kernel, other, forward_in, target_rows,
-        sel["shift"], sel["back"], sel["parity"], sel["gather"],
-        flops=10**10,
+        sel["shift"], sel["back"], sel["parity"], sel["gather"], patches, forward,
+        flops=10**10, limit=large,
     )
     grads_in = across(grads, 2)
-    middle_in = across(middle_send, 1)
-    one = run(
-        prepare_first_kernel, message, "svvv", [packing],
-        where, encoded_in, middle_own, middle_in, limit=small,
-    )
     one = spread(one)
     back_own, back_send = run(
         centre_back_kernel,
@@ -554,21 +558,23 @@
         "shhvvvv",
         [join, buffer, sems],
         where, kernel, other, grads_in, enc_slope, centre_slope, sel["back"],
-        flops=10**10,
+        flops=10**10, limit=large,
     )
     back_in = across(back_send, 1)
+    middle_in = across(middle_send, 1)
     right = run(
         prepare_second_kernel, message, "svvvv", [packing],
         where, back_own, back_in, middle_own, middle_in, limit=small,
     )
     right = spread(right)
+    zero = across(zero, 2)
     zero_other = across(zero, 1)
     one_other = across(one, 1)
     lefts, early = run(
         left_kernel,
         [shape(2, dp * z.packed, width), shape(z.chan, width, dtype=F32)],
         "svvvvv",
-        [packing],
+        [packing, packing, packing],
         where, sel["many"], zero, zero_other, one, one_other,
         flops=10**10, limit=2 * small,
     )

time: 110 us -> 111 us (level); the launches traced: 109 us -> 109 us
  waiting for transfers between devices: 38.8 us -> 29.6 us
  Pallas kernels: 37.5 us -> 45.4 us
  starting transfers between devices: 20.2 us -> 23.5 us
  local copies, waits for them, and re-layouts: 11.7 us -> 9.71 us
    pallas_call x9 -> x7, Pallas kernels: 37.5 us -> 45.4 us  [run(): call(functools.partial(body, z), outs, spaces, scratch, **options)]
    all_to_all x3, waiting for transfers between devices: 33.7 us -> 28 us  [spread(): return lax.all_to_all(x, 'dp', 0, 0, tiled=True)]
    ppermute x8 -> x9, waiting for transfers between devices: 5.11 us -> 1.6 us  [across(): return lax.ppermute(x, 'section', [(s, s ^ bit) for s in range(n_section)])]
    unnamed x36 -> x26, local copies, waits for them, and re-layouts: 9.75 us -> 7.74 us
    ppermute x8 -> x9, starting transfers between devices: 6.93 us -> 8.92 us  [across(): return lax.ppermute(x, 'section', [(s, s ^ bit) for s in range(n_section)])]
    all_to_all x3, starting transfers between devices: 13.2 us -> 14.6 us  [spread(): return lax.all_to_all(x, 'dp', 0, 0, tiled=True)]
  transfers between devices with their start and end apart: 11 -> 12, of which waited for: 6 -> 4; matrix products, arithmetic and copies ran while one was open for 3% -> 3% of each run, Pallas kernels for 14% -> 32%
where the time goes in v3:
time: 111 us; the launch traced here: 109 us
  Pallas kernels  45.4 us (41%)
  waiting for transfers between devices  29.6 us (27%)
  starting transfers between devices  23.5 us (21%)
  local copies, waits for them, and re-layouts  9.71 us (9%)
    pallas_call x7, Pallas kernels, run(): call(functools.partial(body, z), outs, spaces, scratch, **options)  45.4 us
    all_to_all x3, waiting for transfers between devices, spread(): return lax.all_to_all(x, 'dp', 0, 0, tiled=True)  28 us
    all_to_all x3, starting transfers between devices, spread(): return lax.all_to_all(x, 'dp', 0, 0, tiled=True)  14.6 us
    ppermute x9, starting transfers between devices, across(): return lax.ppermute(x, 'section', [(s, s ^ bit) for s in range(n_section)])  8.92 us
    unnamed x26, local copies, waits for them, and re-layouts  7.74 us
  transfers between devices with their start and end apart: 12, of which 4 were waited for; matrix products, arithmetic and copies ran while one was open for 3% of the time, Pallas kernels for 32%

profile of v3, /device:TPU:1, one launch (start us, length us, event | category | flops | bytes accessed | tf_op | source)
XLA Modules:
  0.0 108.9 jit_solution(9065327967417127046)
XLA Ops:
  0.0 0.0 collective-permute-start
  0.0 0.9 copy.12
  1.0 1.0 reshape.6.images
  1.9 7.2 %shard_map.91 = (bf16[4,40,640]{2,1,0:T(8,128)(2,1)}, bf16[9,80,640]{2,1,0:T(8,128)(2,1)}) custom-call(bf16[2880,640]{1,0:T(8,128)(2,1)} %bitcast.9, s32[80,9]{1,0:T(8,128)} %constant.25.clone.sources, bf16[288,320]{1,0:T(8,128)(2,1)} %reshape.6.images), custom_call_target="tpu_custom_call" | custom-call | flops 100000000 | bytes 4194304 | tf_op jit(solution)/shard_map/pallas_call | solution.py:506
  9.1 0.6 collective-permute-start.1
  9.7 0.6 pad_add_fusion.where
  10.3 0.0 copy-start.9
  10.3 0.7 collective-permute-done.1.received
  11.0 0.0 copy-start.8
  11.0 0.0 collective-permute-done.other
  11.0 0.7 copy-done.8
  11.7 7.4 %shard_map.92 = (bf16[2,40,640]{2,1,0:T(8,128)(2,1)}, f32[40,640]{1,0:T(8,128)}, f32[40,640]{1,0:T(8,128)}, bf16[8,40,640]{2,1,0:T(8,128)(2,1)}) custom-call(s32[2]{0:T(128)} %pad_add_fusion.where, bf16[2880,640]{1,0:T(8,128)(2,1)} %bitcast.10, bf16[2880,640]{1,0:T(8,128)(2,1)} %collective-permute-done.other, bf16[4,40,640]{2,1,0:T(8,128)(2,1)} %get-tuple-element.19.own, ...), custom_call_target="tpu_custom_call" | custom-call | flops 100000000 | bytes 4194304 | tf_op jit(solution)/shard_map/pallas_call | solution.py:506
  19.1 2.6 %collective-permute-start.2 = (bf16[2,40,640]{2,1,0:T(8,128)(2,1)}, bf16[2,40,640]{2,1,0:T(8,128)(2,1)S(1)}, u32[]{:S(2)}, u32[]{:S(2)}) collective-permute-start(bf16[2,40,640]{2,1,0:T(8,128)(2,1)} %get-tuple-element.20.mine_forward), channel_id=1, source_target_pairs={{0,16},{8,24},{16,0},{24,8},{1,17},{9,25},{17,1},{25,9},{2,18},{10... | collective-permute-start | bytes 307208 | tf_op jit(solution)/shard_map/ppermute | solution.py:500
  21.7 0.0 copy-done.9
  21.8 1.0 reshape.7.targets
  22.8 5.6 %all-to-all-start.1 = ((bf16[8,40,640]{2,1,0:T(8,128)(2,1)}), bf16[8,40,640]{2,1,0:T(8,128)(2,1)}, u32[]{:S(2)}, u32[]{:S(2)}) async-start(bf16[8,40,640]{2,1,0:T(8,128)(2,1)} %get-tuple-element.29), calls=%async_computation.1 | async-start | bytes 819200 | tf_op jit(solution)/shard_map/all_to_all | solution.py:503
  28.3 0.0 collective-permute-done.2.inbound
  28.3 0.0 copy-start.11
  28.3 0.6 copy-done.11
  29.0 17.3 %shard_map.93 = (bf16[2,40,640]{2,1,0:T(8,128)(2,1)}, bf16[10,40,640]{2,1,0:T(8,128)(2,1)}, bf16[10,40,640]{2,1,0:T(8,128)(2,1)}, bf16[8,72,640]{2,1,0:T(8,128)(2,1)}) custom-call(s32[2]{0:T(128)} %pad_add_fusion.where, bf16[2880,640]{1,0:T(8,128)(2,1)} %bitcast.11, bf16[2880,640]{1,0:T(8,128)(2,1)} %collective-permute-done.other, ...), custom_call_target="tpu_custom_call" | custom-call | flops 10000000000 | bytes 4194304 | tf_op jit(solution)/shard_map/pallas_call | solution.py:506
  46.2 0.0 all-to-all-done.1
  46.3 5.5 %all-to-all-start.2 = ((bf16[8,72,640]{2,1,0:T(8,128)(2,1)}), bf16[8,72,640]{2,1,0:T(8,128)(2,1)S(1)}, u32[]{:S(2)}, u32[]{:S(2)}) async-start(bf16[8,72,640]{2,1,0:T(8,128)(2,1)} %get-tuple-element.30), calls=%async_computation.2 | async-start | bytes 1474560 | tf_op jit(solution)/shard_map/all_to_all | solution.py:503
  51.7 0.1 collective-permute-start.3
  51.9 1.4 %collective-permute-start.5 = (bf16[10,40,640]{2,1,0:T(8,128)(2,1)}, bf16[10,40,640]{2,1,0:T(8,128)(2,1)S(1)}, u32[]{:S(2)}, u32[]{:S(2)}) collective-permute-start(bf16[10,40,640]{2,1,0:T(8,128)(2,1)} %get-tuple-element.28), channel_id=1, source_target_pairs={{0,8},{8,0},{16,24},{24,16},{1,9},{9,1},{17,25},{25,17},{2,10},{10... | collective-permute-start | bytes 1536008 | tf_op jit(solution)/shard_map/ppermute | solution.py:500
  53.3 1.3 %collective-permute-start.6 = (bf16[8,40,640]{2,1,0:T(8,128)(2,1)}, bf16[8,40,640]{2,1,0:T(8,128)(2,1)S(1)}, u32[]{:S(2)}, u32[]{:S(2)}) collective-permute-start(bf16[8,40,640]{2,1,0:T(8,128)(2,1)} %all-to-all-done.1), channel_id=1, source_target_pairs={{0,16},{8,24},{16,0},{24,8},{1,17},{9,25},{17,1},{25,9},{2,18},{10... | collective-permute-start | bytes 1228808 | tf_op jit(solution)/shard_map/ppermute | solution.py:500
  54.6 14.9 %all-to-all-done.2.one = bf16[8,72,640]{2,1,0:T(8,128)(2,1)S(1)} async-done(((bf16[8,72,640]{2,1,0:T(8,128)(2,1)}), bf16[8,72,640]{2,1,0:T(8,128)(2,1)S(1)}, u32[]{:S(2)}, u32[]{:S(2)}) %all-to-all-start.2) | async-done | bytes 737312 | tf_op jit(solution)/shard_map/all_to_all | solution.py:503
  69.5 0.0 copy-start
  69.6 2.2 %collective-permute-start.8 = (bf16[8,72,640]{2,1,0:T(8,128)(2,1)S(1)}, bf16[8,72,640]{2,1,0:T(8,128)(2,1)S(1)}, u32[]{:S(2)}, u32[]{:S(2)}) collective-permute-start(bf16[8,72,640]{2,1,0:T(8,128)(2,1)S(1)} %all-to-all-done.2.one), channel_id=1, source_target_pairs={{0,8},{8,0},{16,24},{24,16},{1,9},{9,1},{17,25},{25,17},{2,10},{10... | collective-permute-start | bytes 2211848 | tf_op jit(solution)/shard_map/ppermute | solution.py:500
  71.8 0.0 collective-permute-done.3.grads
  71.8 0.0 copy-start.10
  71.8 0.6 copy-done.10
  72.4 0.0 copy-start.2
  72.4 0.0 copy-start.4
  72.4 7.3 %shard_map.94 = (bf16[40,640]{1,0:T(8,128)(2,1)}, bf16[40,640]{1,0:T(8,128)(2,1)}) custom-call(s32[2]{0:T(128)} %pad_add_fusion.where, bf16[2880,640]{1,0:T(8,128)(2,1)} %bitcast.12, bf16[2880,640]{1,0:T(8,128)(2,1)} %collective-permute-done.other, bf16[2,40,640]{2,1,0:T(8,128)(2,1)} %copy-done.10, f32[40,640]{1,0:T(8,128)} %get-tuple-element.23.enc_slope, ...), custom_call_target="tpu_custom_call" | custom-call | flops 10000000000 | bytes 4194304 | tf_op jit(solution)/shard_map/pallas_call | solution.py:506
  79.8 0.0 copy-done
  79.8 0.1 collective-permute-start.4
  79.9 0.0 collective-permute-done.6.zero
  79.9 0.5 collective-permute-start.7
  80.3 0.9 collective-permute-done.4.back_received
  81.3 0.0 collective-permute-done.5.middle_received
  81.3 0.0 copy-done.2
  81.3 0.0 copy-done.4
  81.3 0.0 copy-start.3
  81.3 0.8 copy-done.3
  82.1 1.5 %shard_map.95 = bf16[8,72,640]{2,1,0:T(8,128)(2,1)} custom-call(s32[2]{0:T(128)S(1)} %copy-done.4, bf16[40,640]{1,0:T(8,128)(2,1)S(1)} %copy-done.3, bf16[40,640]{1,0:T(8,128)(2,1)S(1)} %collective-permute-done.4.back_received, bf16[10,40,640]{2,1,0:T(8,128)(2,1)S(1)} %copy-done.2, bf16[10,40,640]{2,1,0:T(8,128)(2,1)S(1)} %collective-permute-done.5.middle_received), custom_call_target="tpu_custom_call" | custom-call | flops 100000000 | bytes 4194304 | tf_op jit(solution)/shard_map/pallas_call | solution.py:506
  83.6 3.5 %all-to-all-start = ((bf16[8,72,640]{2,1,0:T(8,128)(2,1)}), bf16[8,72,640]{2,1,0:T(8,128)(2,1)S(1)}, u32[]{:S(2)}, u32[]{:S(2)}) async-start(bf16[8,72,640]{2,1,0:T(8,128)(2,1)} %shard_map.95), calls=%async_computation | async-start | bytes 1474560 | tf_op jit(solution)/shard_map/all_to_all | solution.py:503
  87.1 0.0 collective-permute-done.7.zero_other
  87.1 0.0 collective-permute-done.8.one_other
  87.2 0.0 copy-start.5
  87.2 0.9 copy-done.5
  88.0 0.0 copy-start.1
  88.0 1.1 %copy-done.1 = bf16[8,72,640]{2,1,0:T(8,128)(2,1)S(1)} copy-done((bf16[8,72,640]{2,1,0:T(8,128)(2,1)S(1)}, bf16[8,72,640]{2,1,0:T(8,128)(2,1)}, u32[]{:S(2)}) %copy-start.1) | copy-done | bytes 737304
  89.2 0.0 copy-start.6
  89.2 1.1 %copy-done.6 = bf16[8,72,640]{2,1,0:T(8,128)(2,1)S(1)} copy-done((bf16[8,72,640]{2,1,0:T(8,128)(2,1)S(1)}, bf16[8,72,640]{2,1,0:T(8,128)(2,1)}, u32[]{:S(2)}) %copy-start.6) | copy-done | bytes 737304
  90.3 0.0 copy-start.7
  90.3 0.9 copy-done.7
  91.2 1.8 %shard_map.96 = (bf16[2,576,640]{2,1,0:T(8,128)(2,1)S(1)}, f32[320,640]{1,0:T(8,128)S(1)}) custom-call(s32[2]{0:T(128)S(1)} %copy-done.4, bf16[648,72]{1,0:T(8,128)(2,1)S(1)} %copy-done.7, bf16[8,40,640]{2,1,0:T(8,128)(2,1)S(1)} %collective-permute-done.6.zero, bf16[8,40,640]{2,1,0:T(8,128)(2,1)} %collective-permute-done.7.zero_other, ...), custom_call_target="tpu_custom_call" | custom-call | flops 10000000000 | bytes 4194304 | tf_op jit(solution)/shard_map/pallas_call | solution.py:506
  93.0 13.0 %all-to-all-done.right = bf16[8,72,640]{2,1,0:T(8,128)(2,1)S(1)} async-done(((bf16[8,72,640]{2,1,0:T(8,128)(2,1)}), bf16[8,72,640]{2,1,0:T(8,128)(2,1)S(1)}, u32[]{:S(2)}, u32[]{:S(2)}) %all-to-all-start) | async-done | bytes 737312 | tf_op jit(solution)/shard_map/all_to_all | solution.py:503
  106.0 2.9 %shard_map.97 = f32[360,640]{1,0:T(8,128)} custom-call(s32[2]{0:T(128)S(1)} %copy-done.4, bf16[8,72,640]{2,1,0:T(8,128)(2,1)S(1)} %all-to-all-done.right, bf16[2,576,640]{2,1,0:T(8,128)(2,1)S(1)} %get-tuple-element.31.lefts, f32[320,640]{1,0:T(8,128)S(1)} %get-tuple-element.32.early), custom_call_target="tpu_custom_call" | custom-call | flops 100000000 | bytes 4194304 | tf_op jit(solution)/shard_map/pallas_call | solution.py:506
  (1 shorter events, 0.0 us)
Async XLA Ops:
  0.0 11.0 %collective-permute-start = (bf16[2880,640]{1,0:T(8,128)(2,1)}, bf16[2880,640]{1,0:T(8,128)(2,1)}, u32[]{:S(2)}, u32[]{:S(2)}) collective-permute-start(bf16[2880,640]{1,0:T(8,128)(2,1)} %bitcast.8), channel_id=1, source_target_pairs={{0,8},{8,0},{16,24},{24,16},{1,9},{9,1},{17,25},{25,17},{2,10},{10... | collective-permute-start | bytes 11059208 | tf_op jit(solution)/shard_map/ppermute | solution.py:500
  9.1 1.9 %collective-permute-start.1 = (bf16[4,40,640]{2,1,0:T(8,128)(2,1)}, bf16[4,40,640]{2,1,0:T(8,128)(2,1)S(1)}, u32[]{:S(2)}, u32[]{:S(2)}) collective-permute-start(bf16[4,40,640]{2,1,0:T(8,128)(2,1)} %get-tuple-element.19.own), channel_id=1, source_target_pairs={{0,8},{8,0},{16,24},{24,16},{1,9},{9,1},{17,25},{25,17},{2,10},{10... | collective-permute-start | bytes 614408 | tf_op jit(solution)/shard_map/ppermute | solution.py:500
  10.3 11.4 %copy-start.9 = (bf16[2,1,12,3840]{3,0,2,1:T(2,128)(2,1)S(1)}, bf16[2,1,12,3840]{3,0,2,1:T(2,128)(2,1)}, u32[]{:S(2)}) copy-start(bf16[2,1,12,3840]{3,0,2,1:T(2,128)(2,1)} %param.10) | copy-start | bytes 552964
  11.0 0.7 copy-start.8
  19.1 9.2 %collective-permute-start.2 = (bf16[2,40,640]{2,1,0:T(8,128)(2,1)}, bf16[2,40,640]{2,1,0:T(8,128)(2,1)S(1)}, u32[]{:S(2)}, u32[]{:S(2)}) collective-permute-start(bf16[2,40,640]{2,1,0:T(8,128)(2,1)} %get-tuple-element.20.mine_forward), channel_id=1, source_target_pairs={{0,16},{8,24},{16,0},{24,8},{1,17},{9,25},{17,1},{25,9},{2,18},{10... | collective-permute-start | bytes 307208 | tf_op jit(solution)/shard_map/ppermute | solution.py:500
  22.8 23.5 %all-to-all-start.1 = ((bf16[8,40,640]{2,1,0:T(8,128)(2,1)}), bf16[8,40,640]{2,1,0:T(8,128)(2,1)}, u32[]{:S(2)}, u32[]{:S(2)}) async-start(bf16[8,40,640]{2,1,0:T(8,128)(2,1)} %get-tuple-element.29), calls=%async_computation.1 | async-start | bytes 819200 | tf_op jit(solution)/shard_map/all_to_all | solution.py:503
  28.3 0.6 copy-start.11
  46.3 23.3 %all-to-all-start.2 = ((bf16[8,72,640]{2,1,0:T(8,128)(2,1)}), bf16[8,72,640]{2,1,0:T(8,128)(2,1)S(1)}, u32[]{:S(2)}, u32[]{:S(2)}) async-start(bf16[8,72,640]{2,1,0:T(8,128)(2,1)} %get-tuple-element.30), calls=%async_computation.2 | async-start | bytes 1474560 | tf_op jit(solution)/shard_map/all_to_all | solution.py:503
  51.7 20.1 %collective-permute-start.3 = (bf16[2,40,640]{2,1,0:T(8,128)(2,1)}, bf16[2,40,640]{2,1,0:T(8,128)(2,1)S(1)}, u32[]{:S(2)}, u32[]{:S(2)}) collective-permute-start(bf16[2,40,640]{2,1,0:T(8,128)(2,1)} %get-tuple-element.22), channel_id=1, source_target_pairs={{0,16},{8,24},{16,0},{24,8},{1,17},{9,25},{17,1},{25,9},{2,18},{10... | collective-permute-start | bytes 307208 | tf_op jit(solution)/shard_map/ppermute | solution.py:500
  51.9 29.4 %collective-permute-start.5 = (bf16[10,40,640]{2,1,0:T(8,128)(2,1)}, bf16[10,40,640]{2,1,0:T(8,128)(2,1)S(1)}, u32[]{:S(2)}, u32[]{:S(2)}) collective-permute-start(bf16[10,40,640]{2,1,0:T(8,128)(2,1)} %get-tuple-element.28), channel_id=1, source_target_pairs={{0,8},{8,0},{16,24},{24,16},{1,9},{9,1},{17,25},{25,17},{2,10},{10... | collective-permute-start | bytes 1536008 | tf_op jit(solution)/shard_map/ppermute | solution.py:500
  53.3 26.6 %collective-permute-start.6 = (bf16[8,40,640]{2,1,0:T(8,128)(2,1)}, bf16[8,40,640]{2,1,0:T(8,128)(2,1)S(1)}, u32[]{:S(2)}, u32[]{:S(2)}) collective-permute-start(bf16[8,40,640]{2,1,0:T(8,128)(2,1)} %all-to-all-done.1), channel_id=1, source_target_pairs={{0,16},{8,24},{16,0},{24,8},{1,17},{9,25},{17,1},{25,9},{2,18},{10... | collective-permute-start | bytes 1228808 | tf_op jit(solution)/shard_map/ppermute | solution.py:500
  69.5 10.2 %copy-start = (bf16[8,72,640]{2,1,0:T(8,128)(2,1)}, bf16[8,72,640]{2,1,0:T(8,128)(2,1)S(1)}, u32[]{:S(2)}) copy-start(bf16[8,72,640]{2,1,0:T(8,128)(2,1)S(1)} %all-to-all-done.2.one) | copy-start | bytes 2211844
  69.6 17.6 %collective-permute-start.8 = (bf16[8,72,640]{2,1,0:T(8,128)(2,1)S(1)}, bf16[8,72,640]{2,1,0:T(8,128)(2,1)S(1)}, u32[]{:S(2)}, u32[]{:S(2)}) collective-permute-start(bf16[8,72,640]{2,1,0:T(8,128)(2,1)S(1)} %all-to-all-done.2.one), channel_id=1, source_target_pairs={{0,8},{8,0},{16,24},{24,16},{1,9},{9,1},{17,25},{25,17},{2,10},{10... | collective-permute-start | bytes 2211848 | tf_op jit(solution)/shard_map/ppermute | solution.py:500
  71.8 0.6 copy-start.10
  72.4 8.9 %copy-start.2 = (bf16[10,40,640]{2,1,0:T(8,128)(2,1)S(1)}, bf16[10,40,640]{2,1,0:T(8,128)(2,1)}, u32[]{:S(2)}) copy-start(bf16[10,40,640]{2,1,0:T(8,128)(2,1)} %get-tuple-element.27.middle_own) | copy-start | bytes 1536004
  72.4 8.9 %copy-start.4 = (s32[2]{0:T(128)S(1)}, s32[2]{0:T(128)}, u32[]{:S(2)}) copy-start(s32[2]{0:T(128)} %pad_add_fusion.where) | copy-start | bytes 28
  79.8 1.5 %collective-permute-start.4 = (bf16[40,640]{1,0:T(8,128)(2,1)}, bf16[40,640]{1,0:T(8,128)(2,1)S(1)}, u32[]{:S(2)}, u32[]{:S(2)}) collective-permute-start(bf16[40,640]{1,0:T(8,128)(2,1)} %get-tuple-element.26), channel_id=1, source_target_pairs={{0,8},{8,0},{16,24},{24,16},{1,9},{9,1},{17,25},{25,17},{2,10},{10... | collective-permute-start | bytes 153608 | tf_op jit(solution)/shard_map/ppermute | solution.py:500
  79.9 7.2 %collective-permute-start.7 = (bf16[8,40,640]{2,1,0:T(8,128)(2,1)S(1)}, bf16[8,40,640]{2,1,0:T(8,128)(2,1)}, u32[]{:S(2)}, u32[]{:S(2)}) collective-permute-start(bf16[8,40,640]{2,1,0:T(8,128)(2,1)S(1)} %collective-permute-done.6.zero), channel_id=1, source_target_pairs={{0,8},{8,0},{16,24},{24,16},{1,9},{9,1},{17,25},{25,17},{2,10},{10... | collective-permute-start | bytes 1228808 | tf_op jit(solution)/shard_map/ppermute | solution.py:500
  81.3 0.8 copy-start.3
  83.6 22.4 %all-to-all-start = ((bf16[8,72,640]{2,1,0:T(8,128)(2,1)}), bf16[8,72,640]{2,1,0:T(8,128)(2,1)S(1)}, u32[]{:S(2)}, u32[]{:S(2)}) async-start(bf16[8,72,640]{2,1,0:T(8,128)(2,1)} %shard_map.95), calls=%async_computation | async-start | bytes 1474560 | tf_op jit(solution)/shard_map/all_to_all | solution.py:503
  87.2 0.9 copy-start.5
  88.0 1.1 %copy-start.1 = (bf16[8,72,640]{2,1,0:T(8,128)(2,1)S(1)}, bf16[8,72,640]{2,1,0:T(8,128)(2,1)}, u32[]{:S(2)}) copy-start(bf16[8,72,640]{2,1,0:T(8,128)(2,1)} %copy-done) | copy-start | bytes 2211844
  89.2 1.1 %copy-start.6 = (bf16[8,72,640]{2,1,0:T(8,128)(2,1)S(1)}, bf16[8,72,640]{2,1,0:T(8,128)(2,1)}, u32[]{:S(2)}) copy-start(bf16[8,72,640]{2,1,0:T(8,128)(2,1)} %copy-done.5) | copy-start | bytes 2211844
  90.3 0.9 copy-start.7

commit v4 on v3

--- a/solution.py
+++ b/solution.py
@@ -131,32 +131,25 @@
 
 
 class Weights:
-    def __init__(self, z, mine, own, other, buffer, sems, ahead=2):
-        self.z, self.mine, self.own, self.other = z, mine, own, other
-        self.buffer, self.sems, self.ahead, self.started, self.seen = buffer, sems, ahead, 0, set()
-        for _ in range(ahead):
-            self.start()
-
-    def copy(self, source, t):
-        rows = pl.ds(t * self.z.chan, self.z.chan)
-        return pltpu.make_async_copy(source.at[rows], self.buffer.at[rows], self.sems.at[t])
+    def __init__(self, z, mine, own, other, buffer, sem):
+        self.z, self.buffer, self.there, self.started = z, buffer, False, False
+        self.mine, self.own, self.other, self.sem = mine, own, other, sem
+
+    def copy(self, source):
+        return pltpu.make_async_copy(source, self.buffer, self.sem)
 
     def start(self):
-        t = self.started
-        if t == 9:
-            return
-        self.started = t + 1
         if self.mine is None:
-            self.copy(self.own, t).start()
-            return
-        pl.when(self.mine)(lambda: self.copy(self.own, t).start())
-        pl.when(jnp.logical_not(self.mine))(lambda: self.copy(self.other, t).start())
+            self.copy(self.own).start()
+        else:
+            pl.when(self.mine)(lambda: self.copy(self.own).start())
+            pl.when(jnp.logical_not(self.mine))(lambda: self.copy(self.other).start())
+        return self
+
+    def wait(self):
+        self.copy(self.own).wait()
 
     def tap(self, t, columns=slice(None)):
-        if t not in self.seen:
-            self.seen.add(t)
-            self.copy(self.own, t).wait()
-            self.start()
         return self.buffer[pl.ds(t * self.z.chan, self.z.chan), columns]
 
     def first(self, t):
@@ -166,10 +159,12 @@
         return self.tap(t, slice(self.z.high, self.z.width))
 
 
-def conv_forward(z, value, weights, shift):
+def conv_forward(z, value, weights, shift, ready=None):
     first, second = split_groups(z, value)
     first = dot(shift[...], first).astype(BF)
     second = dot(shift[...], second).astype(BF)
+    if ready is not None:
+        ready()
     total_first = total_second = None
     for t in range(9):
         a = dot(first[tap_rows(z, t)], weights.first(t))
@@ -197,25 +192,31 @@
     return join_groups(z, total_first, total_second, scratch)
 
 
-def conv_backward(z, delta, weights, back, scratch):
+def conv_backward(z, delta, weights, back, scratch, ready=None):
     first = delta[:, : z.low].astype(F32)
     first = jnp.where(lanes(first.shape) < z.group, first, 0.0).astype(BF)
     second = delta[:, z.high :].astype(F32)
     second = jnp.where(lanes(second.shape) >= z.group - z.high, second, 0.0).astype(BF)
     first = dot(back[...], first).astype(BF)
     second = dot(back[...], second).astype(BF)
+    if ready is not None:
+        ready()
     return rows_times_kernel(z, first, second, weights, scratch)
 
 
-def encoder_kernel(z, kernel, sources, images, out, patches_out, buffer, sems):
-    weights = Weights(z, None, kernel, None, buffer, sems)
-    total = None
+def encoder_kernel(z, kernel, sources, images, out, patches_out, buffer, sem):
+    weights = Weights(z, None, kernel, None, buffer, sem).start()
+    parts = []
     for t in range(9):
         at = sources[:, t : t + 1]
         move = jnp.where(lanes((z.both, z.micro * z.fine)) == at, 1.0, 0.0).astype(BF)
         part = dot(move, images[...]).astype(BF)
         patches_out[t, :, : z.chan] = part
-        a = dot(part, weights.tap(t))
+        parts.append(part)
+    weights.wait()
+    total = None
+    for t in range(9):
+        a = dot(parts[t], weights.tap(t))
         total = a if total is None else total + a
     encoded = silu(total).astype(BF)
     steep = slope(total).astype(BF)
@@ -228,10 +229,10 @@
     z, where, kernel, other, own, received, shift, out, slope_out, enc_slope_out, copies_out, buffer, sems
 ):
     odd = lax.rem(where[0], 2) == 1
-    weights = Weights(z, odd, kernel, other, buffer, sems)
+    weights = Weights(z, odd, kernel, other, buffer, sems).start()
     value = jnp.where(odd, received[1].astype(F32), own[0].astype(F32)).astype(BF)
     enc_slope_out[...] = jnp.where(odd, received[3].astype(F32), own[2].astype(F32))
-    preact = conv_forward(z, value, weights, shift)
+    preact = conv_forward(z, value, weights, shift, weights.wait)
     hidden = (value.astype(F32) + silu(preact)).astype(BF)
     out[0] = value
     out[1] = hidden
@@ -247,17 +248,23 @@
 ):
     section = where[0]
     odd = lax.rem(section, 2) == 1
-    centre = Weights(z, jnp.logical_not(odd), kernel, other, buffer2, sems2)
+    centre = Weights(z, jnp.logical_not(odd), kernel, other, buffer2, sems2).start()
     decoder = Weights(z, odd, kernel, other, buffer3, sems3)
     scratch[...] = jnp.zeros_like(scratch)
     encoded = inbound[0]
     hidden = inbound[1]
-    preact = conv_forward(z, hidden, centre, shift)
+
+    def ready():
+        centre.wait()
+        decoder.start()
+
+    preact = conv_forward(z, hidden, centre, shift, ready)
     hidden3 = (hidden.astype(F32) + silu(preact)).astype(BF)
     joined = (hidden3.astype(F32) + encoded.astype(F32)).astype(BF)
     first, second = split_groups(z, joined)
     first = dot(shift[...], first).astype(BF)
     second = dot(shift[...], second).astype(BF)
+    decoder.wait()
     total_p = [None] * 4
     total_q = [None] * 4
     for t, (a, b) in enumerate(TAPS):
@@ -330,11 +337,11 @@
     z, where, kernel, other, grads, enc_slope, centre_slope, back, own_out, send, scratch, buffer, sems
 ):
     odd = lax.rem(where[0], 2) == 1
-    weights = Weights(z, odd, kernel, other, buffer, sems)
+    weights = Weights(z, odd, kernel, other, buffer, sems).start()
     scratch[...] = jnp.zeros_like(scratch)
     above = grads[0].astype(F32)
     delta = (above * centre_slope[...]).astype(BF)
-    flow = conv_backward(z, delta, weights, back, scratch)
+    flow = conv_backward(z, delta, weights, back, scratch, weights.wait)
     below = (above + flow).astype(BF)
     total = below.astype(F32) + grads[1].astype(F32)
     deep = total * enc_slope[...]
@@ -494,7 +501,7 @@
     small = 16 * 2**20
     large = LIMIT
     buffer = pltpu.VMEM((z.taps_rows, width), BF)
-    sems = pltpu.SemaphoreType.DMA((9,))
+    sems = pltpu.SemaphoreType.DMA
 
     def across(x, bit):
         return lax.ppermute(x, "section", [(s, s ^ bit) for s in range(n_section)])

time: 111 us -> 98.6 us (0.89)
  Pallas kernels: 45.4 us -> 33.7 us
    pallas_call x7, Pallas kernels: 45.4 us -> 33.7 us  [run(): call(functools.partial(body, z), outs, spaces, scratch, **options)]
  transfers between devices with their start and end apart: 12 -> 12, of which waited for: 4 -> 4; matrix products, arithmetic and copies ran while one was open for 3% -> 4% of each run, Pallas kernels for 32% -> 26%
where the time goes in v4:
time: 98.6 us; the launch traced here: 97.1 us
  Pallas kernels  33.7 us (34%)
  waiting for transfers between devices  29.2 us (30%)
  starting transfers between devices  23.7 us (24%)
  local copies, waits for them, and re-layouts  9.71 us (10%)
    pallas_call x7, Pallas kernels, run(): call(functools.partial(body, z), outs, spaces, scratch, **options)  33.7 us
    all_to_all x3, waiting for transfers between devices, spread(): return lax.all_to_all(x, 'dp', 0, 0, tiled=True)  27.6 us
    all_to_all x3, starting transfers between devices, spread(): return lax.all_to_all(x, 'dp', 0, 0, tiled=True)  14.6 us
    ppermute x9, starting transfers between devices, across(): return lax.ppermute(x, 'section', [(s, s ^ bit) for s in range(n_section)])  9.09 us
    unnamed x26, local copies, waits for them, and re-layouts  7.74 us
  transfers between devices with their start and end apart: 12, of which 4 were waited for; matrix products, arithmetic and copies ran while one was open for 4% of the time, Pallas kernels for 26%

profile of v4, /device:TPU:1, one launch (start us, length us, event | category | flops | bytes accessed | tf_op | source)
XLA Modules:
  0.0 97.1 jit_solution(1700931439684178540)
XLA Ops:
  0.0 0.0 collective-permute-start
  0.0 0.9 copy.12
  1.0 1.0 %reshape.6.images = bf16[288,320]{1,0:T(8,128)(2,1)} reshape(bf16[2,1,12,3840]{3,2,0,1:T(8,128)(2,1)S(1)} %copy.12) | data formatting | bytes 368640 | tf_op jit(solution)/shard_map/reshape | solution.py:491
  1.9 4.8 %shard_map.91 = (bf16[4,40,640]{2,1,0:T(8,128)(2,1)}, bf16[9,80,640]{2,1,0:T(8,128)(2,1)}) custom-call(bf16[2880,640]{1,0:T(8,128)(2,1)} %bitcast.9, s32[80,9]{1,0:T(8,128)} %constant.25.clone.sources, bf16[288,320]{1,0:T(8,128)(2,1)} %reshape.6.images), custom_call_target="tpu_custom_call" | custom-call | flops 100000000 | bytes 4194304 | tf_op jit(solution)/shard_map/pallas_call | solution.py:513
  6.7 0.5 collective-permute-start.1
  7.3 0.6 pad_add_fusion.where
  7.9 0.0 copy-start.9
  7.9 0.7 collective-permute-done.1.received
  8.6 0.0 copy-start.8
  8.6 0.0 collective-permute-done.other
  8.6 0.7 copy-done.8
  9.2 5.1 %shard_map.92 = (bf16[2,40,640]{2,1,0:T(8,128)(2,1)}, f32[40,640]{1,0:T(8,128)}, f32[40,640]{1,0:T(8,128)}, bf16[8,40,640]{2,1,0:T(8,128)(2,1)}) custom-call(s32[2]{0:T(128)} %pad_add_fusion.where, bf16[2880,640]{1,0:T(8,128)(2,1)} %bitcast.10, bf16[2880,640]{1,0:T(8,128)(2,1)} %collective-permute-done.other, bf16[4,40,640]{2,1,0:T(8,128)(2,1)} %get-tuple-element.19.own, ...), custom_call_target="tpu_custom_call" | custom-call | flops 100000000 | bytes 4194304 | tf_op jit(solution)/shard_map/pallas_call | solution.py:513
  14.3 2.6 %collective-permute-start.2 = (bf16[2,40,640]{2,1,0:T(8,128)(2,1)}, bf16[2,40,640]{2,1,0:T(8,128)(2,1)S(1)}, u32[]{:S(2)}, u32[]{:S(2)}) collective-permute-start(bf16[2,40,640]{2,1,0:T(8,128)(2,1)} %get-tuple-element.20.mine_forward), channel_id=1, source_target_pairs={{0,16},{8,24},{16,0},{24,8},{1,17},{9,25},{17,1},{25,9},{2,18},{10... | collective-permute-start | bytes 307208 | tf_op jit(solution)/shard_map/ppermute | solution.py:507
  17.0 0.0 copy-done.9
  17.0 1.0 %reshape.7.targets = bf16[2,144,320]{2,1,0:T(8,128)(2,1)} reshape(bf16[2,1,12,3840]{3,2,0,1:T(8,128)(2,1)S(1)} %copy.13) | data formatting | bytes 368640 | tf_op jit(solution)/shard_map/reshape | solution.py:492
  18.0 5.6 %all-to-all-start.1 = ((bf16[8,40,640]{2,1,0:T(8,128)(2,1)}), bf16[8,40,640]{2,1,0:T(8,128)(2,1)}, u32[]{:S(2)}, u32[]{:S(2)}) async-start(bf16[8,40,640]{2,1,0:T(8,128)(2,1)} %get-tuple-element.29), calls=%async_computation.1 | async-start | bytes 819200 | tf_op jit(solution)/shard_map/all_to_all | solution.py:510
  23.6 0.0 collective-permute-done.2.inbound
  23.6 0.0 copy-start.11
  23.6 0.6 copy-done.11
  24.2 12.2 %shard_map.93 = (bf16[2,40,640]{2,1,0:T(8,128)(2,1)}, bf16[10,40,640]{2,1,0:T(8,128)(2,1)}, bf16[10,40,640]{2,1,0:T(8,128)(2,1)}, bf16[8,72,640]{2,1,0:T(8,128)(2,1)}) custom-call(s32[2]{0:T(128)} %pad_add_fusion.where, bf16[2880,640]{1,0:T(8,128)(2,1)} %bitcast.11, bf16[2880,640]{1,0:T(8,128)(2,1)} %collective-permute-done.other, ...), custom_call_target="tpu_custom_call" | custom-call | flops 10000000000 | bytes 4194304 | tf_op jit(solution)/shard_map/pallas_call | solution.py:513
  36.4 0.0 all-to-all-done.1
  36.4 5.5 %all-to-all-start.2 = ((bf16[8,72,640]{2,1,0:T(8,128)(2,1)}), bf16[8,72,640]{2,1,0:T(8,128)(2,1)S(1)}, u32[]{:S(2)}, u32[]{:S(2)}) async-start(bf16[8,72,640]{2,1,0:T(8,128)(2,1)} %get-tuple-element.30), calls=%async_computation.2 | async-start | bytes 1474560 | tf_op jit(solution)/shard_map/all_to_all | solution.py:510
  41.9 0.1 collective-permute-start.3
  42.0 1.5 %collective-permute-start.5 = (bf16[10,40,640]{2,1,0:T(8,128)(2,1)}, bf16[10,40,640]{2,1,0:T(8,128)(2,1)S(1)}, u32[]{:S(2)}, u32[]{:S(2)}) collective-permute-start(bf16[10,40,640]{2,1,0:T(8,128)(2,1)} %get-tuple-element.28), channel_id=1, source_target_pairs={{0,8},{8,0},{16,24},{24,16},{1,9},{9,1},{17,25},{25,17},{2,10},{10... | collective-permute-start | bytes 1536008 | tf_op jit(solution)/shard_map/ppermute | solution.py:507
  43.5 1.3 %collective-permute-start.6 = (bf16[8,40,640]{2,1,0:T(8,128)(2,1)}, bf16[8,40,640]{2,1,0:T(8,128)(2,1)S(1)}, u32[]{:S(2)}, u32[]{:S(2)}) collective-permute-start(bf16[8,40,640]{2,1,0:T(8,128)(2,1)} %all-to-all-done.1), channel_id=1, source_target_pairs={{0,16},{8,24},{16,0},{24,8},{1,17},{9,25},{17,1},{25,9},{2,18},{10... | collective-permute-start | bytes 1228808 | tf_op jit(solution)/shard_map/ppermute | solution.py:507
  44.9 14.8 %all-to-all-done.2.one = bf16[8,72,640]{2,1,0:T(8,128)(2,1)S(1)} async-done(((bf16[8,72,640]{2,1,0:T(8,128)(2,1)}), bf16[8,72,640]{2,1,0:T(8,128)(2,1)S(1)}, u32[]{:S(2)}, u32[]{:S(2)}) %all-to-all-start.2) | async-done | bytes 737312 | tf_op jit(solution)/shard_map/all_to_all | solution.py:510
  59.6 0.0 copy-start
  59.6 2.3 %collective-permute-start.8 = (bf16[8,72,640]{2,1,0:T(8,128)(2,1)S(1)}, bf16[8,72,640]{2,1,0:T(8,128)(2,1)S(1)}, u32[]{:S(2)}, u32[]{:S(2)}) collective-permute-start(bf16[8,72,640]{2,1,0:T(8,128)(2,1)S(1)} %all-to-all-done.2.one), channel_id=1, source_target_pairs={{0,8},{8,0},{16,24},{24,16},{1,9},{9,1},{17,25},{25,17},{2,10},{10... | collective-permute-start | bytes 2211848 | tf_op jit(solution)/shard_map/ppermute | solution.py:507
  62.0 0.0 collective-permute-done.3.grads
  62.0 0.0 copy-start.10
  62.0 0.6 copy-done.10
  62.6 0.0 copy-start.2
  62.6 0.0 copy-start.4
  62.6 5.3 %shard_map.94 = (bf16[40,640]{1,0:T(8,128)(2,1)}, bf16[40,640]{1,0:T(8,128)(2,1)}) custom-call(s32[2]{0:T(128)} %pad_add_fusion.where, bf16[2880,640]{1,0:T(8,128)(2,1)} %bitcast.12, bf16[2880,640]{1,0:T(8,128)(2,1)} %collective-permute-done.other, bf16[2,40,640]{2,1,0:T(8,128)(2,1)} %copy-done.10, f32[40,640]{1,0:T(8,128)} %get-tuple-element.23.enc_slope, ...), custom_call_target="tpu_custom_call" | custom-call | flops 10000000000 | bytes 4194304 | tf_op jit(solution)/shard_map/pallas_call | solution.py:513
  67.9 0.0 copy-done
  68.0 0.1 collective-permute-start.4
  68.1 0.0 collective-permute-done.6.zero
  68.1 0.5 collective-permute-start.7
  68.5 0.9 collective-permute-done.4.back_received
  69.5 0.0 collective-permute-done.5.middle_received
  69.5 0.0 copy-done.2
  69.5 0.0 copy-done.4
  69.5 0.0 copy-start.3
  69.5 0.8 copy-done.3
  70.3 1.5 %shard_map.95 = bf16[8,72,640]{2,1,0:T(8,128)(2,1)} custom-call(s32[2]{0:T(128)S(1)} %copy-done.4, bf16[40,640]{1,0:T(8,128)(2,1)S(1)} %copy-done.3, bf16[40,640]{1,0:T(8,128)(2,1)S(1)} %collective-permute-done.4.back_received, bf16[10,40,640]{2,1,0:T(8,128)(2,1)S(1)} %copy-done.2, bf16[10,40,640]{2,1,0:T(8,128)(2,1)S(1)} %collective-permute-done.5.middle_received), custom_call_target="tpu_custom_call" | custom-call | flops 100000000 | bytes 4194304 | tf_op jit(solution)/shard_map/pallas_call | solution.py:513
  71.8 3.5 %all-to-all-start = ((bf16[8,72,640]{2,1,0:T(8,128)(2,1)}), bf16[8,72,640]{2,1,0:T(8,128)(2,1)S(1)}, u32[]{:S(2)}, u32[]{:S(2)}) async-start(bf16[8,72,640]{2,1,0:T(8,128)(2,1)} %shard_map.95), calls=%async_computation | async-start | bytes 1474560 | tf_op jit(solution)/shard_map/all_to_all | solution.py:510
  75.3 0.0 collective-permute-done.7.zero_other
  75.3 0.0 collective-permute-done.8.one_other
  75.3 0.0 copy-start.5
  75.3 0.9 copy-done.5
  76.2 0.0 copy-start.1
  76.2 1.1 %copy-done.1 = bf16[8,72,640]{2,1,0:T(8,128)(2,1)S(1)} copy-done((bf16[8,72,640]{2,1,0:T(8,128)(2,1)S(1)}, bf16[8,72,640]{2,1,0:T(8,128)(2,1)}, u32[]{:S(2)}) %copy-start.1) | copy-done | bytes 737304
  77.3 0.0 copy-start.6
  77.3 1.1 %copy-done.6 = bf16[8,72,640]{2,1,0:T(8,128)(2,1)S(1)} copy-done((bf16[8,72,640]{2,1,0:T(8,128)(2,1)S(1)}, bf16[8,72,640]{2,1,0:T(8,128)(2,1)}, u32[]{:S(2)}) %copy-start.6) | copy-done | bytes 737304
  78.5 0.0 copy-start.7
  78.5 0.9 copy-done.7
  79.4 2.0 %shard_map.96 = (bf16[2,576,640]{2,1,0:T(8,128)(2,1)S(1)}, f32[320,640]{1,0:T(8,128)S(1)}) custom-call(s32[2]{0:T(128)S(1)} %copy-done.4, bf16[648,72]{1,0:T(8,128)(2,1)S(1)} %copy-done.7, bf16[8,40,640]{2,1,0:T(8,128)(2,1)S(1)} %collective-permute-done.6.zero, bf16[8,40,640]{2,1,0:T(8,128)(2,1)} %collective-permute-done.7.zero_other, ...), custom_call_target="tpu_custom_call" | custom-call | flops 10000000000 | bytes 4194304 | tf_op jit(solution)/shard_map/pallas_call | solution.py:513
  81.3 12.8 %all-to-all-done.right = bf16[8,72,640]{2,1,0:T(8,128)(2,1)S(1)} async-done(((bf16[8,72,640]{2,1,0:T(8,128)(2,1)}), bf16[8,72,640]{2,1,0:T(8,128)(2,1)S(1)}, u32[]{:S(2)}, u32[]{:S(2)}) %all-to-all-start) | async-done | bytes 737312 | tf_op jit(solution)/shard_map/all_to_all | solution.py:510
  94.2 2.9 %shard_map.97 = f32[360,640]{1,0:T(8,128)} custom-call(s32[2]{0:T(128)S(1)} %copy-done.4, bf16[8,72,640]{2,1,0:T(8,128)(2,1)S(1)} %all-to-all-done.right, bf16[2,576,640]{2,1,0:T(8,128)(2,1)S(1)} %get-tuple-element.31.lefts, f32[320,640]{1,0:T(8,128)S(1)} %get-tuple-element.32.early), custom_call_target="tpu_custom_call" | custom-call | flops 100000000 | bytes 4194304 | tf_op jit(solution)/shard_map/pallas_call | solution.py:513
  (1 shorter events, 0.0 us)
Async XLA Ops:
  0.0 8.6 %collective-permute-start = (bf16[2880,640]{1,0:T(8,128)(2,1)}, bf16[2880,640]{1,0:T(8,128)(2,1)}, u32[]{:S(2)}, u32[]{:S(2)}) collective-permute-start(bf16[2880,640]{1,0:T(8,128)(2,1)} %bitcast.8), channel_id=1, source_target_pairs={{0,8},{8,0},{16,24},{24,16},{1,9},{9,1},{17,25},{25,17},{2,10},{10... | collective-permute-start | bytes 11059208 | tf_op jit(solution)/shard_map/ppermute | solution.py:507
  6.7 1.8 %collective-permute-start.1 = (bf16[4,40,640]{2,1,0:T(8,128)(2,1)}, bf16[4,40,640]{2,1,0:T(8,128)(2,1)S(1)}, u32[]{:S(2)}, u32[]{:S(2)}) collective-permute-start(bf16[4,40,640]{2,1,0:T(8,128)(2,1)} %get-tuple-element.19.own), channel_id=1, source_target_pairs={{0,8},{8,0},{16,24},{24,16},{1,9},{9,1},{17,25},{25,17},{2,10},{10... | collective-permute-start | bytes 614408 | tf_op jit(solution)/shard_map/ppermute | solution.py:507
  7.9 9.1 %copy-start.9 = (bf16[2,1,12,3840]{3,0,2,1:T(2,128)(2,1)S(1)}, bf16[2,1,12,3840]{3,0,2,1:T(2,128)(2,1)}, u32[]{:S(2)}) copy-start(bf16[2,1,12,3840]{3,0,2,1:T(2,128)(2,1)} %param.10) | copy-start | bytes 552964
  8.6 0.7 copy-start.8
  14.3 9.3 %collective-permute-start.2 = (bf16[2,40,640]{2,1,0:T(8,128)(2,1)}, bf16[2,40,640]{2,1,0:T(8,128)(2,1)S(1)}, u32[]{:S(2)}, u32[]{:S(2)}) collective-permute-start(bf16[2,40,640]{2,1,0:T(8,128)(2,1)} %get-tuple-element.20.mine_forward), channel_id=1, source_target_pairs={{0,16},{8,24},{16,0},{24,8},{1,17},{9,25},{17,1},{25,9},{2,18},{10... | collective-permute-start | bytes 307208 | tf_op jit(solution)/shard_map/ppermute | solution.py:507
  18.0 18.4 %all-to-all-start.1 = ((bf16[8,40,640]{2,1,0:T(8,128)(2,1)}), bf16[8,40,640]{2,1,0:T(8,128)(2,1)}, u32[]{:S(2)}, u32[]{:S(2)}) async-start(bf16[8,40,640]{2,1,0:T(8,128)(2,1)} %get-tuple-element.29), calls=%async_computation.1 | async-start | bytes 819200 | tf_op jit(solution)/shard_map/all_to_all | solution.py:510
  23.6 0.6 copy-start.11
  36.4 23.2 %all-to-all-start.2 = ((bf16[8,72,640]{2,1,0:T(8,128)(2,1)}), bf16[8,72,640]{2,1,0:T(8,128)(2,1)S(1)}, u32[]{:S(2)}, u32[]{:S(2)}) async-start(bf16[8,72,640]{2,1,0:T(8,128)(2,1)} %get-tuple-element.30), calls=%async_computation.2 | async-start | bytes 1474560 | tf_op jit(solution)/shard_map/all_to_all | solution.py:510
  41.9 20.1 %collective-permute-start.3 = (bf16[2,40,640]{2,1,0:T(8,128)(2,1)}, bf16[2,40,640]{2,1,0:T(8,128)(2,1)S(1)}, u32[]{:S(2)}, u32[]{:S(2)}) collective-permute-start(bf16[2,40,640]{2,1,0:T(8,128)(2,1)} %get-tuple-element.22), channel_id=1, source_target_pairs={{0,16},{8,24},{16,0},{24,8},{1,17},{9,25},{17,1},{25,9},{2,18},{10... | collective-permute-start | bytes 307208 | tf_op jit(solution)/shard_map/ppermute | solution.py:507
  42.0 27.5 %collective-permute-start.5 = (bf16[10,40,640]{2,1,0:T(8,128)(2,1)}, bf16[10,40,640]{2,1,0:T(8,128)(2,1)S(1)}, u32[]{:S(2)}, u32[]{:S(2)}) collective-permute-start(bf16[10,40,640]{2,1,0:T(8,128)(2,1)} %get-tuple-element.28), channel_id=1, source_target_pairs={{0,8},{8,0},{16,24},{24,16},{1,9},{9,1},{17,25},{25,17},{2,10},{10... | collective-permute-start | bytes 1536008 | tf_op jit(solution)/shard_map/ppermute | solution.py:507
  43.5 24.5 %collective-permute-start.6 = (bf16[8,40,640]{2,1,0:T(8,128)(2,1)}, bf16[8,40,640]{2,1,0:T(8,128)(2,1)S(1)}, u32[]{:S(2)}, u32[]{:S(2)}) collective-permute-start(bf16[8,40,640]{2,1,0:T(8,128)(2,1)} %all-to-all-done.1), channel_id=1, source_target_pairs={{0,16},{8,24},{16,0},{24,8},{1,17},{9,25},{17,1},{25,9},{2,18},{10... | collective-permute-start | bytes 1228808 | tf_op jit(solution)/shard_map/ppermute | solution.py:507
  59.6 8.3 %copy-start = (bf16[8,72,640]{2,1,0:T(8,128)(2,1)}, bf16[8,72,640]{2,1,0:T(8,128)(2,1)S(1)}, u32[]{:S(2)}) copy-start(bf16[8,72,640]{2,1,0:T(8,128)(2,1)S(1)} %all-to-all-done.2.one) | copy-start | bytes 2211844
  59.6 15.7 %collective-permute-start.8 = (bf16[8,72,640]{2,1,0:T(8,128)(2,1)S(1)}, bf16[8,72,640]{2,1,0:T(8,128)(2,1)S(1)}, u32[]{:S(2)}, u32[]{:S(2)}) collective-permute-start(bf16[8,72,640]{2,1,0:T(8,128)(2,1)S(1)} %all-to-all-done.2.one), channel_id=1, source_target_pairs={{0,8},{8,0},{16,24},{24,16},{1,9},{9,1},{17,25},{25,17},{2,10},{10... | collective-permute-start | bytes 2211848 | tf_op jit(solution)/shard_map/ppermute | solution.py:507
  62.0 0.6 copy-start.10
  62.6 6.8 %copy-start.2 = (bf16[10,40,640]{2,1,0:T(8,128)(2,1)S(1)}, bf16[10,40,640]{2,1,0:T(8,128)(2,1)}, u32[]{:S(2)}) copy-start(bf16[10,40,640]{2,1,0:T(8,128)(2,1)} %get-tuple-element.27.middle_own) | copy-start | bytes 1536004
  62.6 6.8 %copy-start.4 = (s32[2]{0:T(128)S(1)}, s32[2]{0:T(128)}, u32[]{:S(2)}) copy-start(s32[2]{0:T(128)} %pad_add_fusion.where) | copy-start | bytes 28
  68.0 1.5 %collective-permute-start.4 = (bf16[40,640]{1,0:T(8,128)(2,1)}, bf16[40,640]{1,0:T(8,128)(2,1)S(1)}, u32[]{:S(2)}, u32[]{:S(2)}) collective-permute-start(bf16[40,640]{1,0:T(8,128)(2,1)} %get-tuple-element.26), channel_id=1, source_target_pairs={{0,8},{8,0},{16,24},{24,16},{1,9},{9,1},{17,25},{25,17},{2,10},{10... | collective-permute-start | bytes 153608 | tf_op jit(solution)/shard_map/ppermute | solution.py:507
  68.1 7.2 %collective-permute-start.7 = (bf16[8,40,640]{2,1,0:T(8,128)(2,1)S(1)}, bf16[8,40,640]{2,1,0:T(8,128)(2,1)}, u32[]{:S(2)}, u32[]{:S(2)}) collective-permute-start(bf16[8,40,640]{2,1,0:T(8,128)(2,1)S(1)} %collective-permute-done.6.zero), channel_id=1, source_target_pairs={{0,8},{8,0},{16,24},{24,16},{1,9},{9,1},{17,25},{25,17},{2,10},{10... | collective-permute-start | bytes 1228808 | tf_op jit(solution)/shard_map/ppermute | solution.py:507
  69.5 0.8 copy-start.3
  71.8 22.4 %all-to-all-start = ((bf16[8,72,640]{2,1,0:T(8,128)(2,1)}), bf16[8,72,640]{2,1,0:T(8,128)(2,1)S(1)}, u32[]{:S(2)}, u32[]{:S(2)}) async-start(bf16[8,72,640]{2,1,0:T(8,128)(2,1)} %shard_map.95), calls=%async_computation | async-start | bytes 1474560 | tf_op jit(solution)/shard_map/all_to_all | solution.py:510
  75.3 0.9 copy-start.5
  76.2 1.1 %copy-start.1 = (bf16[8,72,640]{2,1,0:T(8,128)(2,1)S(1)}, bf16[8,72,640]{2,1,0:T(8,128)(2,1)}, u32[]{:S(2)}) copy-start(bf16[8,72,640]{2,1,0:T(8,128)(2,1)} %copy-done) | copy-start | bytes 2211844
  77.3 1.1 %copy-start.6 = (bf16[8,72,640]{2,1,0:T(8,128)(2,1)S(1)}, bf16[8,72,640]{2,1,0:T(8,128)(2,1)}, u32[]{:S(2)}) copy-start(bf16[8,72,640]{2,1,0:T(8,128)(2,1)} %copy-done.5) | copy-start | bytes 2211844
  78.5 0.9 copy-start.7
